TPU v7x, 32 devices: a whole 2x2x4 slice. The times are simulated.
32 devices in a mesh: dp: 8 (over y, x, core), tensor: 4 (over z).
Axes of the slice: x: 2, y: 2, z: 4, core: 2. Of those that a mesh axis runs over, the one named last changes fastest.
Arguments:
- hidden_in: bfloat16 [16384, 768], P(('dp', 'tensor')), may hold values from -6 to 6
- token_types: int32 [16384], P('dp'), may hold values 0 or 1
- lengths: int32 [8], P('dp'), may hold values from 512 to 2048, as said below
- cotangent: bfloat16 [16384, 768], P(('dp', 'tensor')), may hold values from -6 to 6
- query_w: bfloat16 [4, 768, 768], P(None, 'dp', 'tensor'), may hold values from -0.4375 to 0.4375
- query_b: bfloat16 [4, 768], replicated, may hold values from -3 to 3
- key_w: bfloat16 [768, 768], P('dp', 'tensor'), may hold values from -0.21875 to 0.21875
- value_w: bfloat16 [768, 768], P('dp', 'tensor'), may hold values from -0.21875 to 0.21875
- value_b: bfloat16 [768], replicated, may hold values from -3 to 3
- out_w: bfloat16 [768, 768], P('tensor', 'dp'), may hold values from -0.875 to 0.875
- out_b: bfloat16 [768], replicated, may hold values from -3 to 3
- gain_one: bfloat16 [768], replicated, may hold values from 0.099609375 to 1.8984375
- shift_one: bfloat16 [768], replicated, may hold values from -3 to 3
- inter_w: bfloat16 [768, 3072], P('dp', 'tensor'), may hold values from -0.21875 to 0.21875
- inter_b: bfloat16 [3072], replicated, may hold values from -3 to 3
- output_w: bfloat16 [3072, 768], P('tensor', 'dp'), may hold values from -0.109375 to 0.109375
- output_b: bfloat16 [768], replicated, may hold values from -3 to 3
- gain_two: bfloat16 [768], replicated, may hold values from 0.099609375 to 1.8984375
- shift_two: bfloat16 [768], replicated, may hold values from -3 to 3
Outputs:
- layer_out: bfloat16 [16384, 768], P(('dp', 'tensor'))
- grad_hidden: float32 [16384, 768], P(('dp', 'tensor'))
- query_weight_gradient: float32 [4, 768, 768], P(None, 'dp', 'tensor')
- grad_query_b: float32 [4, 768], replicated
- grad_key_w: float32 [768, 768], P('dp', 'tensor')
- grad_value_w: float32 [768, 768], P('dp', 'tensor')
- grad_value_b: float32 [768], replicated
- grad_out_w: float32 [768, 768], P('tensor', 'dp')
- grad_out_b: float32 [768], replicated
- grad_gain_one: float32 [768], replicated
- grad_shift_one: float32 [768], replicated
- grad_inter_w: float32 [768, 3072], P('dp', 'tensor')
- grad_inter_b: float32 [3072], replicated
- grad_output_w: float32 [3072, 768], P('tensor', 'dp')
- grad_output_b: float32 [768], replicated
- grad_gain_two: float32 [768], replicated
- grad_shift_two: float32 [768], replicated
Inputs may be any that keep to these rules, and one draw needn't show every extreme that they name: `lengths`: valid slots of each sequence; in every draw one sequence is full and another has exactly 512 valid slots.
All inputs are finite; a program needn't handle non-finite values. No bound on the sum of `token_types` on one device may be relied on, other than what follows from the above.
Results may differ from a plain program's by a relative error of at most 0.019.
The roundings to bfloat16 on the way count: a program that leaves them out, or rounds other values in their place, can miss the bound.
Values may be sent and summed in bfloat16 or wider, within the bound.
No kernel may reach another device: no remote copies, remote signals or barrier semaphores. Data moves between devices by JAX's collectives and lax.ppermute only.
A program may use at most 192 MiB of HBM per device.

v0:
```python
import functools

import jax
import jax.numpy as jnp
from jax import lax
from jax.experimental import pallas as pl
from jax.experimental.pallas import tpu as pltpu
from jax.sharding import PartitionSpec as P

HD = 64
BLOCK = 512
KEY_PARTS = 2
LANES = 128
EPS = 1e-05
MASKED = -1e30
SQRT_HALF = 0.7071067811865476
INV_SQRT_2PI = 0.3989422804014327
VMEM_LIMIT = 60000 * 1024

f32 = jnp.float32
bf16 = jnp.bfloat16


def dot_nn(a, b):
    return lax.dot_general(a, b, (((1,), (0,)), ((), ())), preferred_element_type=f32)


def dot_nt(a, b):
    return lax.dot_general(a, b, (((1,), (1,)), ((), ())), preferred_element_type=f32)


def params(**kw):
    return pltpu.CompilerParams(vmem_limit_bytes=VMEM_LIMIT, **kw)


def cost(flops, nbytes, transcendentals=0, short=1):
    return pl.CostEstimate(
        flops=7 * flops // (2 * short), bytes_accessed=nbytes // short, transcendentals=transcendentals
    )


def copies(jobs, sems):
    started = []
    for at, (source, target) in enumerate(jobs):
        copy = pltpu.make_async_copy(source, target, sems.at[at])
        copy.start()
        started.append(copy)
    return started


def block_rows(index, rows):
    return pl.ds(pl.multiple_of(index * rows, rows), rows)


def head_columns(heads):
    return [[HD * (part * heads + h) for part in range(6)] for h in range(heads)]


def by_heads(value, heads):
    cols = [value[:, at : at + HD] for parts in head_columns(heads) for at in parts]
    return jnp.concatenate(cols, 1)


def by_parts(value, heads):
    cols = [value[:, HD * (6 * h + part) : HD * (6 * h + part + 1)] for part in range(6) for h in range(heads)]
    return jnp.concatenate(cols, 1)


def project_weight_jobs(layout, pos_ref, refs, w_ref):
    jobs = []
    chip = pos_ref[2] // 2
    for masks, ref in zip(layout, refs):
        if masks is None:
            jobs.append((ref, w_ref))
            continue
        for u, (mask, second) in enumerate(masks):
            jobs.append((ref.at[u], w_ref.at[block_rows(2 * (chip ^ mask) + second, ref.shape[1])]))
    return jobs


def project_kernel(heads, layout, pos_ref, x0, x1, x2, x3, b_ref, ent_ref, *rest):
    count = len(layout)
    pieces = rest[:count]
    qc_ref, kc_ref, kv_ref, w_ref, x_ref, raw_ref, b_scr, sems = rest[count:]

    @pl.when(pl.program_id(0) == 0)
    def _():
        jobs = [(ref, x_ref.at[m]) for m, ref in enumerate((x0, x1, x2, x3))]
        for copy in copies(jobs + project_weight_jobs(layout, pos_ref, pieces, raw_ref), sems):
            copy.wait()
        w_ref[...] = by_heads(raw_ref[...], heads)
        b_scr[...] = by_heads(jnp.broadcast_to(b_ref[...], b_scr.shape), heads)

    x = x_ref[pl.program_id(0)]
    ent = ent_ref[...] > 0.5
    lane = lax.broadcasted_iota(jnp.int32, (x.shape[0], LANES), 1)
    low_half = lane < HD
    keep = jnp.logical_xor(low_half, ent)
    every = dot_nn(x, w_ref[...]) + b_scr[:1]
    for h in range(heads):
        y = every[:, 3 * LANES * h : 3 * LANES * (h + 1)]
        q = jnp.where(ent, y[:, LANES : 2 * LANES], y[:, :LANES])
        qc_ref[h] = q.astype(bf16) * (HD ** (-0.5))
        kv = y[:, 2 * LANES :].astype(bf16).astype(f32)
        kv_ref[h] = kv.astype(bf16)
        twice = jnp.where(low_half, kv, pltpu.roll(kv, HD, 1))
        kc_ref[h] = jnp.where(keep, twice, 0.0).astype(bf16)


def project(pos, x, pieces, layout, b, ent):
    own_rows, width = x[0].shape
    tokens = own_rows * len(x)
    columns = b.shape[1]
    heads = columns // (3 * LANES)
    out = jax.ShapeDtypeStruct((heads, tokens, LANES), bf16)
    spec = pl.BlockSpec((heads, own_rows, LANES), lambda m, pos: (0, m ^ pos[0], 0))
    anywhere = pl.BlockSpec(memory_space=pltpu.HBM)
    jobs = sum(1 if masks is None else len(masks) for masks in layout)
    return pl.pallas_call(
        functools.partial(project_kernel, heads, layout),
        grid_spec=pltpu.PrefetchScalarGridSpec(
            num_scalar_prefetch=1,
            grid=(len(x),),
            in_specs=[anywhere] * 4
            + [
                pl.BlockSpec((1, columns), lambda m, pos: (0, 0)),
                pl.BlockSpec((own_rows, LANES), lambda m, pos: (m ^ pos[0], 0)),
            ]
            + [anywhere] * len(pieces),
            out_specs=[spec, spec, spec, pl.BlockSpec((width, columns), lambda m, pos: (0, 0))],
            scratch_shapes=[
                pltpu.VMEM((len(x), own_rows, width), bf16),
                pltpu.VMEM((width, columns), bf16),
                pltpu.VMEM((8, columns), f32),
                pltpu.SemaphoreType.DMA((len(x) + jobs,)),
            ],
        ),
        out_shape=[out, out, out, jax.ShapeDtypeStruct((width, columns), bf16)],
        compiler_params=params(),
        cost_estimate=cost(2 * tokens * width * columns, 2 * tokens * (width + columns)),
        name="project",
    )(pos, *x, b, ent, *pieces)


def masked_keys(pos_ref, scores, first=0):
    keys = first + lax.broadcasted_iota(jnp.int32, (scores.shape[0], 1), 0)
    return scores + jnp.where(keys < pos_ref[4], 0.0, MASKED)


def attend_kernel(pos_ref, q_ref, kc_ref, kv_ref, *rest):
    out_ref, lse_ref, vt_ref = rest[-3:]

    @pl.when(pl.program_id(1) == 0)
    def _():
        vt_ref[...] = kv_ref[0].T[HD:]

    scores = masked_keys(pos_ref, dot_nt(kc_ref[0], q_ref[0]))
    top = jnp.max(scores, 0, keepdims=True)
    exponent = jnp.exp(scores - top)
    total = jnp.sum(exponent, 0, keepdims=True)
    mixed = dot_nn(vt_ref[...], exponent.astype(bf16))
    out_ref[0] = (mixed / total).astype(bf16)
    lse_ref[0] = top + jnp.log(total)


def attend(pos, first, count, qc, kc, kv, before=()):
    heads, tokens, _ = qc.shape
    blocks = tokens // BLOCK
    full = pl.BlockSpec((1, tokens, LANES), lambda h, i, pos: (first + h, 0, 0))
    return pl.pallas_call(
        attend_kernel,
        grid_spec=pltpu.PrefetchScalarGridSpec(
            num_scalar_prefetch=1,
            grid=(count, blocks),
            in_specs=[pl.BlockSpec((1, BLOCK, LANES), lambda h, i, pos: (first + h, i, 0)), full, full]
            + [pl.BlockSpec(memory_space=pltpu.HBM)] * len(before),
            out_specs=[
                pl.BlockSpec((1, HD, BLOCK), lambda h, i, pos: (i ^ pos[0], first + h, 0)),
                pl.BlockSpec((1, 1, BLOCK), lambda h, i, pos: (h, 0, i)),
            ],
            scratch_shapes=[pltpu.VMEM((HD, tokens), bf16)],
        ),
        out_shape=[
            jax.ShapeDtypeStruct((blocks, heads * HD, BLOCK), bf16),
            jax.ShapeDtypeStruct((count, 1, tokens), f32),
        ],
        input_output_aliases={4: 0} if before else {},
        compiler_params=params(),
        cost_estimate=cost(count * tokens * tokens * 2 * 3 * LANES, count * tokens * 8 * LANES),
        name="attend",
    )(pos, qc, kc, kv, *before)


def attend_back_kernel(
    pos_ref, q_ref, kc_ref, kv_ref, ent_ref, lse_ref, out_ref, go_ref,
    dq_ref, dkv_ref, kt_ref, dk_acc, dv_acc, go_pad,
):
    step = pl.program_id(1)

    @pl.when(step == 0)
    def _():
        kt_ref[...] = kc_ref[0].T
        go_pad[:HD] = jnp.zeros((HD, go_pad.shape[1]), bf16)
        dk_acc[...] = jnp.zeros_like(dk_acc)
        dv_acc[...] = jnp.zeros_like(dv_acc)

    go = go_ref[0]
    go_pad[HD:] = go
    delta = jnp.sum(go.astype(f32) * out_ref[0].astype(f32), 0, keepdims=True)
    q = q_ref[0]
    rows = kc_ref.shape[1] // KEY_PARTS

    def keys_part(part, dq):
        at = block_rows(part, rows)
        scores = masked_keys(pos_ref, dot_nt(kc_ref[0, at], q), part * rows)
        probs = jnp.exp(scores - lse_ref[0])
        grad_probs = dot_nn(kv_ref[0, at], go_pad[...])
        grad_scores = (probs * (grad_probs - delta)).astype(bf16)
        dv_acc[at] += dot_nt(probs.astype(bf16), go_pad[...])
        dk_acc[at] += dot_nn(grad_scores, q)
        return dq + dot_nn(kt_ref[:, at], grad_scores)

    dq = lax.fori_loop(0, KEY_PARTS, keys_part, jnp.zeros((LANES, q.shape[0]), f32))
    dq_ref[0] = (dq * (HD ** (-0.5))).T.astype(bf16)

    @pl.when(step == pl.num_programs(1) - 1)
    def _():
        lane = lax.broadcasted_iota(jnp.int32, dk_acc.shape, 1)
        dk = dk_acc[...]
        dk = jnp.where(ent_ref[...] > 0.5, pltpu.roll(dk, HD, 1), dk)
        dkv_ref[0] = jnp.where(lane < HD, dk, dv_acc[...]).astype(bf16)


def attend_back(pos, first, count, qc, kc, kv, ent, lse, mixed, grad_mixed):
    tokens = qc.shape[1]
    blocks = tokens // BLOCK
    full = pl.BlockSpec((1, tokens, LANES), lambda h, i, pos: (first + h, 0, 0))
    slot = pl.BlockSpec((1, HD, BLOCK), lambda h, i, pos: (i ^ pos[0], first + h, 0))
    out = jax.ShapeDtypeStruct((count, tokens, LANES), bf16)
    return pl.pallas_call(
        attend_back_kernel,
        grid_spec=pltpu.PrefetchScalarGridSpec(
            num_scalar_prefetch=1,
            grid=(count, blocks),
            in_specs=[
                pl.BlockSpec((1, BLOCK, LANES), lambda h, i, pos: (first + h, i, 0)),
                full, full,
                pl.BlockSpec((tokens, LANES), lambda h, i, pos: (0, 0)),
                pl.BlockSpec((1, 1, BLOCK), lambda h, i, pos: (h, 0, i)),
                slot, slot,
            ],
            out_specs=[
                pl.BlockSpec((1, BLOCK, LANES), lambda h, i, pos: (h, i, 0)),
                pl.BlockSpec((1, tokens, LANES), lambda h, i, pos: (h, 0, 0)),
            ],
            scratch_shapes=[
                pltpu.VMEM((LANES, tokens), bf16),
                pltpu.VMEM((tokens, LANES), f32),
                pltpu.VMEM((tokens, LANES), f32),
                pltpu.VMEM((LANES, BLOCK), bf16),
            ],
        ),
        out_shape=[out, out],
        compiler_params=params(),
        cost_estimate=cost(count * tokens * tokens * 2 * 5 * LANES, count * tokens * 16 * LANES),
        name="attend_back",
    )(pos, qc, kc, kv, ent, lse, mixed, grad_mixed)


def normed(residual, gain, shift):
    center = residual - jnp.mean(residual, -1, keepdims=True)
    inv = lax.rsqrt(jnp.mean(center * center, -1, keepdims=True) + EPS)
    unit = center * inv
    return unit, inv, unit * gain + shift


def norm_back(grad, unit, inv, gain):
    scaled = grad * gain
    return (
        scaled
        - jnp.mean(scaled, -1, keepdims=True)
        - unit * jnp.mean(scaled * unit, -1, keepdims=True)
    ) * inv


def token_weight_jobs(layout, pos_ref, refs, w_ref):
    jobs = []
    for masks, ref in zip(layout, refs):
        if masks is None:
            jobs.append((ref, w_ref))
            continue
        for u, (mask, group_mask) in enumerate(masks):
            where = block_rows(pos_ref[2] ^ mask, ref.shape[1])
            jobs.append((ref.at[u], w_ref.at[pos_ref[1] ^ group_mask, where]))
    return jobs


def token_kernel(
    layout, pos_ref, m0, m1, m2, m3, hid_ref, cot_ref, valid_ref, vec_ref, *rest
):
    count = len(layout)
    pieces = rest[:count]
    (
        y_ref, mixt_ref, nb_ref, act_ref, gi_ref, gf_ref, ga_ref, gm_ref, gr_ref, sums_ref, gib_ref,
        slope_ref, w_ref, sum_ref, unit_ref, inv_ref, sems,
    ) = rest[count:]
    me = pos_ref[0]
    groups, width, _ = w_ref.shape
    tokens = hid_ref.shape[0]
    ffn = act_ref.shape[2]
    gwidth = mixt_ref.shape[1]
    out_at = 2 * ffn
    jobs = token_weight_jobs(layout, pos_ref, pieces, w_ref)
    early = slice(out_at, out_at + gwidth)
    loads = copies([(s.at[..., early], t.at[..., early]) for s, t in jobs], sems.at[0])
    late = copies([(s.at[..., :out_at], t.at[..., :out_at]) for s, t in jobs], sems.at[1])
    for load in loads:
        load.wait()
    for m, ref in enumerate((m0, m1, m2, m3)):
        mixt_ref[me ^ m] = ref[0]

    def vector(at):
        value = vec_ref[at]
        return jnp.concatenate([value[i : i + 1] for i in range(value.shape[0])], 1)

    out_b, gain_one, shift_one, output_b, gain_two, shift_two = (vector(at) for at in range(6))
    few = min(LANES, tokens)
    sums_ref[...] = jnp.zeros_like(sums_ref)
    gib_ref[...] = jnp.zeros_like(gib_ref)

    def by_blocks(body):
        lax.fori_loop(0, tokens // few, lambda r, _: (body(block_rows(r, few)), 0)[1], 0)

    def total(at, value):
        sums_ref[at] += jnp.sum(value, 0, keepdims=True)

    def first_norm(at):
        attended = out_b
        for g in range(groups):
            part = dot_nt(mixt_ref[g, :, at].T, w_ref[g, :, early])
            attended = attended + part.astype(bf16).astype(f32)
        unit, inv, value = normed(hid_ref[at].astype(f32) + attended, gain_one, shift_one)
        unit_ref[at] = unit
        inv_ref[at] = jnp.broadcast_to(inv, (inv.shape[0], LANES))
        nb_ref[at] = value.astype(bf16)
        sum_ref[at] = jnp.broadcast_to(output_b, value.shape)

    first_norm(slice(0, tokens))
    for load in late:
        load.wait()
    halves = 2
    part_rows = tokens // halves

    def forward(step, _):
        g, at = step // halves, block_rows(step % halves, part_rows)
        pre = dot_nn(nb_ref[at], w_ref[g, :, :ffn]) + vector(6 + g)
        cdf = 0.5 * (1.0 + lax.erf(pre * SQRT_HALF))
        slope_ref[g, at] = cdf + pre * (jnp.exp(-0.5 * pre * pre) * INV_SQRT_2PI)
        active = (pre * cdf).astype(bf16)
        act_ref[g, at] = active
        part = dot_nt(active, w_ref[g, :, ffn:out_at])
        sum_ref[at] += part.astype(bf16).astype(f32)
        return 0

    lax.fori_loop(0, groups * halves, forward, 0)

    def second_norm(at):
        valid = valid_ref[at, :1]
        normed_one = unit_ref[at] * gain_one + shift_one
        unit, inv, value = normed(normed_one + sum_ref[at], gain_two, shift_two)
        y_ref[at] = (value * valid).astype(bf16)
        grad_top = cot_ref[at].astype(f32) * valid
        grad = norm_back(grad_top, unit, inv, gain_two)
        grad_ffn = grad.astype(bf16)
        gf_ref[at] = grad_ffn
        sum_ref[at] = grad
        total(3, grad_ffn.astype(f32))
        total(4, grad_top * unit)
        total(5, grad_top)

    by_blocks(second_norm)

    def backward(step, _):
        g, at = step // halves, block_rows(step % halves, part_rows)
        grad_active = dot_nn(gf_ref[at], w_ref[g, :, ffn:out_at])
        grad_inner = (slope_ref[g, at] * grad_active).astype(bf16)
        gi_ref[g, at] = grad_inner
        gib_ref[g] += jnp.sum(grad_inner.astype(f32), 0, keepdims=True)
        part = dot_nt(grad_inner, w_ref[g, :, :ffn])
        sum_ref[at] += part.astype(bf16).astype(f32)
        return 0

    lax.fori_loop(0, groups * halves, backward, 0)

    def first_norm_back(at):
        grad_normed = sum_ref[at]
        unit = unit_ref[at]
        grad = norm_back(grad_normed, unit, inv_ref[at, :1], gain_one)
        gr_ref[at] = grad
        grad_att = grad.astype(bf16)
        ga_ref[at] = grad_att
        total(0, grad_att.astype(f32))
        total(1, grad_normed * unit)
        total(2, grad_normed)

    by_blocks(first_norm_back)

    def mixed_back(m, _):
        out_rows = w_ref[me ^ m, :, early].T
        gm_ref[m] = dot_nt(out_rows, ga_ref[...]).astype(bf16)
        return 0

    for m in range(groups):
        mixed_back(m, 0)


def per_token(
    pos, mixed, hidden, cot, valid, vectors, pieces, layout, groups, columns
):
    tokens, width = hidden.shape
    ffn = vectors.shape[1] * vectors.shape[2]
    gwidth = mixed[0].shape[1]
    vmem = pl.BlockSpec(memory_space=pltpu.VMEM)
    shape = jax.ShapeDtypeStruct
    jobs = sum(1 if masks is None else len(masks) for masks in layout)
    return pl.pallas_call(
        functools.partial(token_kernel, layout),
        in_specs=[pl.BlockSpec(memory_space=pltpu.SMEM)]
        + [vmem] * 8
        + [pl.BlockSpec(memory_space=pltpu.HBM)] * len(pieces),
        out_specs=[vmem] * 11,
        out_shape=[
            shape((tokens, width), bf16),
            shape((groups, gwidth, tokens), bf16),
            shape((tokens, width), bf16),
            shape((groups, tokens, ffn), bf16),
            shape((groups, tokens, ffn), bf16),
            shape((tokens, width), bf16),
            shape((tokens, width), bf16),
            shape((groups, gwidth, tokens), bf16),
            shape((tokens, width), f32),
            shape((6, 1, width), f32),
            shape((groups, 1, ffn), f32),
        ],
        scratch_shapes=[
            pltpu.VMEM((groups, tokens, ffn), f32),
            pltpu.VMEM((groups, width, columns), bf16),
            pltpu.VMEM((tokens, width), f32),
            pltpu.VMEM((tokens, width), f32),
            pltpu.VMEM((tokens, LANES), f32),
            pltpu.SemaphoreType.DMA((2, jobs)),
        ],
        compiler_params=params(),
        cost_estimate=cost(
            8 * tokens * width * ffn * groups + 4 * tokens * width * width,
            2 * groups * width * columns + 4 * tokens * ffn * groups,
            2 * tokens * ffn * groups,
        ),
        name="per_token",
    )(pos, *mixed, hidden, cot, valid, vectors, *pieces)


def weight_grad_kernel(
    pos_ref, nb_ref, gf_ref, ga_ref, act_ref, gi_ref, mixt_ref, near_ref, far_ref, nbt, gft, gat, turn
):
    ffn = act_ref.shape[2]
    gwidth = mixt_ref.shape[1]
    chips, _, rows, _ = near_ref.shape

    @pl.when(pl.program_id(0) == 0)
    def _():
        for target, source in ((nbt, nb_ref), (gft, gf_ref), (gat, ga_ref)):
            turn[...] = source[...].T
            for mine in range(2):
                for mask in range(chips):
                    block = pos_ref[2] ^ (2 * mask + mine)
                    at = (mine * chips + mask) * rows
                    target[at : at + rows] = turn[block_rows(block, rows)]

    second_half = (pl.program_id(0) ^ pos_ref[1]) % 2

    def put(value, start, stop):
        for mine, out_ref in enumerate((near_ref, far_ref)):
            for mask in range(chips):
                slot = mask + second_half - 1 if mask == 2 else mask + 1 - second_half if mask == 1 else mask
                at = (mine * chips + mask) * rows
                out_ref[slot, 0, :, start:stop] = value[at : at + rows].astype(bf16)

    put(dot_nn(nbt[...], gi_ref[0]), 0, ffn)
    put(dot_nn(gft[...], act_ref[0]), ffn, 2 * ffn)
    put(dot_nt(gat[...], mixt_ref[0]), 2 * ffn, 2 * ffn + gwidth)


def weight_grads(pos, nb, gf, ga, act, gi, mixt, dp):
    groups, tokens, ffn = act.shape
    width = nb.shape[1]
    gwidth = mixt.shape[1]
    rows = width // dp
    whole = pl.BlockSpec((tokens, width), lambda g, pos: (0, 0))
    group = pl.BlockSpec((1, tokens, ffn), lambda g, pos: (g, 0, 0))
    columns = 2 * ffn + gwidth
    out = jax.ShapeDtypeStruct((dp // 2, groups, rows, columns), bf16)

    def slot(g, pos):
        mask = g ^ pos[1]
        return (0, 2 * (mask % 2) + mask // 2, 0, 0)

    spec = pl.BlockSpec((dp // 2, 1, rows, columns), slot)
    return pl.pallas_call(
        weight_grad_kernel,
        grid_spec=pltpu.PrefetchScalarGridSpec(
            num_scalar_prefetch=1,
            grid=(groups,),
            in_specs=[
                whole, whole, whole, group, group,
                pl.BlockSpec((1, gwidth, tokens), lambda g, pos: (g, 0, 0)),
            ],
            out_specs=[spec, spec],
            scratch_shapes=[pltpu.VMEM((width, tokens), bf16)] * 4,
        ),
        out_shape=[out, out],
        compiler_params=params(),
        cost_estimate=cost(2 * tokens * width * columns * groups, 2 * groups * width * columns),
        name="weight_grads",
    )(pos, nb, gf, ga, act, gi, mixt)


def weight_grad_whole_kernel(nb_ref, gf_ref, ga_ref, act_ref, gi_ref, mixt_ref, out_ref, nbt, gft, gat):
    ffn = act_ref.shape[2]
    gwidth = mixt_ref.shape[1]

    @pl.when(pl.program_id(0) == 0)
    def _():
        nbt[...] = nb_ref[...].T
        gft[...] = gf_ref[...].T
        gat[...] = ga_ref[...].T

    out_ref[0, :, :ffn] = dot_nn(nbt[...], gi_ref[0]).astype(bf16)
    out_ref[0, :, ffn : 2 * ffn] = dot_nn(gft[...], act_ref[0]).astype(bf16)
    out_ref[0, :, 2 * ffn : 2 * ffn + gwidth] = dot_nt(gat[...], mixt_ref[0]).astype(bf16)


def weight_grads_whole(nb, gf, ga, act, gi, mixt):
    groups, tokens, ffn = act.shape
    width = nb.shape[1]
    gwidth = mixt.shape[1]
    whole = pl.BlockSpec((tokens, width), lambda g: (0, 0))
    group = pl.BlockSpec((1, tokens, ffn), lambda g: (g, 0, 0))
    columns = 2 * ffn + gwidth
    return pl.pallas_call(
        weight_grad_whole_kernel,
        grid=(groups,),
        in_specs=[whole, whole, whole, group, group, pl.BlockSpec((1, gwidth, tokens), lambda g: (g, 0, 0))],
        out_specs=pl.BlockSpec((1, width, columns), lambda g: (g, 0, 0)),
        out_shape=jax.ShapeDtypeStruct((groups, width, columns), bf16),
        scratch_shapes=[pltpu.VMEM((width, tokens), bf16)] * 3,
        compiler_params=params(),
        cost_estimate=cost(2 * tokens * width * columns * groups, 2 * groups * width * columns),
        name="weight_grads_whole",
    )(nb, gf, ga, act, gi, mixt)


def split_columns(pairs, ent):
    h = 0
    for dq_ref, dkv_ref in pairs:
        for u in range(dq_ref.shape[0]):
            dq = dq_ref[u]
            nothing = jnp.zeros_like(dq)
            yield 3 * h, jnp.where(ent, nothing, dq)
            yield 3 * h + 1, jnp.where(ent, dq, nothing)
            yield 3 * h + 2, dkv_ref[u]
            h += 1


def input_grad_kernel(count, pos_ref, *refs):
    grads, (ent_ref, w_ref, out_ref) = refs[:count], refs[count:]
    ent = ent_ref[...] > 0.5
    cols = [c for _, c in split_columns(list(zip(grads[::2], grads[1::2])), ent)]
    out_ref[0] = dot_nt(jnp.concatenate(cols, 1), w_ref[...]).astype(bf16)


def input_grad(pos, grads, ent, w, far):
    tokens = grads[0].shape[1]
    width, columns = w.shape

    def block(i, pos):
        return i + 2 * (pos[3] ^ far)

    stacked = [pl.BlockSpec((g.shape[0], BLOCK, LANES), lambda i, pos: (0, block(i, pos), 0)) for g in grads]
    return pl.pallas_call(
        functools.partial(input_grad_kernel, len(grads)),
        grid_spec=pltpu.PrefetchScalarGridSpec(
            num_scalar_prefetch=1,
            grid=(2,),
            in_specs=stacked
            + [
                pl.BlockSpec((BLOCK, LANES), lambda i, pos: (block(i, pos), 0)),
                pl.BlockSpec((width, columns), lambda i, pos: (0, 0)),
            ],
            out_specs=pl.BlockSpec((1, BLOCK, width), lambda i, pos: (i ^ (pos[0] % 2), 0, 0)),
        ),
        out_shape=jax.ShapeDtypeStruct((2, BLOCK, width), bf16),
        compiler_params=params(),
        cost_estimate=cost(tokens * width * columns, tokens * (columns + width), short=100),
        name="input_grad",
    )(pos, *grads, ent, w)


def all_sums(pos_ref, bias, sums_ref, gib_ref, out_ref):
    gwidth = bias.shape[1] // 6
    zeros = jnp.zeros((1, gwidth), f32)
    for row, part in enumerate((0, 1, 2, 3, 5)):
        own = bias[:1, gwidth * part : gwidth * (part + 1)]
        out_ref[row : row + 1] = jnp.concatenate(
            [jnp.where(pos_ref[0] == j, own, zeros) for j in range(out_ref.shape[1] // gwidth)], 1
        )
    rest = [sums_ref[i] for i in range(sums_ref.shape[0])] + [gib_ref[i] for i in range(gib_ref.shape[0])]
    for row, value in enumerate(rest):
        out_ref[5 + row : 6 + row] = value
    out_ref[5 + len(rest) :] = jnp.zeros((out_ref.shape[0] - 5 - len(rest), out_ref.shape[1]), f32)


def project_grad_kernel(pos_ref, x0, x1, x2, x3, *refs):
    (
        *grads, ent_ref, sums_ref, gib_ref, keep_ref, first_ref, second_ref, bias_ref, acc_ref, bias_acc,
        x_ref, sems,
    ) = refs
    step = pl.program_id(0)

    @pl.when(step == 0)
    def _():
        loads = copies([(ref, x_ref.at[m]) for m, ref in enumerate((x0, x1, x2, x3))], sems)
        acc_ref[...] = jnp.zeros_like(acc_ref)
        bias_acc[...] = jnp.zeros_like(bias_acc)
        for load in loads:
            load.wait()

    ent = ent_ref[...] > 0.5
    columns = jnp.concatenate([c for _, c in split_columns(list(zip(grads[::2], grads[1::2])), ent)], 1)
    acc_ref[...] += dot_nn(x_ref[step].T, columns)
    bias_acc[:1] += jnp.sum(columns.astype(f32), 0, keepdims=True)

    @pl.when(step == pl.num_programs(0) - 1)
    def _():
        chips, cores, rows, columns = keep_ref.shape
        heads = columns // (3 * LANES)
        all_sums(pos_ref, by_parts(bias_acc[...], heads), sums_ref, gib_ref, bias_ref)
        targets = [
            [keep_ref.at[0, 0], first_ref.at[0], keep_ref.at[1, 0], first_ref.at[1]],
            [keep_ref.at[0, 1], keep_ref.at[1, 1], second_ref.at[0], second_ref.at[1]],
        ]
        for mask in range(4):
            for core in range(2):
                at = block_rows(2 * ((pos_ref[2] // 2) ^ mask) + core, rows)
                targets[core][mask][...] = by_parts(acc_ref[at].astype(bf16), heads)


def project_grad_whole_kernel(*refs):
    *ins, out_ref, bias_ref, acc_ref, bias_acc, x_ref, sems = refs
    heads = out_ref.shape[1] // (3 * LANES)
    pos_ref, x0, x1, x2, x3, *grads, ent_ref, sums_ref, gib_ref = ins
    step = pl.program_id(0)

    @pl.when(step == 0)
    def _():
        loads = copies([(ref, x_ref.at[m]) for m, ref in enumerate((x0, x1, x2, x3))], sems)
        acc_ref[...] = jnp.zeros_like(acc_ref)
        bias_acc[...] = jnp.zeros_like(bias_acc)
        for load in loads:
            load.wait()

    ent = ent_ref[...] > 0.5
    columns = jnp.concatenate([c for _, c in split_columns(list(zip(grads[::2], grads[1::2])), ent)], 1)
    acc_ref[...] += dot_nn(x_ref[step].T, columns)
    bias_acc[:1] += jnp.sum(columns.astype(f32), 0, keepdims=True)

    @pl.when(step == pl.num_programs(0) - 1)
    def _():
        out_ref[...] = by_parts(acc_ref[...].astype(bf16), heads)
        all_sums(pos_ref, by_parts(bias_acc[...], heads), sums_ref, gib_ref, bias_ref)


def project_grad(pos, x, grads, ent, sums, gib, by_hops):
    heads = sum(g.shape[0] for g in grads) // 2
    tokens = grads[0].shape[1]
    own_rows, width = x[0].shape
    columns = 3 * LANES * heads
    rows = width // 8
    shapes = [(2, 2, rows, columns)] + [(2, rows, columns)] * 2 if by_hops else [(width, columns)]
    stacked = [pl.BlockSpec((g.shape[0], own_rows, LANES), lambda m, pos: (0, m ^ pos[0], 0)) for g in grads]

    def fixed(shape):
        return pl.BlockSpec(shape, lambda m, pos: (0,) * len(shape))

    return pl.pallas_call(
        project_grad_kernel if by_hops else project_grad_whole_kernel,
        grid_spec=pltpu.PrefetchScalarGridSpec(
            num_scalar_prefetch=1,
            grid=(len(x),),
            in_specs=[pl.BlockSpec(memory_space=pltpu.HBM)] * 4
            + stacked
            + [pl.BlockSpec((own_rows, LANES), lambda m, pos: (m ^ pos[0], 0))]
            + [fixed(sums.shape), fixed(gib.shape)],
            out_specs=[fixed(shape) for shape in shapes] + [fixed((16, width))],
            scratch_shapes=[
                pltpu.VMEM((width, columns), f32),
                pltpu.VMEM((8, columns), f32),
                pltpu.VMEM((len(x), own_rows, width), bf16),
                pltpu.SemaphoreType.DMA((len(x),)),
            ],
        ),
        out_shape=[jax.ShapeDtypeStruct(shape, bf16) for shape in shapes]
        + [jax.ShapeDtypeStruct((16, width), f32)],
        compiler_params=params(),
        cost_estimate=cost(2 * tokens * width * columns, 2 * tokens * (columns + width)),
        name="project_grad",
    )(pos, *x, *grads, ent, sums, gib)


def finish_project_kernel(kept_ref, arrived_ref, q_ref, k_ref, v_ref):
    total = kept_ref[...].astype(f32) + arrived_ref[...].astype(f32)
    width = k_ref.shape[1]
    for a in range(q_ref.shape[0]):
        q_ref[a] = total[:, width * a : width * (a + 1)]
    k_ref[...] = total[:, 4 * width : 5 * width]
    v_ref[...] = total[:, 5 * width :]


def finish_project(kept, arrived):
    rows, columns = kept.shape
    part = jax.ShapeDtypeStruct((rows, columns // 6), f32)
    return pl.pallas_call(
        finish_project_kernel,
        out_shape=[jax.ShapeDtypeStruct((4, rows, columns // 6), f32), part, part],
        compiler_params=params(),
        cost_estimate=cost(rows * columns, 8 * rows * columns),
        name="finish_project",
    )(kept, arrived)


def finish_ffn_kernel(kept_ref, arrived_ref, inter_ref, output_ref, out_ref):
    total = kept_ref[...].astype(f32) + arrived_ref[...].astype(f32)
    ffn = inter_ref.shape[1]
    inter_ref[...] = total[:, :ffn]
    output_ref[...] = total[:, ffn : 2 * ffn].T
    out_ref[...] = total[:, 2 * ffn :].T


def finish_ffn(kept, arrived, ffn):
    rows, columns = kept.shape
    shape = jax.ShapeDtypeStruct
    return pl.pallas_call(
        finish_ffn_kernel,
        out_shape=[shape((rows, ffn), f32), shape((ffn, rows), f32), shape((columns - 2 * ffn, rows), f32)],
        compiler_params=params(),
        cost_estimate=cost(rows * columns, 8 * rows * columns),
        name="finish_ffn",
    )(kept, arrived)


def local(
    hidden_in, token_types, lengths, cotangent, query_w, query_b, key_w, value_w, value_b, out_w,
    out_b, gain_one, shift_one, inter_w, inter_b, output_w, output_b, gain_two, shift_two,
):
    groups = lax.axis_size("tensor")
    dp = lax.axis_size("dp")
    z = lax.axis_index("tensor")
    d = lax.axis_index("dp")
    half = groups // 2
    core = d % 2
    upper = z // half
    me = z % half + half * core
    own_rows, width = hidden_in.shape
    length = own_rows * groups
    gwidth = query_w.shape[2]
    heads = gwidth // HD
    ffn = inter_w.shape[1]
    rows = key_w.shape[0]
    columns = 2 * ffn + gwidth
    total = dp * groups
    by_hops = dp == 8 and rows % 16 == 0

    def device(dd, zz):
        return dd * groups + zz

    def swapped(dev):
        dd, zz = dev // groups, dev % groups
        return device(dd - dd % 2 + zz // half, zz % half + half * (dd % 2))

    def member(dev, mask):
        dd, zz = dev // groups, dev % groups
        j = (zz % half + half * (dd % 2)) ^ mask
        return device(dd - dd % 2 + j // half, zz - zz % half + j % half)

    stays = core == upper

    def relocate(value):
        moves = [(i, swapped(i)) for i in range(total) if swapped(i) != i]
        return jnp.where(stays, value, lax.ppermute(value, ("dp", "tensor"), moves))

    def to_member(value, mask):
        return lax.ppermute(value, ("dp", "tensor"), [(i, member(i, mask)) for i in range(total)])

    def over_dp(value, mask):
        return lax.ppermute(value, "dp", [(i, i ^ mask) for i in range(dp)])

    def over_z(value, mask):
        return lax.ppermute(value, "tensor", [(i, i ^ mask) for i in range(groups)])

    def add(*terms):
        return functools.reduce(jnp.add, [t.astype(f32) for t in terms])

    def after(value, *others):
        return lax.optimization_barrier((value, *others))[0]

    own_project = jnp.concatenate([*query_w, key_w, value_w], 1)
    own_ffn = jnp.concatenate([inter_w, output_w.T, out_w.T], 1)

    def between(value, pairs):
        return lax.ppermute(value, ("dp", "tensor"), [p for p in pairs if p[0] != p[1]])

    swaps = [(i, swapped(i)) for i in range(total)]
    on_chips = [(i, member(i, 1)) for i in range(total)]
    stay_chips = [p for p in on_chips if swapped(p[0]) == p[0]]
    move_chips = [p for p in on_chips if swapped(p[0]) != p[0]]

    def phase(*values):
        return lax.optimization_barrier(values)

    facts = jnp.concatenate([token_types, lengths])
    facts_moved = over_dp(facts, 1)
    query_b_own = lax.dynamic_slice_in_dim(query_b, me * gwidth, gwidth, 1)
    value_b_own = lax.dynamic_slice_in_dim(value_b, me * gwidth, gwidth)
    b_project = jnp.concatenate([query_b_own.reshape(-1), jnp.zeros((gwidth,), bf16), value_b_own])
    b_project = b_project.reshape(1, 6 * gwidth).astype(f32)
    vectors = jnp.concatenate(
        [
            v.astype(f32).reshape(-1, width // LANES, LANES)
            for v in (out_b, gain_one, shift_one, output_b, gain_two, shift_two, inter_b)
        ]
    )
    to_move = hidden_in
    if by_hops:
        other = over_dp(own_project, 1)
        to_move = after(hidden_in, other)
    near_chip = between(to_move, stay_chips)
    moved = between(to_move, swaps)
    if by_hops:
        pair = jnp.where(core == 0, jnp.stack([own_project, other]), jnp.stack([other, own_project]))
        pair = relocate(pair)
        a, b = pair[0], pair[1]
        own_ffn = after(own_ffn, other)
        own_z = over_z(own_ffn, 1)
        pair_x, pair_y = over_dp(pair, 2), over_dp(pair, 4)
    facts = jnp.where(stays, facts, facts_moved)
    pos = jnp.concatenate([jnp.stack([me, z, d, upper]).astype(jnp.int32), facts[length:]])
    ent = jnp.broadcast_to(facts[:length, None].astype(bf16), (length, LANES))
    valid_own = me * own_rows + jnp.arange(own_rows, dtype=jnp.int32) < facts[length]
    valid_own = jnp.broadcast_to(valid_own[:, None].astype(f32), (own_rows, LANES))
    if by_hops:
        moved, near_chip, pair_x, pair_y, own_z, own_ffn, b_project, vectors, pos, ent, valid_own = phase(
            moved, near_chip, pair_x, pair_y, own_z, own_ffn, b_project, vectors, pos, ent, valid_own
        )
    hidden = jnp.where(stays, hidden_in, moved)
    from_chip = between(hidden, move_chips)
    if by_hops:
        from_chip, a_xy, b_xy, own_x, own_y = phase(
            from_chip, over_dp(pair_x[0], 4), over_dp(pair_y[1], 2), over_dp(own_ffn, 2), over_dp(own_ffn, 4)
        )
        from_chip = jnp.where(stays, near_chip, from_chip)
        x_2, x_3, own_ffn, own_x, own_z = phase(
            to_member(hidden, half), to_member(from_chip, half), own_ffn, own_x, own_z
        )
        both = ((0, 0), (0, 1))
        project_pieces = [pair, pair_x, pair_y, a_xy[None], b_xy[None]]
        project_layout = (both, tuple((1, c) for _, c in both), tuple((2, c) for _, c in both), ((3, 0),), ((3, 1),))
    else:
        project_pieces = [relocate(lax.all_gather(own_project, "dp", axis=0, tiled=True))]
        project_layout = (None,)
        from_chip = jnp.where(stays, near_chip, from_chip)
        x_2, x_3 = to_member(hidden, half), to_member(from_chip, half)
    x = [hidden, from_chip, x_2, x_3]

    qc, kc, kv, w_project = project(pos, x, project_pieces, project_layout, b_project, ent)
    if by_hops:
        token_pieces, token_layout = [], []

        def pieces(group_mask, **by):
            masks = [({"own": 0, "x": 2, "y": 4, "xy": 6}[axes], group_mask) for axes in by]
            token_layout.extend([tuple(masks), tuple((m + 1, g) for m, g in masks)])
            return jnp.stack(list(by.values()))

        qc, far, own_zx, own_zy, own_xy = phase(
            qc, over_z(own_ffn, 2), over_dp(own_z, 2), over_dp(own_z, 4), over_dp(own_x, 4)
        )
        quad = pieces(0, own=own_ffn, x=own_x, y=own_y, xy=own_xy)
        mixed, lse_0 = attend(pos, 0, 1, qc, kc, kv)
        mixed, far_z, far_x, far_y, quad_core = phase(
            mixed, over_z(far, 1), over_dp(far, 2), over_dp(far, 4), over_dp(quad, 1)
        )
        token_pieces += [quad, quad_core]
        mixed, lse_1 = attend(pos, 1, heads - 1, qc, kc, kv, (mixed,))
        mixed, far_zx, far_zy, far_xy, own_zxy, cot = phase(
            mixed, over_dp(far_z, 2), over_dp(far_z, 4), over_dp(far_x, 4), over_dp(own_zy, 2),
            between(after(cotangent, far_x), swaps),
        )
        cot = jnp.where(stays, cotangent, cot)
        quad = pieces(1, own=own_z, x=own_zx, y=own_zy, xy=own_zxy)
        mixed_own, far_zxy, quad_core, cot = phase(
            [mixed[:1]] + [to_member(mixed[m : m + 1], m) for m in range(1, groups)], over_dp(far_zy, 2),
            over_dp(quad, 1), cot
        )
        token_pieces += [quad, quad_core]
        for quad in (
            pieces(2, own=far, x=far_x, y=far_y, xy=far_xy),
            pieces(3, own=far_z, x=far_zx, y=far_zy, xy=far_zxy),
        ):
            token_pieces += [quad, over_dp(quad, 1)]
        token_layout = tuple(token_layout)
    else:
        token_pieces = [lax.all_gather(lax.all_gather(own_ffn, "tensor"), "dp", axis=1, tiled=True)]
        token_layout = (None,)
        mixed, lse_0 = attend(pos, 0, 1, qc, kc, kv)
        mixed, lse_1 = attend(pos, 1, heads - 1, qc, kc, kv, (mixed,))
        mixed_own = [mixed[:1]] + [to_member(mixed[m : m + 1], m) for m in range(1, groups)]
        cot = jnp.where(stays, cotangent, between(cotangent, swaps))
    y, mixt, nb, act, gi, gf, ga, gm, grad_resid_one, sums, gib = per_token(
        pos, mixed_own, hidden, cot, valid_own, vectors, token_pieces, token_layout, groups, columns
    )
    grad_mixed = jnp.concatenate([gm[:1]] + [to_member(gm[m : m + 1], m) for m in range(1, groups)])

    order = ((1, 2), (2, 1))
    if by_hops:
        near, far = weight_grads(pos, nb, gf, ga, act, gi, mixt, dp)
        arrived = over_dp(after(far, grad_mixed), 1)
        grads = attend_back(pos, 0, 1, qc, kc, kv, ent, lse_0, mixed, grad_mixed)
        groups_at = (slice(0, 2), slice(2, 4))
        kept = [add(near[:2, g], arrived[:2, g]).astype(bf16) for g in groups_at]
        sent = [add(near[2:, g], arrived[2:, g]).astype(bf16) for g in groups_at]
        grads, kept, sent, qc, y = phase(grads, kept, sent, qc, y)
        more = attend_back(pos, 1, heads - 1, qc, kc, kv, ent, lse_1, mixed, grad_mixed)
        more, moved, layer_moved = phase(
            more, [over_dp(v, 2 * one) for v, (one, _) in zip(sent, order)], between(y, swaps)
        )
    else:
        ffn_grads = weight_grads_whole(nb, gf, ga, act, gi, mixt)
        ffn_grads = lax.psum_scatter(ffn_grads, "tensor", scatter_dimension=0, tiled=False)
        ffn_grads = lax.psum_scatter(ffn_grads, "dp", scatter_dimension=0, tiled=True)
        grads = attend_back(pos, 0, 1, qc, kc, kv, ent, lse_0, mixed, grad_mixed)
        more = attend_back(pos, 1, heads - 1, qc, kc, kv, ent, lse_1, mixed, grad_mixed)
        layer_moved = between(y, swaps)
    layer_out = jnp.where(stays, y, layer_moved)
    grads = [*grads, *more]

    core_stay = [(i, i ^ groups) for i in range(total) if swapped(i) == i]
    core_move = [(i, i ^ groups) for i in range(total) if swapped(i) != i]
    if by_hops:
        sent = [add(k[1], m[1]).astype(bf16) for k, m in zip(kept, moved)]
        kept = [add(k[0], m[0]).astype(bf16) for k, m in zip(kept, moved)]
        first_x, sent, kept = phase(x[0], sent, kept)
        moved = [over_dp(v, 2 * two) for v, (_, two) in zip(sent, order)]
        project_kept, *project_sent, flat = project_grad(pos, [first_x, *x[1:]], grads, ent, sums, gib, True)
        project_kept, project_sent, flat, moved = phase(project_kept, project_sent, flat, moved)
        kept, sent_z = [add(k, m).astype(bf16) for k, m in zip(kept, moved)]
        kept, sent_z, first, project_sent = phase(kept, sent_z, grads[0], project_sent)
    else:
        project_grads, flat = project_grad(pos, x, grads, ent, sums, gib, False)
        first = grads[0]
    partial_far = input_grad(pos, [first, *grads[1:]], ent, w_project, 1)
    far_core = between(partial_far, core_stay)
    if by_hops:
        arrived = [over_dp(v, 2 * one) for v, (one, _) in zip(project_sent, order)]
        arrived_z = over_z(sent_z, 1)
        far_sum = add(partial_far, far_core)
        far_here, far_there, flat, second = phase(far_sum[0], far_sum[1].astype(bf16), flat, grads[3])
    else:
        far_sum = add(partial_far, far_core)
        far_here, far_there, second = far_sum[0], far_sum[1].astype(bf16), grads[3]
    far_chip = between(far_there, move_chips)
    partial_near = input_grad(pos, [*grads[:3], second], ent, w_project, 0)
    if by_hops:
        partial_near, arrived, arrived_z, hop = phase(partial_near, arrived, arrived_z, over_z(flat, 2))
        flat = flat + hop
        sent = [add(project_kept[1, s], m[1]).astype(bf16) for s, m in enumerate(arrived)]
        project_kept = [add(project_kept[0, s], m[0]).astype(bf16) for s, m in enumerate(arrived)]
        kept_z = add(kept, arrived_z)
        kept_z, last = kept_z[0], kept_z[1].astype(bf16)
        sent, last, flat, partial_near = phase(sent, last, flat, partial_near)
        far_chip, moved, last, near_core = phase(
            far_chip, [over_dp(v, 2 * two) for v, (_, two) in zip(sent, order)], over_z(last, 2),
            between(partial_near, core_move),
        )
        near_sum = add(partial_near, near_core)
        near_here, near_there = near_sum[0], near_sum[1].astype(bf16)
        far_sum = add(far_here, far_chip, grad_resid_one).astype(bf16)
        project_ends = jnp.stack([add(k, m).astype(bf16) for k, m in zip(project_kept, moved)])
        far_sum, project_ends, near_here, near_there, flat = phase(
            far_sum, project_ends, near_here, near_there, flat
        )
        project_moved, far_moved, near_chip, hop = phase(
            between(project_ends, swaps), between(far_sum, swaps), between(near_there, stay_chips),
            over_z(flat, 1),
        )
        flat = flat + hop
        flat = flat + over_dp(flat, 2)
        flat = flat + over_dp(flat, 4)
        flat = flat + over_dp(flat, 1)
        project_ends = jnp.where(stays, project_ends, project_moved)
        project_kept = jnp.where(core == 0, project_ends[0], project_ends[1])
        sent = jnp.where(core == 0, project_ends[1], project_ends[0])
        query_grads, key_grads, value_grads = finish_project(project_kept, over_dp(sent, 1))
        inter_grads, output_grads, out_grads = finish_ffn(kept_z, last, ffn)
    else:
        far_moved = between(add(far_here, far_chip, grad_resid_one).astype(bf16), swaps)
        near_sum = add(partial_near, between(partial_near, core_move))
        near_here = near_sum[0]
        near_chip = between(near_sum[1].astype(bf16), stay_chips)
        project_grads = relocate(project_grads)
        project_grads = lax.psum_scatter(project_grads, "dp", scatter_dimension=0, tiled=True)
        query_grads, key_grads, value_grads = finish_project(project_grads, jnp.zeros_like(project_grads))
        inter_grads, output_grads, out_grads = finish_ffn(ffn_grads, jnp.zeros_like(ffn_grads), ffn)
        flat = lax.psum(flat, ("dp", "tensor"))
    near_sum = add(near_here, near_chip, grad_resid_one)
    grad_hidden = jnp.where(stays, near_sum, far_moved.astype(f32))
    return (
        layer_out,
        grad_hidden,
        query_grads,
        flat[:4],
        key_grads,
        value_grads,
        flat[4],
        out_grads,
        flat[5],
        flat[6],
        flat[7],
        inter_grads,
        flat[11 : 11 + groups].reshape(groups * ffn),
        output_grads,
        flat[8],
        flat[9],
        flat[10],
    )


def solution(mesh):
    weights = P("dp", "tensor")
    tokens = P(("dp", "tensor"), None)
    return jax.shard_map(
        local,
        mesh=mesh,
        in_specs=(
            tokens, P("dp"), P("dp"), tokens, P(None, "dp", "tensor"), P(), weights, weights, P(),
            P("tensor", "dp"), P(), P(), P(), weights, P(), P("tensor", "dp"), P(), P(), P(),
        ),
        out_specs=(
            tokens, tokens, P(None, "dp", "tensor"), P(), weights, weights, P(), P("tensor", "dp"),
            P(), P(), P(), weights, P(), P("tensor", "dp"), P(), P(), P(),
        ),
        check_vma=False,
    )
```

profile of v0, /device:TPU:0, one launch (start us, length us, event | category | flops | bytes accessed | tf_op | source)
XLA Modules:
  0.0 379.0 jit_solution(5095940754472604356)
XLA Ops:
  13.5 4.9 %collective-permute-start.2 = (bf16[512,768]{1,0:T(8,128)(2,1)S(1)}, bf16[512,768]{1,0:T(8,128)(2,1)S(1)}, u32[]{:S(2)}, u32[]{:S(2)}) collective-permute-start(bf16[512,768]{1,0:T(8,128)(2,1)S(1)} %copy-done.12), channel_id=1, source_target_pairs={{0,1},{1,0},{6,7},{7,6},{8,9},{9,8},{14,15},{15,14},{16,17},{17,16... | collective-permute-start | bytes 2359304 | tf_op jit(solution)/shard_map/ppermute | solution.py:820
  25.9 20.5 %collective-permute-done.6 = bf16[96,1728]{1,0:T(8,128)(2,1)S(1)} collective-permute-done((bf16[96,1728]{1,0:T(8,128)(2,1)S(1)}, bf16[96,1728]{1,0:T(8,128)(2,1)S(1)}, u32[]{:S(2)}, u32[]{:S(2)}) %collective-permute-start.6) | collective-permute-done | bytes 331808 | tf_op jit(solution)/shard_map/ppermute | solution.py:808
  48.4 2.9 collective-permute-start.12
  51.3 1.9 collective-permute-start.11
  55.4 10.5 %collective-permute-done.10 = bf16[96,1152]{1,0:T(8,128)(2,1)S(1)} collective-permute-done((bf16[96,1152]{1,0:T(8,128)(2,1)S(1)}, bf16[96,1152]{1,0:T(8,128)(2,1)S(1)}, u32[]{:S(2)}, u32[]{:S(2)}) %collective-permute-start.10) | collective-permute-done | bytes 221216 | tf_op jit(solution)/shard_map/ppermute | solution.py:805
  66.7 1.6 collective-permute-done.13.x2
  69.7 1.7 collective-permute-start.16
  71.4 1.6 collective-permute-start.15
  74.5 11.5 %project.1 = (bf16[3,2048,128]{2,1,0:T(8,128)(2,1)}, bf16[3,2048,128]{2,1,0:T(8,128)(2,1)}, bf16[3,2048,128]{2,1,0:T(8,128)(2,1)}, bf16[768,1152]{1,0:T(8,128)(2,1)}) custom-call(s32[5]{0:T(128)} %concatenate.43.pos_ref, bf16[512,768]{1,0:T(8,128)(2,1)} %copy-done.14, bf16[512,768]{1,0:T(8,128)(2,1)} %copy-done.15, bf16[512,768]{1,0:T(8,128)(2,1)} %copy-done.33, ...), custom_call_target="tpu_custom_call" | custom-call | flops 12683575296 | bytes 7864320 | tf_op jit(solution)/shard_map/project/pallas_call | solution.py:119
  86.0 3.2 collective-permute-done.15
  89.5 1.7 collective-permute-start.21
  93.3 10.1 %attend.2 = (bf16[4,192,512]{2,1,0:T(8,128)(2,1)}, f32[1,1,2048]{2,1,0:T(1,128)}) custom-call(s32[5]{0:T(128)} %concatenate.43.pos_ref, bf16[3,2048,128]{2,1,0:T(8,128)(2,1)} %get-tuple-element.224.q_ref, bf16[3,2048,128]{2,1,0:T(8,128)(2,1)} %get-tuple-element.179.kc_ref, bf16[3,2048,128]{2,1,0:T(8,128)(2,1)} %get-tuple-element.180.kv_ref), custom_call_target="tpu_custom_call" | custom-call | flops 11274289152 | bytes 2097152 | tf_op jit(solution)/shard_map/attend/pallas_call | solution.py:170
  104.9 1.5 collective-permute-start.25
  107.4 17.4 %attend.3 = (bf16[4,192,512]{2,1,0:T(8,128)(2,1)}, f32[2,1,2048]{2,1,0:T(1,128)}) custom-call(s32[5]{0:T(128)} %concatenate.43.pos_ref, bf16[3,2048,128]{2,1,0:T(8,128)(2,1)} %get-tuple-element.224.q_ref, bf16[3,2048,128]{2,1,0:T(8,128)(2,1)} %get-tuple-element.179.kc_ref, ...), custom_call_target="tpu_custom_call", output_to_operand_aliasing={{0}: (4, {})} | custom-call | flops 22548578304 | bytes 4194304 | tf_op jit(solution)/shard_map/attend/pallas_call | solution.py:170
  125.0 4.7 %collective-permute-start.32 = (bf16[4,96,1728]{2,1,0:T(8,128)(2,1)S(1)}, bf16[4,96,1728]{2,1,0:T(8,128)(2,1)S(1)}, u32[]{:S(2)}, u32[]{:S(2)}) collective-permute-start(bf16[4,96,1728]{2,1,0:T(8,128)(2,1)S(1)} %pad_maximum_fusion.1.rest_2_), channel_id=1, source_target_pairs={{0,4},{4,0},{8,12},{12,8},{16,20},{20,16},{24,28},{28,24},{1,5},{5... | collective-permute-start | bytes 3981320 | tf_op jit(solution)/shard_map/ppermute | solution.py:805
  132.2 2.0 collective-permute-start.28
  134.4 4.6 %collective-permute-done.30.m3 = bf16[1,192,512]{2,1,0:T(8,128)(2,1)S(1)} collective-permute-done((bf16[1,192,512]{2,1,0:T(8,128)(2,1)S(1)}, bf16[1,192,512]{2,1,0:T(8,128)(2,1)S(1)}, u32[]{:S(2)}, u32[]{:S(2)}) %collective-permute-start.30) | collective-permute-done | bytes 196640 | tf_op jit(solution)/shard_map/ppermute | solution.py:802
  139.7 3.9 %collective-permute-done.28.m1 = bf16[1,192,512]{2,1,0:T(8,128)(2,1)S(1)} collective-permute-done((bf16[1,192,512]{2,1,0:T(8,128)(2,1)S(1)}, bf16[1,192,512]{2,1,0:T(8,128)(2,1)S(1)}, u32[]{:S(2)}, u32[]{:S(2)}) %collective-permute-start.28) | collective-permute-done | bytes 196640 | tf_op jit(solution)/shard_map/ppermute | solution.py:802
  145.9 1.9 collective-permute-done.34.rest_7_
  148.9 29.8 %per_token.1 = (bf16[512,768]{1,0:T(8,128)(2,1)}, bf16[4,192,512]{2,1,0:T(8,128)(2,1)}, bf16[512,768]{1,0:T(8,128)(2,1)}, bf16[4,512,768]{2,1,0:T(8,128)(2,1)}, ...) custom-call(s32[5]{0:T(128)} %concatenate.43.pos_ref, ...), custom_call_target="tpu_custom_call" | custom-call | flops 38050725888 | bytes 16908288 | tf_op jit(solution)/shard_map/per_token/pallas_call | solution.py:426
  180.3 1.9 collective-permute-start.35
  182.2 12.9 %weight_grads.1 = (bf16[4,4,96,1728]{3,2,1,0:T(8,128)(2,1)}, bf16[4,4,96,1728]{3,2,1,0:T(8,128)(2,1)}) custom-call(s32[5]{0:T(128)} %concatenate.43.pos_ref, bf16[512,768]{1,0:T(8,128)(2,1)} %get-tuple-element.213.nb_ref, bf16[512,768]{1,0:T(8,128)(2,1)} %get-tuple-element.214.gf_ref, bf16[512,768]{1,0:T(8,128)(2,1)} %get-tuple-element.215.ga_ref, ...), custom_call_target="tpu_custom_call" | custom-call | flops 19025362944 | bytes 10616832 | tf_op jit(solution)/shard_map/weight_grads/pallas_call | solution.py:509
  196.2 17.4 %attend_back.2 = (bf16[1,2048,128]{2,1,0:T(8,128)(2,1)}, bf16[1,2048,128]{2,1,0:T(8,128)(2,1)}) custom-call(s32[5]{0:T(128)} %concatenate.43.pos_ref, bf16[3,2048,128]{2,1,0:T(8,128)(2,1)} %get-tuple-element.224.q_ref, bf16[3,2048,128]{2,1,0:T(8,128)(2,1)} %get-tuple-element.179.kc_ref, bf16[3,2048,128]{2,1,0:T(8,128)(2,1)} %get-tuple-element.180.kv_ref, ...), custom_call_target="tpu_custom_call" | custom-call | flops 18790481920 | bytes 4194304 | tf_op jit(solution)/shard_map/attend_back/pallas_call | solution.py:240
  213.7 4.8 %add_convert_fusion = (bf16[2,2,96,1728]{3,2,1,0:T(8,128)(2,1)}, bf16[2,2,96,1728]{3,2,1,0:T(8,128)(2,1)}, bf16[2,2,96,1728]{3,2,1,0:T(8,128)(2,1)}, bf16[2,2,96,1728]{3,2,1,0:T(8,128)(2,1)}) fusion(bf16[4,4,96,1728]{3,2,1,0:T(8,128)(2,1)} %collective-permute-done.38, bf16[4,4,96,1728]{3,2,1,0:T(8,128)(2,1)S(1)} %bitcast.104), kind=kLoop, calls=%fused_computation.2 | loop fusion | flops 10616832 | bytes 15925248 | tf_op jit(solution)/shard_map/convert_element_type | solution.py:939
  218.4 1.5 collective-permute-start.41
  221.9 30.7 %attend_back.3 = (bf16[2,2048,128]{2,1,0:T(8,128)(2,1)}, bf16[2,2048,128]{2,1,0:T(8,128)(2,1)}) custom-call(s32[5]{0:T(128)} %concatenate.43.pos_ref, bf16[3,2048,128]{2,1,0:T(8,128)(2,1)} %get-tuple-element.224.q_ref, bf16[3,2048,128]{2,1,0:T(8,128)(2,1)} %get-tuple-element.179.kc_ref, bf16[3,2048,128]{2,1,0:T(8,128)(2,1)} %get-tuple-element.180.kv_ref, ...), custom_call_target="tpu_custom_call" | custom-call | flops 37580963840 | bytes 8388608 | tf_op jit(solution)/shard_map/attend_back/pallas_call | solution.py:240
  252.7 1.5 collective-permute-done.40
  255.3 3.3 fusion.4
  259.7 10.6 %project_grad.1 = (bf16[2,2,96,1152]{3,2,1,0:T(8,128)(2,1)}, bf16[2,96,1152]{2,1,0:T(8,128)(2,1)}, bf16[2,96,1152]{2,1,0:T(8,128)(2,1)}, f32[16,768]{1,0:T(8,128)}) custom-call(s32[5]{0:T(128)} %concatenate.43.pos_ref, bf16[512,768]{1,0:T(8,128)(2,1)} %copy-done.14, bf16[512,768]{1,0:T(8,128)(2,1)} %copy-done.15, bf16[512,768]{1,0:T(8,128)(2,1)} %copy-done.33, ...), custom_call_target="tpu_custom_call" | custom-call | flops 12683575296 | bytes 7864320 | tf_op jit(solution)/shard_map/project_grad/pallas_call | solution.py:695
  270.4 6.0 %collective-permute-done.42 = bf16[2,96,1728]{2,1,0:T(8,128)(2,1)S(1)} collective-permute-done((bf16[2,96,1728]{2,1,0:T(8,128)(2,1)}, bf16[2,96,1728]{2,1,0:T(8,128)(2,1)S(1)}, u32[]{:S(2)}, u32[]{:S(2)}) %collective-permute-start.42) | collective-permute-done | bytes 663584 | tf_op jit(solution)/shard_map/ppermute | solution.py:805
  277.4 5.9 %input_grad.2 = bf16[2,512,768]{2,1,0:T(8,128)(2,1)} custom-call(s32[5]{0:T(128)} %concatenate.43.pos_ref, bf16[1,2048,128]{2,1,0:T(8,128)(2,1)} %get-tuple-element.254.refs_0_, bf16[1,2048,128]{2,1,0:T(8,128)(2,1)} %get-tuple-element.238.refs_1_, bf16[2,2048,128]{2,1,0:T(8,128)(2,1)} %get-tuple-element.239.refs_2_, ...), custom_call_target="tpu_custom_call" | custom-call | flops 63417876 | bytes 39321 | tf_op jit(solution)/shard_map/input_grad/pallas_call | solution.py:590
  283.3 1.6 collective-permute-start.44
  288.0 1.7 convert_add_fusion.1
  291.3 5.9 %input_grad.3 = bf16[2,512,768]{2,1,0:T(8,128)(2,1)} custom-call(s32[5]{0:T(128)} %concatenate.43.pos_ref, bf16[1,2048,128]{2,1,0:T(8,128)(2,1)} %get-tuple-element.254.refs_0_, bf16[1,2048,128]{2,1,0:T(8,128)(2,1)} %get-tuple-element.238.refs_1_, bf16[2,2048,128]{2,1,0:T(8,128)(2,1)} %get-tuple-element.239.refs_2_, ...), custom_call_target="tpu_custom_call" | custom-call | flops 63417876 | bytes 39321 | tf_op jit(solution)/shard_map/input_grad/pallas_call | solution.py:590
  297.3 6.0 %collective-permute-done.48 = bf16[2,96,1728]{2,1,0:T(8,128)(2,1)S(1)} collective-permute-done((bf16[2,96,1728]{2,1,0:T(8,128)(2,1)S(1)}, bf16[2,96,1728]{2,1,0:T(8,128)(2,1)S(1)}, u32[]{:S(2)}, u32[]{:S(2)}) %collective-permute-start.48) | collective-permute-done | bytes 663584 | tf_op jit(solution)/shard_map/ppermute | solution.py:808
  307.3 5.3 %collective-permute-start.52 = (bf16[96,1728]{1,0:T(8,128)(2,1)S(1)}, bf16[96,1728]{1,0:T(8,128)(2,1)S(1)}, u32[]{:S(2)}, u32[]{:S(2)}) collective-permute-start(bf16[96,1728]{1,0:T(8,128)(2,1)S(1)} %fusion.10), channel_id=1, source_target_pairs={{0,2},{1,3},{2,0},{3,1},{4,6},{5,7},{6,4},{7,5},{8,10},{9,11},{10,... | collective-permute-start | bytes 995336 | tf_op jit(solution)/shard_map/ppermute | solution.py:808
  315.4 3.3 collective-permute-done.50
  319.8 5.0 %collective-permute-done.52.arrived_ref = bf16[96,1728]{1,0:T(8,128)(2,1)S(1)} collective-permute-done((bf16[96,1728]{1,0:T(8,128)(2,1)S(1)}, bf16[96,1728]{1,0:T(8,128)(2,1)S(1)}, u32[]{:S(2)}, u32[]{:S(2)}) %collective-permute-start.52) | collective-permute-done | bytes 331808 | tf_op jit(solution)/shard_map/ppermute | solution.py:808
  330.5 1.5 collective-permute-start.55
  332.0 6.7 %collective-permute-start.56 = (bf16[512,768]{1,0:T(8,128)(2,1)}, bf16[512,768]{1,0:T(8,128)(2,1)}, u32[]{:S(2)}, u32[]{:S(2)}) collective-permute-start(bf16[512,768]{1,0:T(8,128)(2,1)} %fusion.1), channel_id=1, source_target_pairs={{0,1},{1,0},{6,7},{7,6},{8,9},{9,8},{14,15},{15,14},{16,17},{17,16... | collective-permute-start | bytes 2359304 | tf_op jit(solution)/shard_map/ppermute | solution.py:820
  338.7 2.1 broadcast_select_fusion
  343.2 2.2 finish_ffn.1
  345.4 1.9 copy.40
  347.3 11.7 %collective-permute-done.57 = f32[16,768]{1,0:T(8,128)S(1)} collective-permute-done((f32[16,768]{1,0:T(8,128)S(1)}, f32[16,768]{1,0:T(8,128)S(1)}, u32[]{:S(2)}, u32[]{:S(2)}) %collective-permute-start.57) | collective-permute-done | bytes 49184 | tf_op jit(solution)/shard_map/ppermute | solution.py:808
  361.6 1.6 collective-permute-done.59
  365.4 5.0 %collective-permute-start.58 = (bf16[96,1152]{1,0:T(8,128)(2,1)}, bf16[96,1152]{1,0:T(8,128)(2,1)S(1)}, u32[]{:S(2)}, u32[]{:S(2)}) collective-permute-start(bf16[96,1152]{1,0:T(8,128)(2,1)} %get-tuple-element.358), channel_id=1, source_target_pairs={{0,4},{4,0},{8,12},{12,8},{16,20},{20,16},{24,28},{28,24},{1,5},{5... | collective-permute-start | bytes 663560 | tf_op jit(solution)/shard_map/ppermute | solution.py:805
  371.5 2.9 convert_select_fusion
  377.0 1.9 finish_project.1
  (246 shorter events, 75.5 us)
Async XLA Ops:
  2.1 20.9 %collective-permute-start.7 = (s32[2049]{0:T(1024)S(1)}, s32[2049]{0:T(1024)S(1)}, u32[]{:S(2)}, u32[]{:S(2)}) collective-permute-start(s32[2049]{0:T(1024)S(1)} %constant_dynamic-update-slice_fusion.8), channel_id=1, source_target_pairs={{0,4},{4,0},{8,12},{12,8},{16,20},{20,16},{24,28},{28,24},{1,5},{5... | collective-permute-start | bytes 24596 | tf_op jit(solution)/shard_map/ppermute | solution.py:805
  13.5 32.9 %collective-permute-start.2 = (bf16[512,768]{1,0:T(8,128)(2,1)S(1)}, bf16[512,768]{1,0:T(8,128)(2,1)S(1)}, u32[]{:S(2)}, u32[]{:S(2)}) collective-permute-start(bf16[512,768]{1,0:T(8,128)(2,1)S(1)} %copy-done.12), channel_id=1, source_target_pairs={{0,1},{1,0},{6,7},{7,6},{8,9},{9,8},{14,15},{15,14},{16,17},{17,16... | collective-permute-start | bytes 2359304 | tf_op jit(solution)/shard_map/ppermute | solution.py:820
  18.3 28.0 %collective-permute-start.1 = (bf16[512,768]{1,0:T(8,128)(2,1)S(1)}, bf16[512,768]{1,0:T(8,128)(2,1)S(1)}, u32[]{:S(2)}, u32[]{:S(2)}) collective-permute-start(bf16[512,768]{1,0:T(8,128)(2,1)S(1)} %copy-done.12), channel_id=1, source_target_pairs={{2,4},{3,5},{4,2},{5,3},{10,12},{11,13},{12,10},{13,11},{18,20},{1... | collective-permute-start | bytes 2359304 | tf_op jit(solution)/shard_map/ppermute | solution.py:820
  20.0 26.4 %collective-permute-start.5 = (bf16[2,96,1152]{2,1,0:T(8,128)(2,1)}, bf16[2,96,1152]{2,1,0:T(8,128)(2,1)S(1)}, u32[]{:S(2)}, u32[]{:S(2)}) collective-permute-start(bf16[2,96,1152]{2,1,0:T(8,128)(2,1)} %broadcast_select_fusion.5.rest_0_), channel_id=1, source_target_pairs={{0,16},{4,20},{8,24},{12,28},{16,0},{20,4},{24,8},{28,12},{1,17},{... | collective-permute-start | bytes 1327112 | tf_op jit(solution)/shard_map/ppermute | solution.py:805
  21.5 24.9 %collective-permute-start.4 = (bf16[2,96,1152]{2,1,0:T(8,128)(2,1)}, bf16[2,96,1152]{2,1,0:T(8,128)(2,1)}, u32[]{:S(2)}, u32[]{:S(2)}) collective-permute-start(bf16[2,96,1152]{2,1,0:T(8,128)(2,1)} %broadcast_select_fusion.5.rest_0_), channel_id=1, source_target_pairs={{0,8},{4,12},{8,0},{12,4},{16,24},{20,28},{24,16},{28,20},{1,9},{5... | collective-permute-start | bytes 1327112 | tf_op jit(solution)/shard_map/ppermute | solution.py:805
  24.8 21.6 %collective-permute-start.6 = (bf16[96,1728]{1,0:T(8,128)(2,1)S(1)}, bf16[96,1728]{1,0:T(8,128)(2,1)S(1)}, u32[]{:S(2)}, u32[]{:S(2)}) collective-permute-start(bf16[96,1728]{1,0:T(8,128)(2,1)S(1)} %pad_maximum_fusion.6), channel_id=1, source_target_pairs={{0,1},{1,0},{2,3},{3,2},{4,5},{5,4},{6,7},{7,6},{8,9},{9,8},{10,11... | collective-permute-start | bytes 995336 | tf_op jit(solution)/shard_map/ppermute | solution.py:808
  48.4 17.6 %collective-permute-start.12 = (bf16[96,1728]{1,0:T(8,128)(2,1)S(1)}, bf16[96,1728]{1,0:T(8,128)(2,1)S(1)}, u32[]{:S(2)}, u32[]{:S(2)}) collective-permute-start(bf16[96,1728]{1,0:T(8,128)(2,1)S(1)} %pad_maximum_fusion.6), channel_id=1, source_target_pairs={{0,16},{4,20},{8,24},{12,28},{16,0},{20,4},{24,8},{28,12},{1,17},{... | collective-permute-start | bytes 995336 | tf_op jit(solution)/shard_map/ppermute | solution.py:805
  51.3 14.7 %collective-permute-start.11 = (bf16[96,1728]{1,0:T(8,128)(2,1)S(1)}, bf16[96,1728]{1,0:T(8,128)(2,1)S(1)}, u32[]{:S(2)}, u32[]{:S(2)}) collective-permute-start(bf16[96,1728]{1,0:T(8,128)(2,1)S(1)} %pad_maximum_fusion.6), channel_id=1, source_target_pairs={{0,8},{4,12},{8,0},{12,4},{16,24},{20,28},{24,16},{28,20},{1,9},{5... | collective-permute-start | bytes 995336 | tf_op jit(solution)/shard_map/ppermute | solution.py:805
  53.3 12.7 %collective-permute-start.8 = (bf16[512,768]{1,0:T(8,128)(2,1)S(1)}, bf16[512,768]{1,0:T(8,128)(2,1)S(1)}, u32[]{:S(2)}, u32[]{:S(2)}) collective-permute-start(bf16[512,768]{1,0:T(8,128)(2,1)S(1)} %broadcast_select_fusion.3.x0.hid_ref), channel_id=1, source_target_pairs={{2,3},{3,2},{4,5},{5,4},{10,11},{11,10},{12,13},{13,12},{18,19},{1... | collective-permute-start | bytes 2359304 | tf_op jit(solution)/shard_map/ppermute | solution.py:820
  54.1 11.9 %collective-permute-start.10 = (bf16[96,1152]{1,0:T(8,128)(2,1)S(1)}, bf16[96,1152]{1,0:T(8,128)(2,1)S(1)}, u32[]{:S(2)}, u32[]{:S(2)}) collective-permute-start(bf16[96,1152]{1,0:T(8,128)(2,1)S(1)} %slice_bitcast_fusion.3), channel_id=1, source_target_pairs={{0,8},{4,12},{8,0},{12,4},{16,24},{20,28},{24,16},{28,20},{1,9},{5... | collective-permute-start | bytes 663560 | tf_op jit(solution)/shard_map/ppermute | solution.py:805
  55.3 10.7 %collective-permute-start.9 = (bf16[96,1152]{1,0:T(8,128)(2,1)S(1)}, bf16[96,1152]{1,0:T(8,128)(2,1)S(1)}, u32[]{:S(2)}, u32[]{:S(2)}) collective-permute-start(bf16[96,1152]{1,0:T(8,128)(2,1)S(1)} %slice_bitcast_fusion.4), channel_id=1, source_target_pairs={{0,16},{4,20},{8,24},{12,28},{16,0},{20,4},{24,8},{28,12},{1,17},{... | collective-permute-start | bytes 663560 | tf_op jit(solution)/shard_map/ppermute | solution.py:805
  69.4 19.9 %collective-permute-start.17 = (bf16[96,1728]{1,0:T(8,128)(2,1)S(1)}, bf16[96,1728]{1,0:T(8,128)(2,1)S(1)}, u32[]{:S(2)}, u32[]{:S(2)}) collective-permute-start(bf16[96,1728]{1,0:T(8,128)(2,1)S(1)} %collective-permute-done.6), channel_id=1, source_target_pairs={{0,16},{4,20},{8,24},{12,28},{16,0},{20,4},{24,8},{28,12},{1,17},{... | collective-permute-start | bytes 995336 | tf_op jit(solution)/shard_map/ppermute | solution.py:805
  69.7 19.5 %collective-permute-start.16 = (bf16[96,1728]{1,0:T(8,128)(2,1)S(1)}, bf16[96,1728]{1,0:T(8,128)(2,1)S(1)}, u32[]{:S(2)}, u32[]{:S(2)}) collective-permute-start(bf16[96,1728]{1,0:T(8,128)(2,1)S(1)} %collective-permute-done.6), channel_id=1, source_target_pairs={{0,8},{4,12},{8,0},{12,4},{16,24},{20,28},{24,16},{28,20},{1,9},{5... | collective-permute-start | bytes 995336 | tf_op jit(solution)/shard_map/ppermute | solution.py:805
  71.4 17.8 %collective-permute-start.15 = (bf16[96,1728]{1,0:T(8,128)(2,1)S(1)}, bf16[96,1728]{1,0:T(8,128)(2,1)S(1)}, u32[]{:S(2)}, u32[]{:S(2)}) collective-permute-start(bf16[96,1728]{1,0:T(8,128)(2,1)S(1)} %pad_maximum_fusion.6), channel_id=1, source_target_pairs={{0,2},{1,3},{2,0},{3,1},{4,6},{5,7},{6,4},{7,5},{8,10},{9,11},{10,... | collective-permute-start | bytes 995336 | tf_op jit(solution)/shard_map/ppermute | solution.py:808
  73.0 16.3 %collective-permute-start.18 = (bf16[96,1728]{1,0:T(8,128)(2,1)S(1)}, bf16[96,1728]{1,0:T(8,128)(2,1)S(1)}, u32[]{:S(2)}, u32[]{:S(2)}) collective-permute-start(bf16[96,1728]{1,0:T(8,128)(2,1)S(1)} %collective-permute-done.11), channel_id=1, source_target_pairs={{0,16},{4,20},{8,24},{12,28},{16,0},{20,4},{24,8},{28,12},{1,17},{... | collective-permute-start | bytes 995336 | tf_op jit(solution)/shard_map/ppermute | solution.py:805
  89.4 14.0 %collective-permute-start.22 = (bf16[4,96,1728]{2,1,0:T(8,128)(2,1)S(1)}, bf16[4,96,1728]{2,1,0:T(8,128)(2,1)}, u32[]{:S(2)}, u32[]{:S(2)}) collective-permute-start(bf16[4,96,1728]{2,1,0:T(8,128)(2,1)S(1)} %pad_maximum_fusion.rest_0_), channel_id=1, source_target_pairs={{0,4},{4,0},{8,12},{12,8},{16,20},{20,16},{24,28},{28,24},{1,5},{5... | collective-permute-start | bytes 3981320 | tf_op jit(solution)/shard_map/ppermute | solution.py:805
  89.5 13.9 %collective-permute-start.21 = (bf16[96,1728]{1,0:T(8,128)(2,1)S(1)}, bf16[96,1728]{1,0:T(8,128)(2,1)S(1)}, u32[]{:S(2)}, u32[]{:S(2)}) collective-permute-start(bf16[96,1728]{1,0:T(8,128)(2,1)S(1)} %collective-permute-done.15), channel_id=1, source_target_pairs={{0,16},{4,20},{8,24},{12,28},{16,0},{20,4},{24,8},{28,12},{1,17},{... | collective-permute-start | bytes 995336 | tf_op jit(solution)/shard_map/ppermute | solution.py:805
  91.3 12.1 %collective-permute-start.20 = (bf16[96,1728]{1,0:T(8,128)(2,1)S(1)}, bf16[96,1728]{1,0:T(8,128)(2,1)S(1)}, u32[]{:S(2)}, u32[]{:S(2)}) collective-permute-start(bf16[96,1728]{1,0:T(8,128)(2,1)S(1)} %collective-permute-done.15), channel_id=1, source_target_pairs={{0,8},{4,12},{8,0},{12,4},{16,24},{20,28},{24,16},{28,20},{1,9},{5... | collective-permute-start | bytes 995336 | tf_op jit(solution)/shard_map/ppermute | solution.py:805
  91.6 11.8 %collective-permute-start.19 = (bf16[96,1728]{1,0:T(8,128)(2,1)S(1)}, bf16[96,1728]{1,0:T(8,128)(2,1)S(1)}, u32[]{:S(2)}, u32[]{:S(2)}) collective-permute-start(bf16[96,1728]{1,0:T(8,128)(2,1)S(1)} %collective-permute-done.15), channel_id=1, source_target_pairs={{0,1},{1,0},{2,3},{3,2},{4,5},{5,4},{6,7},{7,6},{8,9},{9,8},{10,11... | collective-permute-start | bytes 995336 | tf_op jit(solution)/shard_map/ppermute | solution.py:808
  92.2 32.6 %collective-permute-start.26 = (bf16[96,1728]{1,0:T(8,128)(2,1)S(1)}, bf16[96,1728]{1,0:T(8,128)(2,1)S(1)}, u32[]{:S(2)}, u32[]{:S(2)}) collective-permute-start(bf16[96,1728]{1,0:T(8,128)(2,1)S(1)} %collective-permute-done.17), channel_id=1, source_target_pairs={{0,8},{4,12},{8,0},{12,4},{16,24},{20,28},{24,16},{28,20},{1,9},{5... | collective-permute-start | bytes 995336 | tf_op jit(solution)/shard_map/ppermute | solution.py:805
  103.4 21.4 %collective-permute-start.24 = (bf16[96,1728]{1,0:T(8,128)(2,1)S(1)}, bf16[96,1728]{1,0:T(8,128)(2,1)S(1)}, u32[]{:S(2)}, u32[]{:S(2)}) collective-permute-start(bf16[96,1728]{1,0:T(8,128)(2,1)S(1)} %collective-permute-done.19), channel_id=1, source_target_pairs={{0,16},{4,20},{8,24},{12,28},{16,0},{20,4},{24,8},{28,12},{1,17},{... | collective-permute-start | bytes 995336 | tf_op jit(solution)/shard_map/ppermute | solution.py:805
  103.8 21.0 %collective-permute-start.23 = (bf16[96,1728]{1,0:T(8,128)(2,1)S(1)}, bf16[96,1728]{1,0:T(8,128)(2,1)S(1)}, u32[]{:S(2)}, u32[]{:S(2)}) collective-permute-start(bf16[96,1728]{1,0:T(8,128)(2,1)S(1)} %collective-permute-done.19), channel_id=1, source_target_pairs={{0,8},{4,12},{8,0},{12,4},{16,24},{20,28},{24,16},{28,20},{1,9},{5... | collective-permute-start | bytes 995336 | tf_op jit(solution)/shard_map/ppermute | solution.py:805
  104.9 19.9 %collective-permute-start.25 = (bf16[96,1728]{1,0:T(8,128)(2,1)S(1)}, bf16[96,1728]{1,0:T(8,128)(2,1)S(1)}, u32[]{:S(2)}, u32[]{:S(2)}) collective-permute-start(bf16[96,1728]{1,0:T(8,128)(2,1)S(1)} %collective-permute-done.20), channel_id=1, source_target_pairs={{0,16},{4,20},{8,24},{12,28},{16,0},{20,4},{24,8},{28,12},{1,17},{... | collective-permute-start | bytes 995336 | tf_op jit(solution)/shard_map/ppermute | solution.py:805
  106.5 18.4 %collective-permute-start.27 = (bf16[512,768]{1,0:T(8,128)(2,1)S(1)}, bf16[512,768]{1,0:T(8,128)(2,1)S(1)}, u32[]{:S(2)}, u32[]{:S(2)}) collective-permute-start(bf16[512,768]{1,0:T(8,128)(2,1)S(1)} %copy-done.13), channel_id=1, source_target_pairs={{2,4},{3,5},{4,2},{5,3},{10,12},{11,13},{12,10},{13,11},{18,20},{1... | collective-permute-start | bytes 2359304 | tf_op jit(solution)/shard_map/ppermute | solution.py:820
  125.0 18.5 %collective-permute-start.32 = (bf16[4,96,1728]{2,1,0:T(8,128)(2,1)S(1)}, bf16[4,96,1728]{2,1,0:T(8,128)(2,1)S(1)}, u32[]{:S(2)}, u32[]{:S(2)}) collective-permute-start(bf16[4,96,1728]{2,1,0:T(8,128)(2,1)S(1)} %pad_maximum_fusion.1.rest_2_), channel_id=1, source_target_pairs={{0,4},{4,0},{8,12},{12,8},{16,20},{20,16},{24,28},{28,24},{1,5},{5... | collective-permute-start | bytes 3981320 | tf_op jit(solution)/shard_map/ppermute | solution.py:805
  129.8 13.7 %collective-permute-start.31 = (bf16[96,1728]{1,0:T(8,128)(2,1)S(1)}, bf16[96,1728]{1,0:T(8,128)(2,1)S(1)}, u32[]{:S(2)}, u32[]{:S(2)}) collective-permute-start(bf16[96,1728]{1,0:T(8,128)(2,1)S(1)} %collective-permute-done.24), channel_id=1, source_target_pairs={{0,8},{4,12},{8,0},{12,4},{16,24},{20,28},{24,16},{28,20},{1,9},{5... | collective-permute-start | bytes 995336 | tf_op jit(solution)/shard_map/ppermute | solution.py:805
  132.2 11.3 %collective-permute-start.28 = (bf16[1,192,512]{2,1,0:T(8,128)(2,1)S(1)}, bf16[1,192,512]{2,1,0:T(8,128)(2,1)S(1)}, u32[]{:S(2)}, u32[]{:S(2)}) collective-permute-start(bf16[1,192,512]{2,1,0:T(8,128)(2,1)S(1)} %get-tuple-element.356), channel_id=1, source_target_pairs={{0,1},{1,0},{2,3},{3,2},{4,5},{5,4},{6,7},{7,6},{8,9},{9,8},{10,11... | collective-permute-start | bytes 589832 | tf_op jit(solution)/shard_map/ppermute | solution.py:802
  180.0 15.1 %collective-permute-start.37 = (bf16[1,192,512]{2,1,0:T(8,128)(2,1)S(1)}, bf16[1,192,512]{2,1,0:T(8,128)(2,1)S(1)}, u32[]{:S(2)}, u32[]{:S(2)}) collective-permute-start(bf16[1,192,512]{2,1,0:T(8,128)(2,1)S(1)} %get-tuple-element.351), channel_id=1, source_target_pairs={{0,5},{1,4},{2,7},{3,6},{4,1},{5,0},{6,3},{7,2},{8,13},{9,12},{10,... | collective-permute-start | bytes 589832 | tf_op jit(solution)/shard_map/ppermute | solution.py:802
  180.1 15.0 %collective-permute-start.36 = (bf16[1,192,512]{2,1,0:T(8,128)(2,1)S(1)}, bf16[1,192,512]{2,1,0:T(8,128)(2,1)S(1)}, u32[]{:S(2)}, u32[]{:S(2)}) collective-permute-start(bf16[1,192,512]{2,1,0:T(8,128)(2,1)S(1)} %get-tuple-element.352), channel_id=1, source_target_pairs={{0,4},{1,5},{2,6},{3,7},{4,0},{5,1},{6,2},{7,3},{8,12},{9,13},{10,... | collective-permute-start | bytes 589832 | tf_op jit(solution)/shard_map/ppermute | solution.py:802
  180.3 14.9 %collective-permute-start.35 = (bf16[1,192,512]{2,1,0:T(8,128)(2,1)S(1)}, bf16[1,192,512]{2,1,0:T(8,128)(2,1)S(1)}, u32[]{:S(2)}, u32[]{:S(2)}) collective-permute-start(bf16[1,192,512]{2,1,0:T(8,128)(2,1)S(1)} %get-tuple-element.353), channel_id=1, source_target_pairs={{0,1},{1,0},{2,3},{3,2},{4,5},{5,4},{6,7},{7,6},{8,9},{9,8},{10,11... | collective-permute-start | bytes 589832 | tf_op jit(solution)/shard_map/ppermute | solution.py:802
  196.2 17.5 %collective-permute-start.38 = (bf16[4,4,96,1728]{3,2,1,0:T(8,128)(2,1)}, bf16[4,4,96,1728]{3,2,1,0:T(8,128)(2,1)}, u32[]{:S(2)}, u32[]{:S(2)}) collective-permute-start(bf16[4,4,96,1728]{3,2,1,0:T(8,128)(2,1)} %get-tuple-element.221), channel_id=1, source_target_pairs={{0,4},{4,0},{8,12},{12,8},{16,20},{20,16},{24,28},{28,24},{1,5},{5... | collective-permute-start | bytes 15925256 | tf_op jit(solution)/shard_map/ppermute | solution.py:805
  218.4 34.2 %collective-permute-start.41 = (bf16[512,768]{1,0:T(8,128)(2,1)}, bf16[512,768]{1,0:T(8,128)(2,1)}, u32[]{:S(2)}, u32[]{:S(2)}) collective-permute-start(bf16[512,768]{1,0:T(8,128)(2,1)} %get-tuple-element.223), channel_id=1, source_target_pairs={{2,4},{3,5},{4,2},{5,3},{10,12},{11,13},{12,10},{13,11},{18,20},{1... | collective-permute-start | bytes 2359304 | tf_op jit(solution)/shard_map/ppermute | solution.py:820
  220.0 32.7 %collective-permute-start.39 = (bf16[2,2,96,1728]{3,2,1,0:T(8,128)(2,1)}, bf16[2,2,96,1728]{3,2,1,0:T(8,128)(2,1)S(1)}, u32[]{:S(2)}, u32[]{:S(2)}) collective-permute-start(bf16[2,2,96,1728]{3,2,1,0:T(8,128)(2,1)} %get-tuple-element.228), channel_id=1, source_target_pairs={{0,8},{4,12},{8,0},{12,4},{16,24},{20,28},{24,16},{28,20},{1,9},{5... | collective-permute-start | bytes 3981320 | tf_op jit(solution)/shard_map/ppermute | solution.py:805
  221.4 32.8 %collective-permute-start.40 = (bf16[2,2,96,1728]{3,2,1,0:T(8,128)(2,1)}, bf16[2,2,96,1728]{3,2,1,0:T(8,128)(2,1)S(1)}, u32[]{:S(2)}, u32[]{:S(2)}) collective-permute-start(bf16[2,2,96,1728]{3,2,1,0:T(8,128)(2,1)} %get-tuple-element.229), channel_id=1, source_target_pairs={{0,16},{4,20},{8,24},{12,28},{16,0},{20,4},{24,8},{28,12},{1,17},{... | collective-permute-start | bytes 3981320 | tf_op jit(solution)/shard_map/ppermute | solution.py:805
  258.6 17.8 %collective-permute-start.42 = (bf16[2,96,1728]{2,1,0:T(8,128)(2,1)}, bf16[2,96,1728]{2,1,0:T(8,128)(2,1)S(1)}, u32[]{:S(2)}, u32[]{:S(2)}) collective-permute-start(bf16[2,96,1728]{2,1,0:T(8,128)(2,1)} %get-tuple-element.247), channel_id=1, source_target_pairs={{0,16},{4,20},{8,24},{12,28},{16,0},{20,4},{24,8},{28,12},{1,17},{... | collective-permute-start | bytes 1990664 | tf_op jit(solution)/shard_map/ppermute | solution.py:805
  259.1 17.9 %collective-permute-start.43 = (bf16[2,96,1728]{2,1,0:T(8,128)(2,1)}, bf16[2,96,1728]{2,1,0:T(8,128)(2,1)S(1)}, u32[]{:S(2)}, u32[]{:S(2)}) collective-permute-start(bf16[2,96,1728]{2,1,0:T(8,128)(2,1)} %get-tuple-element.248), channel_id=1, source_target_pairs={{0,8},{4,12},{8,0},{12,4},{16,24},{20,28},{24,16},{28,20},{1,9},{5... | collective-permute-start | bytes 1990664 | tf_op jit(solution)/shard_map/ppermute | solution.py:805
  284.9 12.4 %collective-permute-start.46 = (bf16[2,96,1152]{2,1,0:T(8,128)(2,1)}, bf16[2,96,1152]{2,1,0:T(8,128)(2,1)S(1)}, u32[]{:S(2)}, u32[]{:S(2)}) collective-permute-start(bf16[2,96,1152]{2,1,0:T(8,128)(2,1)} %get-tuple-element.261), channel_id=1, source_target_pairs={{0,8},{4,12},{8,0},{12,4},{16,24},{20,28},{24,16},{28,20},{1,9},{5... | collective-permute-start | bytes 1327112 | tf_op jit(solution)/shard_map/ppermute | solution.py:805
  285.4 11.8 %collective-permute-start.47 = (bf16[2,96,1152]{2,1,0:T(8,128)(2,1)}, bf16[2,96,1152]{2,1,0:T(8,128)(2,1)S(1)}, u32[]{:S(2)}, u32[]{:S(2)}) collective-permute-start(bf16[2,96,1152]{2,1,0:T(8,128)(2,1)} %get-tuple-element.262), channel_id=1, source_target_pairs={{0,16},{4,20},{8,24},{12,28},{16,0},{20,4},{24,8},{28,12},{1,17},{... | collective-permute-start | bytes 1327112 | tf_op jit(solution)/shard_map/ppermute | solution.py:805
  286.5 16.8 %collective-permute-start.48 = (bf16[2,96,1728]{2,1,0:T(8,128)(2,1)S(1)}, bf16[2,96,1728]{2,1,0:T(8,128)(2,1)S(1)}, u32[]{:S(2)}, u32[]{:S(2)}) collective-permute-start(bf16[2,96,1728]{2,1,0:T(8,128)(2,1)S(1)} %add_convert_fusion.5), channel_id=1, source_target_pairs={{0,1},{1,0},{2,3},{3,2},{4,5},{5,4},{6,7},{7,6},{8,9},{9,8},{10,11... | collective-permute-start | bytes 1990664 | tf_op jit(solution)/shard_map/ppermute | solution.py:808
  290.6 12.7 %collective-permute-start.49 = (f32[16,768]{1,0:T(8,128)S(1)}, f32[16,768]{1,0:T(8,128)S(1)}, u32[]{:S(2)}, u32[]{:S(2)}) collective-permute-start(f32[16,768]{1,0:T(8,128)S(1)} %copy-done.28), channel_id=1, source_target_pairs={{0,2},{1,3},{2,0},{3,1},{4,6},{5,7},{6,4},{7,5},{8,10},{9,11},{10,... | collective-permute-start | bytes 147464 | tf_op jit(solution)/shard_map/ppermute | solution.py:808
  305.0 19.8 %collective-permute-start.53 = (bf16[2,512,768]{2,1,0:T(8,128)(2,1)S(1)}, bf16[2,512,768]{2,1,0:T(8,128)(2,1)S(1)}, u32[]{:S(2)}, u32[]{:S(2)}) collective-permute-start(bf16[2,512,768]{2,1,0:T(8,128)(2,1)S(1)} %copy-done.3), channel_id=1, source_target_pairs={{2,6},{3,7},{4,0},{5,1},{10,14},{11,15},{12,8},{13,9},{18,22},{19,... | collective-permute-start | bytes 4718600 | tf_op jit(solution)/shard_map/ppermute | solution.py:820
  306.3 18.5 %collective-permute-start.45 = (bf16[512,768]{1,0:T(8,128)(2,1)S(1)}, bf16[512,768]{1,0:T(8,128)(2,1)S(1)}, u32[]{:S(2)}, u32[]{:S(2)}) collective-permute-start(bf16[512,768]{1,0:T(8,128)(2,1)S(1)} %fusion), channel_id=1, source_target_pairs={{2,3},{3,2},{4,5},{5,4},{10,11},{11,10},{12,13},{13,12},{18,19},{1... | collective-permute-start | bytes 2359304 | tf_op jit(solution)/shard_map/ppermute | solution.py:820
  307.3 17.5 %collective-permute-start.52 = (bf16[96,1728]{1,0:T(8,128)(2,1)S(1)}, bf16[96,1728]{1,0:T(8,128)(2,1)S(1)}, u32[]{:S(2)}, u32[]{:S(2)}) collective-permute-start(bf16[96,1728]{1,0:T(8,128)(2,1)S(1)} %fusion.10), channel_id=1, source_target_pairs={{0,2},{1,3},{2,0},{3,1},{4,6},{5,7},{6,4},{7,5},{8,10},{9,11},{10,... | collective-permute-start | bytes 995336 | tf_op jit(solution)/shard_map/ppermute | solution.py:808
  330.5 28.5 %collective-permute-start.55 = (bf16[512,768]{1,0:T(8,128)(2,1)}, bf16[512,768]{1,0:T(8,128)(2,1)}, u32[]{:S(2)}, u32[]{:S(2)}) collective-permute-start(bf16[512,768]{1,0:T(8,128)(2,1)} %add_convert_fusion.4), channel_id=1, source_target_pairs={{2,4},{3,5},{4,2},{5,3},{10,12},{11,13},{12,10},{13,11},{18,20},{1... | collective-permute-start | bytes 2359304 | tf_op jit(solution)/shard_map/ppermute | solution.py:820
  332.0 27.0 %collective-permute-start.56 = (bf16[512,768]{1,0:T(8,128)(2,1)}, bf16[512,768]{1,0:T(8,128)(2,1)}, u32[]{:S(2)}, u32[]{:S(2)}) collective-permute-start(bf16[512,768]{1,0:T(8,128)(2,1)} %fusion.1), channel_id=1, source_target_pairs={{0,1},{1,0},{6,7},{7,6},{8,9},{9,8},{14,15},{15,14},{16,17},{17,16... | collective-permute-start | bytes 2359304 | tf_op jit(solution)/shard_map/ppermute | solution.py:820
  340.9 18.2 %collective-permute-start.57 = (f32[16,768]{1,0:T(8,128)S(1)}, f32[16,768]{1,0:T(8,128)S(1)}, u32[]{:S(2)}, u32[]{:S(2)}) collective-permute-start(f32[16,768]{1,0:T(8,128)S(1)} %add.133), channel_id=1, source_target_pairs={{0,1},{1,0},{2,3},{3,2},{4,5},{5,4},{6,7},{7,6},{8,9},{9,8},{10,11... | collective-permute-start | bytes 147464 | tf_op jit(solution)/shard_map/ppermute | solution.py:808
  340.9 18.2 %collective-permute-start.54 = (bf16[2,96,1152]{2,1,0:T(8,128)(2,1)}, bf16[2,96,1152]{2,1,0:T(8,128)(2,1)}, u32[]{:S(2)}, u32[]{:S(2)}) collective-permute-start(bf16[2,96,1152]{2,1,0:T(8,128)(2,1)} %pad_maximum_fusion.5), channel_id=1, source_target_pairs={{2,4},{3,5},{4,2},{5,3},{10,12},{11,13},{12,10},{13,11},{18,20},{1... | collective-permute-start | bytes 1327112 | tf_op jit(solution)/shard_map/ppermute | solution.py:820
  365.4 11.0 %collective-permute-start.58 = (bf16[96,1152]{1,0:T(8,128)(2,1)}, bf16[96,1152]{1,0:T(8,128)(2,1)S(1)}, u32[]{:S(2)}, u32[]{:S(2)}) collective-permute-start(bf16[96,1152]{1,0:T(8,128)(2,1)} %get-tuple-element.358), channel_id=1, source_target_pairs={{0,4},{4,0},{8,12},{12,8},{16,20},{20,16},{24,28},{28,24},{1,5},{5... | collective-permute-start | bytes 663560 | tf_op jit(solution)/shard_map/ppermute | solution.py:805
  (56 other events, 405.9 us)
where the time goes:
time: 381 us; the launch traced here: 379 us
  Pallas kernels  157 us (41%)
  waiting for transfers between devices  86 us (23%)
  starting transfers between devices  78.1 us (20%)
  local copies, waits for them, and re-layouts  29.7 us (8%)
  other arithmetic  26.4 us (7%)
    pallas_call x2, Pallas kernels, attend_back(): pl.pallas_call(attend_back_kernel, grid_spec=pltpu.PrefetchScalarGridSpec...  48.2 us
    ppermute x7, waiting for transfers between devices, over_z(): return lax.ppermute(value, 'tensor', [(i, i ^ mask) for i in range(groups)])  46.4 us
    ppermute x35, starting transfers between devices, over_dp(): return lax.ppermute(value, 'dp', [(i, i ^ mask) for i in range(dp)])  41 us
    pallas_call x1, Pallas kernels, per_token(): pl.pallas_call(functools.partial(token_kernel, layout), in_specs=[pl.Bloc...  29.8 us
    pallas_call x2, Pallas kernels, attend(): pl.pallas_call(attend_kernel, grid_spec=pltpu.PrefetchScalarGridSpec(num_...  27.5 us
    ppermute x35, waiting for transfers between devices, over_dp(): return lax.ppermute(value, 'dp', [(i, i ^ mask) for i in range(dp)])  26.8 us
    ppermute x11, starting transfers between devices, between(): lax.ppermute(value, ('dp', 'tensor'), [p for p in pairs if p[0] != p[1]])  22.2 us
    unnamed x93, local copies, waits for them, and re-layouts  16 us
  transfers between devices with their start and end apart: 62, of which 18 were waited for; matrix products, arithmetic and copies ran while one was open for 8% of the time, Pallas kernels for 31%

commit v1 on v0

--- a/solution.py
+++ b/solution.py
@@ -827,43 +827,34 @@
     def phase(*values):
         return lax.optimization_barrier(values)
 
+    near_chip = between(hidden_in, stay_chips)
+    moved = between(hidden_in, swaps)
     facts = jnp.concatenate([token_types, lengths])
     facts_moved = over_dp(facts, 1)
+    few = (query_b, value_b, out_b, gain_one, shift_one, output_b, gain_two, shift_two, inter_b)
+    if by_hops:
+        other = over_dp(own_project, 1)
+        pair = jnp.where(core == 0, jnp.stack([own_project, other]), jnp.stack([other, own_project]))
+        pair, facts_moved, facts, *few = phase(relocate(pair), facts_moved, facts, *few)
+    query_b, value_b, *rest = few
     query_b_own = lax.dynamic_slice_in_dim(query_b, me * gwidth, gwidth, 1)
     value_b_own = lax.dynamic_slice_in_dim(value_b, me * gwidth, gwidth)
     b_project = jnp.concatenate([query_b_own.reshape(-1), jnp.zeros((gwidth,), bf16), value_b_own])
     b_project = b_project.reshape(1, 6 * gwidth).astype(f32)
-    vectors = jnp.concatenate(
-        [
-            v.astype(f32).reshape(-1, width // LANES, LANES)
-            for v in (out_b, gain_one, shift_one, output_b, gain_two, shift_two, inter_b)
-        ]
-    )
-    to_move = hidden_in
-    if by_hops:
-        other = over_dp(own_project, 1)
-        to_move = after(hidden_in, other)
-    near_chip = between(to_move, stay_chips)
-    moved = between(to_move, swaps)
-    if by_hops:
-        pair = jnp.where(core == 0, jnp.stack([own_project, other]), jnp.stack([other, own_project]))
-        pair = relocate(pair)
-        a, b = pair[0], pair[1]
-        own_ffn = after(own_ffn, other)
-        own_z = over_z(own_ffn, 1)
-        pair_x, pair_y = over_dp(pair, 2), over_dp(pair, 4)
+    vectors = jnp.concatenate([v.astype(f32).reshape(-1, width // LANES, LANES) for v in rest])
     facts = jnp.where(stays, facts, facts_moved)
     pos = jnp.concatenate([jnp.stack([me, z, d, upper]).astype(jnp.int32), facts[length:]])
     ent = jnp.broadcast_to(facts[:length, None].astype(bf16), (length, LANES))
     valid_own = me * own_rows + jnp.arange(own_rows, dtype=jnp.int32) < facts[length]
     valid_own = jnp.broadcast_to(valid_own[:, None].astype(f32), (own_rows, LANES))
     if by_hops:
-        moved, near_chip, pair_x, pair_y, own_z, own_ffn, b_project, vectors, pos, ent, valid_own = phase(
-            moved, near_chip, pair_x, pair_y, own_z, own_ffn, b_project, vectors, pos, ent, valid_own
+        moved, near_chip, own_z, own_ffn, b_project, vectors, pos, ent, valid_own = phase(
+            moved, near_chip, over_z(own_ffn, 1), own_ffn, b_project, vectors, pos, ent, valid_own
         )
     hidden = jnp.where(stays, hidden_in, moved)
     from_chip = between(hidden, move_chips)
     if by_hops:
+        pair_x, pair_y = over_dp(pair, 2), over_dp(pair, 4)
         from_chip, a_xy, b_xy, own_x, own_y = phase(
             from_chip, over_dp(pair_x[0], 4), over_dp(pair_y[1], 2), over_dp(own_ffn, 2), over_dp(own_ffn, 4)
         )
@@ -997,14 +988,11 @@
         far_sum, project_ends, near_here, near_there, flat = phase(
             far_sum, project_ends, near_here, near_there, flat
         )
-        project_moved, far_moved, near_chip, hop = phase(
-            between(project_ends, swaps), between(far_sum, swaps), between(near_there, stay_chips),
-            over_z(flat, 1),
-        )
-        flat = flat + hop
-        flat = flat + over_dp(flat, 2)
-        flat = flat + over_dp(flat, 4)
-        flat = flat + over_dp(flat, 1)
+        flat = flat + over_z(flat, 1)
+        for mask in (2, 4, 1):
+            flat = flat + over_dp(flat, mask)
+        project_moved = between(project_ends, swaps)
+        far_moved, near_chip, flat = phase(between(far_sum, swaps), between(near_there, stay_chips), flat)
         project_ends = jnp.where(stays, project_ends, project_moved)
         project_kept = jnp.where(core == 0, project_ends[0], project_ends[1])
         sent = jnp.where(core == 0, project_ends[1], project_ends[0])

time: 381 us -> 371 us (0.974); the launches traced: 379 us -> 364 us
  waiting for transfers between devices: 86 us -> 72 us
    ppermute x7, waiting for transfers between devices: 46.4 us -> 31.3 us  [over_z(): return lax.ppermute(value, 'tensor', [(i, i ^ mask) for i in range(groups)])]
    ppermute x7, starting transfers between devices: 8.69 us -> 15.9 us  [over_z(): return lax.ppermute(value, 'tensor', [(i, i ^ mask) for i in range(groups)])]
    unnamed x93 -> x101, local copies, waits for them, and re-layouts: 16 us -> 11.9 us
  transfers between devices with their start and end apart: 62 -> 62, of which waited for: 18 -> 22; matrix products, arithmetic and copies ran while one was open for 8% -> 6% of each run, Pallas kernels for 31% -> 33%
where the time goes in v1:
time: 371 us; the launch traced here: 364 us
  Pallas kernels  157 us (42%)
  starting transfers between devices  81.2 us (22%)
  waiting for transfers between devices  72 us (19%)
  local copies, waits for them, and re-layouts  26.7 us (7%)
  other arithmetic  25.5 us (7%)
    pallas_call x2, Pallas kernels, attend_back(): pl.pallas_call(attend_back_kernel, grid_spec=pltpu.PrefetchScalarGridSpec...  48.2 us
    ppermute x35, starting transfers between devices, over_dp(): return lax.ppermute(value, 'dp', [(i, i ^ mask) for i in range(dp)])  40.4 us
    ppermute x7, waiting for transfers between devices, over_z(): return lax.ppermute(value, 'tensor', [(i, i ^ mask) for i in range(groups)])  31.3 us
    pallas_call x1, Pallas kernels, per_token(): pl.pallas_call(functools.partial(token_kernel, layout), in_specs=[pl.Bloc...  29.8 us
    pallas_call x2, Pallas kernels, attend(): pl.pallas_call(attend_kernel, grid_spec=pltpu.PrefetchScalarGridSpec(num_...  27.5 us
    ppermute x35, waiting for transfers between devices, over_dp(): return lax.ppermute(value, 'dp', [(i, i ^ mask) for i in range(dp)])  26.6 us
    ppermute x11, starting transfers between devices, between(): lax.ppermute(value, ('dp', 'tensor'), [p for p in pairs if p[0] != p[1]])  18.9 us
    ppermute x7, starting transfers between devices, over_z(): return lax.ppermute(value, 'tensor', [(i, i ^ mask) for i in range(groups)])  15.9 us
  transfers between devices with their start and end apart: 62, of which 22 were waited for; matrix products, arithmetic and copies ran while one was open for 6% of the time, Pallas kernels for 33%

profile of v1, /device:TPU:0, one launch (start us, length us, event | category | flops | bytes accessed | tf_op | source)
XLA Modules:
  0.0 364.0 jit_solution(4476794691884165625)
XLA Ops:
  7.3 4.9 %collective-permute-start.1 = (bf16[512,768]{1,0:T(8,128)(2,1)S(1)}, bf16[512,768]{1,0:T(8,128)(2,1)S(1)}, u32[]{:S(2)}, u32[]{:S(2)}) collective-permute-start(bf16[512,768]{1,0:T(8,128)(2,1)S(1)} %copy-done.12), channel_id=1, source_target_pairs={{0,1},{1,0},{6,7},{7,6},{8,9},{9,8},{14,15},{15,14},{16,17},{17,16... | collective-permute-start | bytes 2359304 | tf_op jit(solution)/shard_map/ppermute | solution.py:820
  12.9 1.7 collective-permute-start.5
  15.6 1.7 collective-permute-start.2
  26.1 15.7 %collective-permute-done.2 = bf16[96,1728]{1,0:T(8,128)(2,1)S(1)} collective-permute-done((bf16[96,1728]{1,0:T(8,128)(2,1)S(1)}, bf16[96,1728]{1,0:T(8,128)(2,1)S(1)}, u32[]{:S(2)}, u32[]{:S(2)}) %collective-permute-start.2) | collective-permute-done | bytes 331808 | tf_op jit(solution)/shard_map/ppermute | solution.py:808
  43.8 1.8 collective-permute-start.12
  50.7 2.1 collective-permute-done.12
  52.8 2.4 collective-permute-done.11
  55.2 3.6 collective-permute-done.10
  59.0 2.2 collective-permute-done.14.x3
  63.3 3.2 collective-permute-start.15
  68.0 11.5 %project.1 = (bf16[3,2048,128]{2,1,0:T(8,128)(2,1)}, bf16[3,2048,128]{2,1,0:T(8,128)(2,1)}, bf16[3,2048,128]{2,1,0:T(8,128)(2,1)}, bf16[768,1152]{1,0:T(8,128)(2,1)}) custom-call(s32[5]{0:T(128)} %concatenate.43.pos_ref, bf16[512,768]{1,0:T(8,128)(2,1)} %copy-done.14, bf16[512,768]{1,0:T(8,128)(2,1)} %copy-done.15, bf16[512,768]{1,0:T(8,128)(2,1)} %copy-done.37, ...), custom_call_target="tpu_custom_call" | custom-call | flops 12683575296 | bytes 7864320 | tf_op jit(solution)/shard_map/project/pallas_call | solution.py:119
  79.5 2.1 collective-permute-done.15
  81.9 1.6 collective-permute-start.21
  85.5 10.1 %attend.2 = (bf16[4,192,512]{2,1,0:T(8,128)(2,1)}, f32[1,1,2048]{2,1,0:T(1,128)}) custom-call(s32[5]{0:T(128)} %concatenate.43.pos_ref, bf16[3,2048,128]{2,1,0:T(8,128)(2,1)} %get-tuple-element.239.q_ref, bf16[3,2048,128]{2,1,0:T(8,128)(2,1)} %get-tuple-element.194.kc_ref, bf16[3,2048,128]{2,1,0:T(8,128)(2,1)} %get-tuple-element.195.kv_ref), custom_call_target="tpu_custom_call" | custom-call | flops 11274289152 | bytes 2097152 | tf_op jit(solution)/shard_map/attend/pallas_call | solution.py:170
  97.2 1.6 collective-permute-start.25
  99.6 17.4 %attend.3 = (bf16[4,192,512]{2,1,0:T(8,128)(2,1)}, f32[2,1,2048]{2,1,0:T(1,128)}) custom-call(s32[5]{0:T(128)} %concatenate.43.pos_ref, bf16[3,2048,128]{2,1,0:T(8,128)(2,1)} %get-tuple-element.239.q_ref, bf16[3,2048,128]{2,1,0:T(8,128)(2,1)} %get-tuple-element.194.kc_ref, ...), custom_call_target="tpu_custom_call", output_to_operand_aliasing={{0}: (4, {})} | custom-call | flops 22548578304 | bytes 4194304 | tf_op jit(solution)/shard_map/attend/pallas_call | solution.py:170
  117.3 4.3 %collective-permute-start.32 = (bf16[4,96,1728]{2,1,0:T(8,128)(2,1)S(1)}, bf16[4,96,1728]{2,1,0:T(8,128)(2,1)S(1)}, u32[]{:S(2)}, u32[]{:S(2)}) collective-permute-start(bf16[4,96,1728]{2,1,0:T(8,128)(2,1)S(1)} %pad_maximum_fusion.1.rest_2_), channel_id=1, source_target_pairs={{0,4},{4,0},{8,12},{12,8},{16,20},{20,16},{24,28},{28,24},{1,5},{5... | collective-permute-start | bytes 3981320 | tf_op jit(solution)/shard_map/ppermute | solution.py:805
  124.3 2.1 collective-permute-start.28
  126.6 4.9 %collective-permute-done.30.m3 = bf16[1,192,512]{2,1,0:T(8,128)(2,1)S(1)} collective-permute-done((bf16[1,192,512]{2,1,0:T(8,128)(2,1)S(1)}, bf16[1,192,512]{2,1,0:T(8,128)(2,1)S(1)}, u32[]{:S(2)}, u32[]{:S(2)}) %collective-permute-start.30) | collective-permute-done | bytes 196640 | tf_op jit(solution)/shard_map/ppermute | solution.py:802
  131.6 4.1 %collective-permute-done.28.m1 = bf16[1,192,512]{2,1,0:T(8,128)(2,1)S(1)} collective-permute-done((bf16[1,192,512]{2,1,0:T(8,128)(2,1)S(1)}, bf16[1,192,512]{2,1,0:T(8,128)(2,1)S(1)}, u32[]{:S(2)}, u32[]{:S(2)}) %collective-permute-start.28) | collective-permute-done | bytes 196640 | tf_op jit(solution)/shard_map/ppermute | solution.py:802
  138.2 1.8 collective-permute-done.34.rest_7_
  141.1 29.8 %per_token.1 = (bf16[512,768]{1,0:T(8,128)(2,1)}, bf16[4,192,512]{2,1,0:T(8,128)(2,1)}, bf16[512,768]{1,0:T(8,128)(2,1)}, bf16[4,512,768]{2,1,0:T(8,128)(2,1)}, ...) custom-call(s32[5]{0:T(128)} %concatenate.43.pos_ref, ...), custom_call_target="tpu_custom_call" | custom-call | flops 38050725888 | bytes 16908288 | tf_op jit(solution)/shard_map/per_token/pallas_call | solution.py:426
  172.5 1.9 collective-permute-start.35
  174.4 12.9 %weight_grads.1 = (bf16[4,4,96,1728]{3,2,1,0:T(8,128)(2,1)}, bf16[4,4,96,1728]{3,2,1,0:T(8,128)(2,1)}) custom-call(s32[5]{0:T(128)} %concatenate.43.pos_ref, bf16[512,768]{1,0:T(8,128)(2,1)} %get-tuple-element.228.nb_ref, bf16[512,768]{1,0:T(8,128)(2,1)} %get-tuple-element.229.gf_ref, bf16[512,768]{1,0:T(8,128)(2,1)} %get-tuple-element.230.ga_ref, ...), custom_call_target="tpu_custom_call" | custom-call | flops 19025362944 | bytes 10616832 | tf_op jit(solution)/shard_map/weight_grads/pallas_call | solution.py:509
  188.3 17.5 %attend_back.2 = (bf16[1,2048,128]{2,1,0:T(8,128)(2,1)}, bf16[1,2048,128]{2,1,0:T(8,128)(2,1)}) custom-call(s32[5]{0:T(128)} %concatenate.43.pos_ref, bf16[3,2048,128]{2,1,0:T(8,128)(2,1)} %get-tuple-element.239.q_ref, bf16[3,2048,128]{2,1,0:T(8,128)(2,1)} %get-tuple-element.194.kc_ref, bf16[3,2048,128]{2,1,0:T(8,128)(2,1)} %get-tuple-element.195.kv_ref, ...), custom_call_target="tpu_custom_call" | custom-call | flops 18790481920 | bytes 4194304 | tf_op jit(solution)/shard_map/attend_back/pallas_call | solution.py:240
  205.8 4.8 %add_convert_fusion = (bf16[2,2,96,1728]{3,2,1,0:T(8,128)(2,1)}, bf16[2,2,96,1728]{3,2,1,0:T(8,128)(2,1)}, bf16[2,2,96,1728]{3,2,1,0:T(8,128)(2,1)}, bf16[2,2,96,1728]{3,2,1,0:T(8,128)(2,1)}) fusion(bf16[4,4,96,1728]{3,2,1,0:T(8,128)(2,1)} %collective-permute-done.38, bf16[4,4,96,1728]{3,2,1,0:T(8,128)(2,1)S(1)} %bitcast.104), kind=kLoop, calls=%fused_computation.2 | loop fusion | flops 10616832 | bytes 15925248 | tf_op jit(solution)/shard_map/convert_element_type | solution.py:930
  213.6 30.7 %attend_back.3 = (bf16[2,2048,128]{2,1,0:T(8,128)(2,1)}, bf16[2,2048,128]{2,1,0:T(8,128)(2,1)}) custom-call(s32[5]{0:T(128)} %concatenate.43.pos_ref, bf16[3,2048,128]{2,1,0:T(8,128)(2,1)} %get-tuple-element.239.q_ref, bf16[3,2048,128]{2,1,0:T(8,128)(2,1)} %get-tuple-element.194.kc_ref, bf16[3,2048,128]{2,1,0:T(8,128)(2,1)} %get-tuple-element.195.kv_ref, ...), custom_call_target="tpu_custom_call" | custom-call | flops 37580963840 | bytes 8388608 | tf_op jit(solution)/shard_map/attend_back/pallas_call | solution.py:240
  247.2 3.3 fusion.4
  252.0 10.6 %project_grad.1 = (bf16[2,2,96,1152]{3,2,1,0:T(8,128)(2,1)}, bf16[2,96,1152]{2,1,0:T(8,128)(2,1)}, bf16[2,96,1152]{2,1,0:T(8,128)(2,1)}, f32[16,768]{1,0:T(8,128)}) custom-call(s32[5]{0:T(128)} %concatenate.43.pos_ref, bf16[512,768]{1,0:T(8,128)(2,1)} %copy-done.14, bf16[512,768]{1,0:T(8,128)(2,1)} %copy-done.15, bf16[512,768]{1,0:T(8,128)(2,1)} %copy-done.37, ...), custom_call_target="tpu_custom_call" | custom-call | flops 12683575296 | bytes 7864320 | tf_op jit(solution)/shard_map/project_grad/pallas_call | solution.py:695
  262.6 5.5 %collective-permute-done.42 = bf16[2,96,1728]{2,1,0:T(8,128)(2,1)S(1)} collective-permute-done((bf16[2,96,1728]{2,1,0:T(8,128)(2,1)}, bf16[2,96,1728]{2,1,0:T(8,128)(2,1)S(1)}, u32[]{:S(2)}, u32[]{:S(2)}) %collective-permute-start.42) | collective-permute-done | bytes 663584 | tf_op jit(solution)/shard_map/ppermute | solution.py:805
  268.8 5.9 %input_grad.2 = bf16[2,512,768]{2,1,0:T(8,128)(2,1)} custom-call(s32[5]{0:T(128)} %concatenate.43.pos_ref, bf16[1,2048,128]{2,1,0:T(8,128)(2,1)} %get-tuple-element.269.refs_0_, bf16[1,2048,128]{2,1,0:T(8,128)(2,1)} %get-tuple-element.253.refs_1_, bf16[2,2048,128]{2,1,0:T(8,128)(2,1)} %get-tuple-element.254.refs_2_, ...), custom_call_target="tpu_custom_call" | custom-call | flops 63417876 | bytes 39321 | tf_op jit(solution)/shard_map/input_grad/pallas_call | solution.py:590
  279.3 1.7 convert_add_fusion.1
  282.8 5.9 %input_grad.3 = bf16[2,512,768]{2,1,0:T(8,128)(2,1)} custom-call(s32[5]{0:T(128)} %concatenate.43.pos_ref, bf16[1,2048,128]{2,1,0:T(8,128)(2,1)} %get-tuple-element.269.refs_0_, bf16[1,2048,128]{2,1,0:T(8,128)(2,1)} %get-tuple-element.253.refs_1_, bf16[2,2048,128]{2,1,0:T(8,128)(2,1)} %get-tuple-element.254.refs_2_, ...), custom_call_target="tpu_custom_call" | custom-call | flops 63417876 | bytes 39321 | tf_op jit(solution)/shard_map/input_grad/pallas_call | solution.py:590
  288.8 6.6 %collective-permute-done.48 = bf16[2,96,1728]{2,1,0:T(8,128)(2,1)S(1)} collective-permute-done((bf16[2,96,1728]{2,1,0:T(8,128)(2,1)S(1)}, bf16[2,96,1728]{2,1,0:T(8,128)(2,1)S(1)}, u32[]{:S(2)}, u32[]{:S(2)}) %collective-permute-start.48) | collective-permute-done | bytes 663584 | tf_op jit(solution)/shard_map/ppermute | solution.py:808
  299.4 5.1 %collective-permute-start.52 = (bf16[96,1728]{1,0:T(8,128)(2,1)S(1)}, bf16[96,1728]{1,0:T(8,128)(2,1)S(1)}, u32[]{:S(2)}, u32[]{:S(2)}) collective-permute-start(bf16[96,1728]{1,0:T(8,128)(2,1)S(1)} %fusion.10), channel_id=1, source_target_pairs={{0,2},{1,3},{2,0},{3,1},{4,6},{5,7},{6,4},{7,5},{8,10},{9,11},{10,... | collective-permute-start | bytes 995336 | tf_op jit(solution)/shard_map/ppermute | solution.py:808
  306.9 3.7 %collective-permute-done.50 = bf16[96,1152]{1,0:T(8,128)(2,1)S(1)} collective-permute-done((bf16[96,1152]{1,0:T(8,128)(2,1)S(1)}, bf16[96,1152]{1,0:T(8,128)(2,1)S(1)}, u32[]{:S(2)}, u32[]{:S(2)}) %collective-permute-start.50) | collective-permute-done | bytes 221216 | tf_op jit(solution)/shard_map/ppermute | solution.py:805
  311.7 4.8 %collective-permute-done.52.arrived_ref = bf16[96,1728]{1,0:T(8,128)(2,1)S(1)} collective-permute-done((bf16[96,1728]{1,0:T(8,128)(2,1)S(1)}, bf16[96,1728]{1,0:T(8,128)(2,1)S(1)}, u32[]{:S(2)}, u32[]{:S(2)}) %collective-permute-start.52) | collective-permute-done | bytes 331808 | tf_op jit(solution)/shard_map/ppermute | solution.py:808
  322.8 5.0 %collective-permute-start.56 = (f32[16,768]{1,0:T(8,128)S(1)}, f32[16,768]{1,0:T(8,128)S(1)}, u32[]{:S(2)}, u32[]{:S(2)}) collective-permute-start(f32[16,768]{1,0:T(8,128)S(1)} %add.133), channel_id=1, source_target_pairs={{0,1},{1,0},{2,3},{3,2},{4,5},{5,4},{6,7},{7,6},{8,9},{9,8},{10,11... | collective-permute-start | bytes 147464 | tf_op jit(solution)/shard_map/ppermute | solution.py:808
  327.7 2.1 collective-permute-done.56
  330.9 3.0 collective-permute-done.57
  335.4 2.1 broadcast_select_fusion
  339.0 4.4 %collective-permute-start.55 = (bf16[512,768]{1,0:T(8,128)(2,1)}, bf16[512,768]{1,0:T(8,128)(2,1)}, u32[]{:S(2)}, u32[]{:S(2)}) collective-permute-start(bf16[512,768]{1,0:T(8,128)(2,1)} %fusion.1), channel_id=1, source_target_pairs={{0,1},{1,0},{6,7},{7,6},{8,9},{9,8},{14,15},{15,14},{16,17},{17,16... | collective-permute-start | bytes 2359304 | tf_op jit(solution)/shard_map/ppermute | solution.py:820
  343.5 4.7 %collective-permute-start.59 = (f32[16,768]{1,0:T(8,128)S(1)}, f32[16,768]{1,0:T(8,128)S(1)}, u32[]{:S(2)}, u32[]{:S(2)}) collective-permute-start(f32[16,768]{1,0:T(8,128)S(1)} %add.143), channel_id=1, source_target_pairs={{0,4},{4,0},{8,12},{12,8},{16,20},{20,16},{24,28},{28,24},{1,5},{5... | collective-permute-start | bytes 147464 | tf_op jit(solution)/shard_map/ppermute | solution.py:805
  350.0 2.2 finish_ffn.1
  352.2 1.9 copy.40
  354.8 1.9 finish_project.1
  356.7 2.4 collective-permute-done.55
  361.0 2.9 convert_select_fusion
  (254 shorter events, 77.7 us)
Async XLA Ops:
  5.2 12.2 %collective-permute-start.4 = (bf16[2,96,1152]{2,1,0:T(8,128)(2,1)}, bf16[2,96,1152]{2,1,0:T(8,128)(2,1)}, u32[]{:S(2)}, u32[]{:S(2)}) collective-permute-start(bf16[2,96,1152]{2,1,0:T(8,128)(2,1)} %maximum_select_fusion), channel_id=1, source_target_pairs={{2,4},{3,5},{4,2},{5,3},{10,12},{11,13},{12,10},{13,11},{18,20},{1... | collective-permute-start | bytes 1327112 | tf_op jit(solution)/shard_map/ppermute | solution.py:799
  6.6 35.1 %collective-permute-start = (bf16[512,768]{1,0:T(8,128)(2,1)S(1)}, bf16[512,768]{1,0:T(8,128)(2,1)S(1)}, u32[]{:S(2)}, u32[]{:S(2)}) collective-permute-start(bf16[512,768]{1,0:T(8,128)(2,1)S(1)} %copy-done.12), channel_id=1, source_target_pairs={{2,4},{3,5},{4,2},{5,3},{10,12},{11,13},{12,10},{13,11},{18,20},{1... | collective-permute-start | bytes 2359304 | tf_op jit(solution)/shard_map/ppermute | solution.py:820
  7.3 34.4 %collective-permute-start.1 = (bf16[512,768]{1,0:T(8,128)(2,1)S(1)}, bf16[512,768]{1,0:T(8,128)(2,1)S(1)}, u32[]{:S(2)}, u32[]{:S(2)}) collective-permute-start(bf16[512,768]{1,0:T(8,128)(2,1)S(1)} %copy-done.12), channel_id=1, source_target_pairs={{0,1},{1,0},{6,7},{7,6},{8,9},{9,8},{14,15},{15,14},{16,17},{17,16... | collective-permute-start | bytes 2359304 | tf_op jit(solution)/shard_map/ppermute | solution.py:820
  15.6 26.1 %collective-permute-start.2 = (bf16[96,1728]{1,0:T(8,128)(2,1)S(1)}, bf16[96,1728]{1,0:T(8,128)(2,1)S(1)}, u32[]{:S(2)}, u32[]{:S(2)}) collective-permute-start(bf16[96,1728]{1,0:T(8,128)(2,1)S(1)} %pad_maximum_fusion.6), channel_id=1, source_target_pairs={{0,1},{1,0},{2,3},{3,2},{4,5},{5,4},{6,7},{7,6},{8,9},{9,8},{10,11... | collective-permute-start | bytes 995336 | tf_op jit(solution)/shard_map/ppermute | solution.py:808
  18.2 29.6 %collective-permute-start.9 = (bf16[2,96,1152]{2,1,0:T(8,128)(2,1)}, bf16[2,96,1152]{2,1,0:T(8,128)(2,1)}, u32[]{:S(2)}, u32[]{:S(2)}) collective-permute-start(bf16[2,96,1152]{2,1,0:T(8,128)(2,1)} %broadcast_select_fusion.5.rest_0_), channel_id=1, source_target_pairs={{0,16},{4,20},{8,24},{12,28},{16,0},{20,4},{24,8},{28,12},{1,17},{... | collective-permute-start | bytes 1327112 | tf_op jit(solution)/shard_map/ppermute | solution.py:805
  19.7 29.7 %collective-permute-start.7 = (bf16[2,96,1152]{2,1,0:T(8,128)(2,1)}, bf16[2,96,1152]{2,1,0:T(8,128)(2,1)}, u32[]{:S(2)}, u32[]{:S(2)}) collective-permute-start(bf16[2,96,1152]{2,1,0:T(8,128)(2,1)} %broadcast_select_fusion.5.rest_0_), channel_id=1, source_target_pairs={{0,8},{4,12},{8,0},{12,4},{16,24},{20,28},{24,16},{28,20},{1,9},{5... | collective-permute-start | bytes 1327112 | tf_op jit(solution)/shard_map/ppermute | solution.py:805
  43.8 9.0 %collective-permute-start.12 = (bf16[96,1728]{1,0:T(8,128)(2,1)S(1)}, bf16[96,1728]{1,0:T(8,128)(2,1)S(1)}, u32[]{:S(2)}, u32[]{:S(2)}) collective-permute-start(bf16[96,1728]{1,0:T(8,128)(2,1)S(1)} %pad_maximum_fusion.6), channel_id=1, source_target_pairs={{0,16},{4,20},{8,24},{12,28},{16,0},{20,4},{24,8},{28,12},{1,17},{... | collective-permute-start | bytes 995336 | tf_op jit(solution)/shard_map/ppermute | solution.py:805
  45.5 9.7 %collective-permute-start.11 = (bf16[96,1728]{1,0:T(8,128)(2,1)S(1)}, bf16[96,1728]{1,0:T(8,128)(2,1)S(1)}, u32[]{:S(2)}, u32[]{:S(2)}) collective-permute-start(bf16[96,1728]{1,0:T(8,128)(2,1)S(1)} %pad_maximum_fusion.6), channel_id=1, source_target_pairs={{0,8},{4,12},{8,0},{12,4},{16,24},{20,28},{24,16},{28,20},{1,9},{5... | collective-permute-start | bytes 995336 | tf_op jit(solution)/shard_map/ppermute | solution.py:805
  47.1 11.7 %collective-permute-start.6 = (bf16[512,768]{1,0:T(8,128)(2,1)S(1)}, bf16[512,768]{1,0:T(8,128)(2,1)S(1)}, u32[]{:S(2)}, u32[]{:S(2)}) collective-permute-start(bf16[512,768]{1,0:T(8,128)(2,1)S(1)} %broadcast_select_fusion.3.x0.hid_ref), channel_id=1, source_target_pairs={{2,3},{3,2},{4,5},{5,4},{10,11},{11,10},{12,13},{13,12},{18,19},{1... | collective-permute-start | bytes 2359304 | tf_op jit(solution)/shard_map/ppermute | solution.py:820
  48.8 10.0 %collective-permute-start.10 = (bf16[96,1152]{1,0:T(8,128)(2,1)S(1)}, bf16[96,1152]{1,0:T(8,128)(2,1)S(1)}, u32[]{:S(2)}, u32[]{:S(2)}) collective-permute-start(bf16[96,1152]{1,0:T(8,128)(2,1)S(1)} %slice_bitcast_fusion.3), channel_id=1, source_target_pairs={{0,8},{4,12},{8,0},{12,4},{16,24},{20,28},{24,16},{28,20},{1,9},{5... | collective-permute-start | bytes 663560 | tf_op jit(solution)/shard_map/ppermute | solution.py:805
  50.4 8.4 %collective-permute-start.8 = (bf16[96,1152]{1,0:T(8,128)(2,1)S(1)}, bf16[96,1152]{1,0:T(8,128)(2,1)S(1)}, u32[]{:S(2)}, u32[]{:S(2)}) collective-permute-start(bf16[96,1152]{1,0:T(8,128)(2,1)S(1)} %slice_bitcast_fusion.4), channel_id=1, source_target_pairs={{0,16},{4,20},{8,24},{12,28},{16,0},{20,4},{24,8},{28,12},{1,17},{... | collective-permute-start | bytes 663560 | tf_op jit(solution)/shard_map/ppermute | solution.py:805
  61.3 20.4 %collective-permute-start.17 = (bf16[96,1728]{1,0:T(8,128)(2,1)S(1)}, bf16[96,1728]{1,0:T(8,128)(2,1)S(1)}, u32[]{:S(2)}, u32[]{:S(2)}) collective-permute-start(bf16[96,1728]{1,0:T(8,128)(2,1)S(1)} %collective-permute-done.2), channel_id=1, source_target_pairs={{0,16},{4,20},{8,24},{12,28},{16,0},{20,4},{24,8},{28,12},{1,17},{... | collective-permute-start | bytes 995336 | tf_op jit(solution)/shard_map/ppermute | solution.py:805
  61.8 19.9 %collective-permute-start.16 = (bf16[96,1728]{1,0:T(8,128)(2,1)S(1)}, bf16[96,1728]{1,0:T(8,128)(2,1)S(1)}, u32[]{:S(2)}, u32[]{:S(2)}) collective-permute-start(bf16[96,1728]{1,0:T(8,128)(2,1)S(1)} %collective-permute-done.2), channel_id=1, source_target_pairs={{0,8},{4,12},{8,0},{12,4},{16,24},{20,28},{24,16},{28,20},{1,9},{5... | collective-permute-start | bytes 995336 | tf_op jit(solution)/shard_map/ppermute | solution.py:805
  63.3 18.3 %collective-permute-start.15 = (bf16[96,1728]{1,0:T(8,128)(2,1)S(1)}, bf16[96,1728]{1,0:T(8,128)(2,1)S(1)}, u32[]{:S(2)}, u32[]{:S(2)}) collective-permute-start(bf16[96,1728]{1,0:T(8,128)(2,1)S(1)} %pad_maximum_fusion.6), channel_id=1, source_target_pairs={{0,2},{1,3},{2,0},{3,1},{4,6},{5,7},{6,4},{7,5},{8,10},{9,11},{10,... | collective-permute-start | bytes 995336 | tf_op jit(solution)/shard_map/ppermute | solution.py:808
  66.4 15.2 %collective-permute-start.18 = (bf16[96,1728]{1,0:T(8,128)(2,1)S(1)}, bf16[96,1728]{1,0:T(8,128)(2,1)S(1)}, u32[]{:S(2)}, u32[]{:S(2)}) collective-permute-start(bf16[96,1728]{1,0:T(8,128)(2,1)S(1)} %collective-permute-done.11), channel_id=1, source_target_pairs={{0,16},{4,20},{8,24},{12,28},{16,0},{20,4},{24,8},{28,12},{1,17},{... | collective-permute-start | bytes 995336 | tf_op jit(solution)/shard_map/ppermute | solution.py:805
  81.8 13.8 %collective-permute-start.22 = (bf16[4,96,1728]{2,1,0:T(8,128)(2,1)S(1)}, bf16[4,96,1728]{2,1,0:T(8,128)(2,1)}, u32[]{:S(2)}, u32[]{:S(2)}) collective-permute-start(bf16[4,96,1728]{2,1,0:T(8,128)(2,1)S(1)} %pad_maximum_fusion.rest_0_), channel_id=1, source_target_pairs={{0,4},{4,0},{8,12},{12,8},{16,20},{20,16},{24,28},{28,24},{1,5},{5... | collective-permute-start | bytes 3981320 | tf_op jit(solution)/shard_map/ppermute | solution.py:805
  81.9 13.7 %collective-permute-start.21 = (bf16[96,1728]{1,0:T(8,128)(2,1)S(1)}, bf16[96,1728]{1,0:T(8,128)(2,1)S(1)}, u32[]{:S(2)}, u32[]{:S(2)}) collective-permute-start(bf16[96,1728]{1,0:T(8,128)(2,1)S(1)} %collective-permute-done.15), channel_id=1, source_target_pairs={{0,16},{4,20},{8,24},{12,28},{16,0},{20,4},{24,8},{28,12},{1,17},{... | collective-permute-start | bytes 995336 | tf_op jit(solution)/shard_map/ppermute | solution.py:805
  83.5 12.1 %collective-permute-start.20 = (bf16[96,1728]{1,0:T(8,128)(2,1)S(1)}, bf16[96,1728]{1,0:T(8,128)(2,1)S(1)}, u32[]{:S(2)}, u32[]{:S(2)}) collective-permute-start(bf16[96,1728]{1,0:T(8,128)(2,1)S(1)} %collective-permute-done.15), channel_id=1, source_target_pairs={{0,8},{4,12},{8,0},{12,4},{16,24},{20,28},{24,16},{28,20},{1,9},{5... | collective-permute-start | bytes 995336 | tf_op jit(solution)/shard_map/ppermute | solution.py:805
  84.5 11.1 %collective-permute-start.19 = (bf16[96,1728]{1,0:T(8,128)(2,1)S(1)}, bf16[96,1728]{1,0:T(8,128)(2,1)S(1)}, u32[]{:S(2)}, u32[]{:S(2)}) collective-permute-start(bf16[96,1728]{1,0:T(8,128)(2,1)S(1)} %collective-permute-done.15), channel_id=1, source_target_pairs={{0,1},{1,0},{2,3},{3,2},{4,5},{5,4},{6,7},{7,6},{8,9},{9,8},{10,11... | collective-permute-start | bytes 995336 | tf_op jit(solution)/shard_map/ppermute | solution.py:808
  84.5 32.6 %collective-permute-start.26 = (bf16[96,1728]{1,0:T(8,128)(2,1)S(1)}, bf16[96,1728]{1,0:T(8,128)(2,1)S(1)}, u32[]{:S(2)}, u32[]{:S(2)}) collective-permute-start(bf16[96,1728]{1,0:T(8,128)(2,1)S(1)} %collective-permute-done.17), channel_id=1, source_target_pairs={{0,8},{4,12},{8,0},{12,4},{16,24},{20,28},{24,16},{28,20},{1,9},{5... | collective-permute-start | bytes 995336 | tf_op jit(solution)/shard_map/ppermute | solution.py:805
  95.6 21.4 %collective-permute-start.24 = (bf16[96,1728]{1,0:T(8,128)(2,1)S(1)}, bf16[96,1728]{1,0:T(8,128)(2,1)S(1)}, u32[]{:S(2)}, u32[]{:S(2)}) collective-permute-start(bf16[96,1728]{1,0:T(8,128)(2,1)S(1)} %collective-permute-done.19), channel_id=1, source_target_pairs={{0,16},{4,20},{8,24},{12,28},{16,0},{20,4},{24,8},{28,12},{1,17},{... | collective-permute-start | bytes 995336 | tf_op jit(solution)/shard_map/ppermute | solution.py:805
  96.2 20.8 %collective-permute-start.23 = (bf16[96,1728]{1,0:T(8,128)(2,1)S(1)}, bf16[96,1728]{1,0:T(8,128)(2,1)S(1)}, u32[]{:S(2)}, u32[]{:S(2)}) collective-permute-start(bf16[96,1728]{1,0:T(8,128)(2,1)S(1)} %collective-permute-done.19), channel_id=1, source_target_pairs={{0,8},{4,12},{8,0},{12,4},{16,24},{20,28},{24,16},{28,20},{1,9},{5... | collective-permute-start | bytes 995336 | tf_op jit(solution)/shard_map/ppermute | solution.py:805
  97.2 19.9 %collective-permute-start.25 = (bf16[96,1728]{1,0:T(8,128)(2,1)S(1)}, bf16[96,1728]{1,0:T(8,128)(2,1)S(1)}, u32[]{:S(2)}, u32[]{:S(2)}) collective-permute-start(bf16[96,1728]{1,0:T(8,128)(2,1)S(1)} %collective-permute-done.20), channel_id=1, source_target_pairs={{0,16},{4,20},{8,24},{12,28},{16,0},{20,4},{24,8},{28,12},{1,17},{... | collective-permute-start | bytes 995336 | tf_op jit(solution)/shard_map/ppermute | solution.py:805
  98.7 18.3 %collective-permute-start.27 = (bf16[512,768]{1,0:T(8,128)(2,1)S(1)}, bf16[512,768]{1,0:T(8,128)(2,1)S(1)}, u32[]{:S(2)}, u32[]{:S(2)}) collective-permute-start(bf16[512,768]{1,0:T(8,128)(2,1)S(1)} %copy-done.13), channel_id=1, source_target_pairs={{2,4},{3,5},{4,2},{5,3},{10,12},{11,13},{12,10},{13,11},{18,20},{1... | collective-permute-start | bytes 2359304 | tf_op jit(solution)/shard_map/ppermute | solution.py:820
  117.3 18.4 %collective-permute-start.32 = (bf16[4,96,1728]{2,1,0:T(8,128)(2,1)S(1)}, bf16[4,96,1728]{2,1,0:T(8,128)(2,1)S(1)}, u32[]{:S(2)}, u32[]{:S(2)}) collective-permute-start(bf16[4,96,1728]{2,1,0:T(8,128)(2,1)S(1)} %pad_maximum_fusion.1.rest_2_), channel_id=1, source_target_pairs={{0,4},{4,0},{8,12},{12,8},{16,20},{20,16},{24,28},{28,24},{1,5},{5... | collective-permute-start | bytes 3981320 | tf_op jit(solution)/shard_map/ppermute | solution.py:805
  121.6 14.1 %collective-permute-start.31 = (bf16[96,1728]{1,0:T(8,128)(2,1)S(1)}, bf16[96,1728]{1,0:T(8,128)(2,1)S(1)}, u32[]{:S(2)}, u32[]{:S(2)}) collective-permute-start(bf16[96,1728]{1,0:T(8,128)(2,1)S(1)} %collective-permute-done.24), channel_id=1, source_target_pairs={{0,8},{4,12},{8,0},{12,4},{16,24},{20,28},{24,16},{28,20},{1,9},{5... | collective-permute-start | bytes 995336 | tf_op jit(solution)/shard_map/ppermute | solution.py:805
  124.3 11.4 %collective-permute-start.28 = (bf16[1,192,512]{2,1,0:T(8,128)(2,1)S(1)}, bf16[1,192,512]{2,1,0:T(8,128)(2,1)S(1)}, u32[]{:S(2)}, u32[]{:S(2)}) collective-permute-start(bf16[1,192,512]{2,1,0:T(8,128)(2,1)S(1)} %get-tuple-element.370), channel_id=1, source_target_pairs={{0,1},{1,0},{2,3},{3,2},{4,5},{5,4},{6,7},{7,6},{8,9},{9,8},{10,11... | collective-permute-start | bytes 589832 | tf_op jit(solution)/shard_map/ppermute | solution.py:802
  172.2 15.1 %collective-permute-start.37 = (bf16[1,192,512]{2,1,0:T(8,128)(2,1)S(1)}, bf16[1,192,512]{2,1,0:T(8,128)(2,1)S(1)}, u32[]{:S(2)}, u32[]{:S(2)}) collective-permute-start(bf16[1,192,512]{2,1,0:T(8,128)(2,1)S(1)} %get-tuple-element.365), channel_id=1, source_target_pairs={{0,5},{1,4},{2,7},{3,6},{4,1},{5,0},{6,3},{7,2},{8,13},{9,12},{10,... | collective-permute-start | bytes 589832 | tf_op jit(solution)/shard_map/ppermute | solution.py:802
  172.3 15.0 %collective-permute-start.36 = (bf16[1,192,512]{2,1,0:T(8,128)(2,1)S(1)}, bf16[1,192,512]{2,1,0:T(8,128)(2,1)S(1)}, u32[]{:S(2)}, u32[]{:S(2)}) collective-permute-start(bf16[1,192,512]{2,1,0:T(8,128)(2,1)S(1)} %get-tuple-element.366), channel_id=1, source_target_pairs={{0,4},{1,5},{2,6},{3,7},{4,0},{5,1},{6,2},{7,3},{8,12},{9,13},{10,... | collective-permute-start | bytes 589832 | tf_op jit(solution)/shard_map/ppermute | solution.py:802
  172.5 14.8 %collective-permute-start.35 = (bf16[1,192,512]{2,1,0:T(8,128)(2,1)S(1)}, bf16[1,192,512]{2,1,0:T(8,128)(2,1)S(1)}, u32[]{:S(2)}, u32[]{:S(2)}) collective-permute-start(bf16[1,192,512]{2,1,0:T(8,128)(2,1)S(1)} %get-tuple-element.367), channel_id=1, source_target_pairs={{0,1},{1,0},{2,3},{3,2},{4,5},{5,4},{6,7},{7,6},{8,9},{9,8},{10,11... | collective-permute-start | bytes 589832 | tf_op jit(solution)/shard_map/ppermute | solution.py:802
  188.3 17.5 %collective-permute-start.38 = (bf16[4,4,96,1728]{3,2,1,0:T(8,128)(2,1)}, bf16[4,4,96,1728]{3,2,1,0:T(8,128)(2,1)}, u32[]{:S(2)}, u32[]{:S(2)}) collective-permute-start(bf16[4,4,96,1728]{3,2,1,0:T(8,128)(2,1)} %get-tuple-element.236), channel_id=1, source_target_pairs={{0,4},{4,0},{8,12},{12,8},{16,20},{20,16},{24,28},{28,24},{1,5},{5... | collective-permute-start | bytes 15925256 | tf_op jit(solution)/shard_map/ppermute | solution.py:805
  210.6 33.8 %collective-permute-start.41 = (bf16[512,768]{1,0:T(8,128)(2,1)}, bf16[512,768]{1,0:T(8,128)(2,1)}, u32[]{:S(2)}, u32[]{:S(2)}) collective-permute-start(bf16[512,768]{1,0:T(8,128)(2,1)} %get-tuple-element.238), channel_id=1, source_target_pairs={{2,4},{3,5},{4,2},{5,3},{10,12},{11,13},{12,10},{13,11},{18,20},{1... | collective-permute-start | bytes 2359304 | tf_op jit(solution)/shard_map/ppermute | solution.py:820
  212.1 32.8 %collective-permute-start.39 = (bf16[2,2,96,1728]{3,2,1,0:T(8,128)(2,1)}, bf16[2,2,96,1728]{3,2,1,0:T(8,128)(2,1)S(1)}, u32[]{:S(2)}, u32[]{:S(2)}) collective-permute-start(bf16[2,2,96,1728]{3,2,1,0:T(8,128)(2,1)} %get-tuple-element.243), channel_id=1, source_target_pairs={{0,8},{4,12},{8,0},{12,4},{16,24},{20,28},{24,16},{28,20},{1,9},{5... | collective-permute-start | bytes 3981320 | tf_op jit(solution)/shard_map/ppermute | solution.py:805
  213.1 33.0 %collective-permute-start.40 = (bf16[2,2,96,1728]{3,2,1,0:T(8,128)(2,1)}, bf16[2,2,96,1728]{3,2,1,0:T(8,128)(2,1)S(1)}, u32[]{:S(2)}, u32[]{:S(2)}) collective-permute-start(bf16[2,2,96,1728]{3,2,1,0:T(8,128)(2,1)} %get-tuple-element.244), channel_id=1, source_target_pairs={{0,16},{4,20},{8,24},{12,28},{16,0},{20,4},{24,8},{28,12},{1,17},{... | collective-permute-start | bytes 3981320 | tf_op jit(solution)/shard_map/ppermute | solution.py:805
  250.5 17.7 %collective-permute-start.42 = (bf16[2,96,1728]{2,1,0:T(8,128)(2,1)}, bf16[2,96,1728]{2,1,0:T(8,128)(2,1)S(1)}, u32[]{:S(2)}, u32[]{:S(2)}) collective-permute-start(bf16[2,96,1728]{2,1,0:T(8,128)(2,1)} %get-tuple-element.262), channel_id=1, source_target_pairs={{0,16},{4,20},{8,24},{12,28},{16,0},{20,4},{24,8},{28,12},{1,17},{... | collective-permute-start | bytes 1990664 | tf_op jit(solution)/shard_map/ppermute | solution.py:805
  250.8 17.6 %collective-permute-start.43 = (bf16[2,96,1728]{2,1,0:T(8,128)(2,1)}, bf16[2,96,1728]{2,1,0:T(8,128)(2,1)S(1)}, u32[]{:S(2)}, u32[]{:S(2)}) collective-permute-start(bf16[2,96,1728]{2,1,0:T(8,128)(2,1)} %get-tuple-element.263), channel_id=1, source_target_pairs={{0,8},{4,12},{8,0},{12,4},{16,24},{20,28},{24,16},{28,20},{1,9},{5... | collective-permute-start | bytes 1990664 | tf_op jit(solution)/shard_map/ppermute | solution.py:805
  276.1 12.6 %collective-permute-start.46 = (bf16[2,96,1152]{2,1,0:T(8,128)(2,1)}, bf16[2,96,1152]{2,1,0:T(8,128)(2,1)S(1)}, u32[]{:S(2)}, u32[]{:S(2)}) collective-permute-start(bf16[2,96,1152]{2,1,0:T(8,128)(2,1)} %get-tuple-element.276), channel_id=1, source_target_pairs={{0,8},{4,12},{8,0},{12,4},{16,24},{20,28},{24,16},{28,20},{1,9},{5... | collective-permute-start | bytes 1327112 | tf_op jit(solution)/shard_map/ppermute | solution.py:805
  277.2 11.6 %collective-permute-start.47 = (bf16[2,96,1152]{2,1,0:T(8,128)(2,1)}, bf16[2,96,1152]{2,1,0:T(8,128)(2,1)S(1)}, u32[]{:S(2)}, u32[]{:S(2)}) collective-permute-start(bf16[2,96,1152]{2,1,0:T(8,128)(2,1)} %get-tuple-element.277), channel_id=1, source_target_pairs={{0,16},{4,20},{8,24},{12,28},{16,0},{20,4},{24,8},{28,12},{1,17},{... | collective-permute-start | bytes 1327112 | tf_op jit(solution)/shard_map/ppermute | solution.py:805
  278.7 16.7 %collective-permute-start.48 = (bf16[2,96,1728]{2,1,0:T(8,128)(2,1)S(1)}, bf16[2,96,1728]{2,1,0:T(8,128)(2,1)S(1)}, u32[]{:S(2)}, u32[]{:S(2)}) collective-permute-start(bf16[2,96,1728]{2,1,0:T(8,128)(2,1)S(1)} %add_convert_fusion.5), channel_id=1, source_target_pairs={{0,1},{1,0},{2,3},{3,2},{4,5},{5,4},{6,7},{7,6},{8,9},{9,8},{10,11... | collective-permute-start | bytes 1990664 | tf_op jit(solution)/shard_map/ppermute | solution.py:808
  281.9 13.5 %collective-permute-start.49 = (f32[16,768]{1,0:T(8,128)S(1)}, f32[16,768]{1,0:T(8,128)S(1)}, u32[]{:S(2)}, u32[]{:S(2)}) collective-permute-start(f32[16,768]{1,0:T(8,128)S(1)} %copy-done.25), channel_id=1, source_target_pairs={{0,2},{1,3},{2,0},{3,1},{4,6},{5,7},{6,4},{7,5},{8,10},{9,11},{10,... | collective-permute-start | bytes 147464 | tf_op jit(solution)/shard_map/ppermute | solution.py:808
  297.1 19.4 %collective-permute-start.53 = (bf16[2,512,768]{2,1,0:T(8,128)(2,1)S(1)}, bf16[2,512,768]{2,1,0:T(8,128)(2,1)S(1)}, u32[]{:S(2)}, u32[]{:S(2)}) collective-permute-start(bf16[2,512,768]{2,1,0:T(8,128)(2,1)S(1)} %copy-done.3), channel_id=1, source_target_pairs={{2,6},{3,7},{4,0},{5,1},{10,14},{11,15},{12,8},{13,9},{18,22},{19,... | collective-permute-start | bytes 4718600 | tf_op jit(solution)/shard_map/ppermute | solution.py:820
  298.4 18.1 %collective-permute-start.45 = (bf16[512,768]{1,0:T(8,128)(2,1)S(1)}, bf16[512,768]{1,0:T(8,128)(2,1)S(1)}, u32[]{:S(2)}, u32[]{:S(2)}) collective-permute-start(bf16[512,768]{1,0:T(8,128)(2,1)S(1)} %fusion), channel_id=1, source_target_pairs={{2,3},{3,2},{4,5},{5,4},{10,11},{11,10},{12,13},{13,12},{18,19},{1... | collective-permute-start | bytes 2359304 | tf_op jit(solution)/shard_map/ppermute | solution.py:820
  299.4 17.2 %collective-permute-start.52 = (bf16[96,1728]{1,0:T(8,128)(2,1)S(1)}, bf16[96,1728]{1,0:T(8,128)(2,1)S(1)}, u32[]{:S(2)}, u32[]{:S(2)}) collective-permute-start(bf16[96,1728]{1,0:T(8,128)(2,1)S(1)} %fusion.10), channel_id=1, source_target_pairs={{0,2},{1,3},{2,0},{3,1},{4,6},{5,7},{6,4},{7,5},{8,10},{9,11},{10,... | collective-permute-start | bytes 995336 | tf_op jit(solution)/shard_map/ppermute | solution.py:808
  322.1 26.1 %collective-permute-start.60 = (bf16[2,96,1152]{2,1,0:T(8,128)(2,1)S(1)}, bf16[2,96,1152]{2,1,0:T(8,128)(2,1)S(1)}, u32[]{:S(2)}, u32[]{:S(2)}) collective-permute-start(bf16[2,96,1152]{2,1,0:T(8,128)(2,1)S(1)} %pad_maximum_fusion.5), channel_id=1, source_target_pairs={{2,4},{3,5},{4,2},{5,3},{10,12},{11,13},{12,10},{13,11},{18,20},{1... | collective-permute-start | bytes 1327112 | tf_op jit(solution)/shard_map/ppermute | solution.py:820
  334.0 9.5 %collective-permute-start.58 = (f32[16,768]{1,0:T(8,128)S(1)}, f32[16,768]{1,0:T(8,128)S(1)}, u32[]{:S(2)}, u32[]{:S(2)}) collective-permute-start(f32[16,768]{1,0:T(8,128)S(1)} %add.142), channel_id=1, source_target_pairs={{0,16},{4,20},{8,24},{12,28},{16,0},{20,4},{24,8},{28,12},{1,17},{... | collective-permute-start | bytes 147464 | tf_op jit(solution)/shard_map/ppermute | solution.py:805
  337.5 19.2 %collective-permute-start.54 = (bf16[512,768]{1,0:T(8,128)(2,1)}, bf16[512,768]{1,0:T(8,128)(2,1)}, u32[]{:S(2)}, u32[]{:S(2)}) collective-permute-start(bf16[512,768]{1,0:T(8,128)(2,1)} %add_convert_fusion.4), channel_id=1, source_target_pairs={{2,4},{3,5},{4,2},{5,3},{10,12},{11,13},{12,10},{13,11},{18,20},{1... | collective-permute-start | bytes 2359304 | tf_op jit(solution)/shard_map/ppermute | solution.py:820
  339.0 20.1 %collective-permute-start.55 = (bf16[512,768]{1,0:T(8,128)(2,1)}, bf16[512,768]{1,0:T(8,128)(2,1)}, u32[]{:S(2)}, u32[]{:S(2)}) collective-permute-start(bf16[512,768]{1,0:T(8,128)(2,1)} %fusion.1), channel_id=1, source_target_pairs={{0,1},{1,0},{6,7},{7,6},{8,9},{9,8},{14,15},{15,14},{16,17},{17,16... | collective-permute-start | bytes 2359304 | tf_op jit(solution)/shard_map/ppermute | solution.py:820
  343.5 10.6 %collective-permute-start.59 = (f32[16,768]{1,0:T(8,128)S(1)}, f32[16,768]{1,0:T(8,128)S(1)}, u32[]{:S(2)}, u32[]{:S(2)}) collective-permute-start(f32[16,768]{1,0:T(8,128)S(1)} %add.143), channel_id=1, source_target_pairs={{0,4},{4,0},{8,12},{12,8},{16,20},{20,16},{24,28},{28,24},{1,5},{5... | collective-permute-start | bytes 147464 | tf_op jit(solution)/shard_map/ppermute | solution.py:805
  (60 other events, 501.3 us)

commit v2 on v1

--- a/solution.py
+++ b/solution.py
@@ -848,15 +848,17 @@
     valid_own = me * own_rows + jnp.arange(own_rows, dtype=jnp.int32) < facts[length]
     valid_own = jnp.broadcast_to(valid_own[:, None].astype(f32), (own_rows, LANES))
     if by_hops:
-        moved, near_chip, own_z, own_ffn, b_project, vectors, pos, ent, valid_own = phase(
-            moved, near_chip, over_z(own_ffn, 1), own_ffn, b_project, vectors, pos, ent, valid_own
+        pair_x, pair_y, b_project, vectors, pos, ent, valid_own = phase(
+            over_dp(pair, 2), over_dp(pair, 4), b_project, vectors, pos, ent, valid_own
+        )
+        moved, near_chip, own_z, own_ffn, a_x, b_y = phase(
+            moved, near_chip, over_z(own_ffn, 1), own_ffn, pair_x[0], pair_y[1]
         )
     hidden = jnp.where(stays, hidden_in, moved)
     from_chip = between(hidden, move_chips)
     if by_hops:
-        pair_x, pair_y = over_dp(pair, 2), over_dp(pair, 4)
         from_chip, a_xy, b_xy, own_x, own_y = phase(
-            from_chip, over_dp(pair_x[0], 4), over_dp(pair_y[1], 2), over_dp(own_ffn, 2), over_dp(own_ffn, 4)
+            from_chip, over_dp(a_x, 4), over_dp(b_y, 2), over_dp(own_ffn, 2), over_dp(own_ffn, 4)
         )
         from_chip = jnp.where(stays, near_chip, from_chip)
         x_2, x_3, own_ffn, own_x, own_z = phase(

time: 371 us -> 369 us (level)
    ppermute x35, waiting for transfers between devices: 26.6 us -> 30.6 us  [over_dp(): return lax.ppermute(value, 'dp', [(i, i ^ mask) for i in range(dp)])]
    unnamed x101 -> x99, local copies, waits for them, and re-layouts: 11.9 us -> 13.4 us
  transfers between devices with their start and end apart: 62 -> 62, of which waited for: 22 -> 23; matrix products, arithmetic and copies ran while one was open for 6% -> 6% of each run, Pallas kernels for 33% -> 33%
where the time goes in v2:
time: 369 us; the launch traced here: 364 us
  Pallas kernels  157 us (43%)
  starting transfers between devices  78.2 us (21%)
  waiting for transfers between devices  74.8 us (20%)
  local copies, waits for them, and re-layouts  27.2 us (7%)
  other arithmetic  24.8 us (7%)
    pallas_call x2, Pallas kernels, attend_back(): pl.pallas_call(attend_back_kernel, grid_spec=pltpu.PrefetchScalarGridSpec...  48.2 us
    ppermute x35, starting transfers between devices, over_dp(): return lax.ppermute(value, 'dp', [(i, i ^ mask) for i in range(dp)])  38.1 us
    ppermute x35, waiting for transfers between devices, over_dp(): return lax.ppermute(value, 'dp', [(i, i ^ mask) for i in range(dp)])  30.6 us
    ppermute x7, waiting for transfers between devices, over_z(): return lax.ppermute(value, 'tensor', [(i, i ^ mask) for i in range(groups)])  30 us
    pallas_call x1, Pallas kernels, per_token(): pl.pallas_call(functools.partial(token_kernel, layout), in_specs=[pl.Bloc...  29.9 us
    pallas_call x2, Pallas kernels, attend(): pl.pallas_call(attend_kernel, grid_spec=pltpu.PrefetchScalarGridSpec(num_...  27.5 us
    ppermute x11, starting transfers between devices, between(): lax.ppermute(value, ('dp', 'tensor'), [p for p in pairs if p[0] != p[1]])  18.9 us
    ppermute x7, starting transfers between devices, over_z(): return lax.ppermute(value, 'tensor', [(i, i ^ mask) for i in range(groups)])  13.6 us
  transfers between devices with their start and end apart: 62, of which 23 were waited for; matrix products, arithmetic and copies ran while one was open for 6% of the time, Pallas kernels for 33%

profile of v2, /device:TPU:0, one launch (start us, length us, event | category | flops | bytes accessed | tf_op | source)
XLA Modules:
  0.0 363.6 jit_solution(8471416384183222363)
XLA Ops:
  7.3 4.9 %collective-permute-start.6 = (bf16[512,768]{1,0:T(8,128)(2,1)S(1)}, bf16[512,768]{1,0:T(8,128)(2,1)S(1)}, u32[]{:S(2)}, u32[]{:S(2)}) collective-permute-start(bf16[512,768]{1,0:T(8,128)(2,1)S(1)} %copy-done.11), channel_id=1, source_target_pairs={{0,1},{1,0},{6,7},{7,6},{8,9},{9,8},{14,15},{15,14},{16,17},{17,16... | collective-permute-start | bytes 2359304 | tf_op jit(solution)/shard_map/ppermute | solution.py:820
  12.8 1.7 collective-permute-start.2
  14.7 1.7 collective-permute-start.7
  17.3 1.5 collective-permute-start.4
  30.4 11.3 %collective-permute-done.7 = bf16[96,1728]{1,0:T(8,128)(2,1)S(1)} collective-permute-done((bf16[96,1728]{1,0:T(8,128)(2,1)S(1)}, bf16[96,1728]{1,0:T(8,128)(2,1)S(1)}, u32[]{:S(2)}, u32[]{:S(2)}) %collective-permute-start.7) | collective-permute-done | bytes 331808 | tf_op jit(solution)/shard_map/ppermute | solution.py:808
  42.6 1.8 collective-permute-start.12
  46.7 10.4 %collective-permute-done.9 = bf16[96,1152]{1,0:T(8,128)(2,1)S(1)} collective-permute-done((bf16[96,1152]{1,0:T(8,128)(2,1)S(1)}, bf16[96,1152]{1,0:T(8,128)(2,1)S(1)}, u32[]{:S(2)}, u32[]{:S(2)}) %collective-permute-start.9) | collective-permute-done | bytes 221216 | tf_op jit(solution)/shard_map/ppermute | solution.py:805
  60.3 1.8 collective-permute-done.14.x3
  63.1 1.6 collective-permute-start.16
  67.0 11.5 %project.1 = (bf16[3,2048,128]{2,1,0:T(8,128)(2,1)}, bf16[3,2048,128]{2,1,0:T(8,128)(2,1)}, bf16[3,2048,128]{2,1,0:T(8,128)(2,1)}, bf16[768,1152]{1,0:T(8,128)(2,1)}) custom-call(s32[5]{0:T(128)} %concatenate.42.pos_ref, bf16[512,768]{1,0:T(8,128)(2,1)} %copy-done.13, bf16[512,768]{1,0:T(8,128)(2,1)} %copy-done.14, bf16[512,768]{1,0:T(8,128)(2,1)} %copy-done.37, ...), custom_call_target="tpu_custom_call" | custom-call | flops 12683575296 | bytes 7864320 | tf_op jit(solution)/shard_map/project/pallas_call | solution.py:119
  78.5 4.3 %collective-permute-done.15 = bf16[96,1728]{1,0:T(8,128)(2,1)S(1)} collective-permute-done((bf16[96,1728]{1,0:T(8,128)(2,1)S(1)}, bf16[96,1728]{1,0:T(8,128)(2,1)S(1)}, u32[]{:S(2)}, u32[]{:S(2)}) %collective-permute-start.15) | collective-permute-done | bytes 331808 | tf_op jit(solution)/shard_map/ppermute | solution.py:808
  86.1 10.1 %attend.2 = (bf16[4,192,512]{2,1,0:T(8,128)(2,1)}, f32[1,1,2048]{2,1,0:T(1,128)}) custom-call(s32[5]{0:T(128)} %concatenate.42.pos_ref, bf16[3,2048,128]{2,1,0:T(8,128)(2,1)} %get-tuple-element.247.q_ref, bf16[3,2048,128]{2,1,0:T(8,128)(2,1)} %get-tuple-element.202.kc_ref, bf16[3,2048,128]{2,1,0:T(8,128)(2,1)} %get-tuple-element.203.kv_ref), custom_call_target="tpu_custom_call" | custom-call | flops 11274289152 | bytes 2097152 | tf_op jit(solution)/shard_map/attend/pallas_call | solution.py:170
  99.7 17.4 %attend.3 = (bf16[4,192,512]{2,1,0:T(8,128)(2,1)}, f32[2,1,2048]{2,1,0:T(1,128)}) custom-call(s32[5]{0:T(128)} %concatenate.42.pos_ref, bf16[3,2048,128]{2,1,0:T(8,128)(2,1)} %get-tuple-element.247.q_ref, bf16[3,2048,128]{2,1,0:T(8,128)(2,1)} %get-tuple-element.202.kc_ref, ...), custom_call_target="tpu_custom_call", output_to_operand_aliasing={{0}: (4, {})} | custom-call | flops 22548578304 | bytes 4194304 | tf_op jit(solution)/shard_map/attend/pallas_call | solution.py:170
  118.4 4.3 %collective-permute-start.32 = (bf16[4,96,1728]{2,1,0:T(8,128)(2,1)S(1)}, bf16[4,96,1728]{2,1,0:T(8,128)(2,1)S(1)}, u32[]{:S(2)}, u32[]{:S(2)}) collective-permute-start(bf16[4,96,1728]{2,1,0:T(8,128)(2,1)S(1)} %pad_maximum_fusion.1.rest_2_), channel_id=1, source_target_pairs={{0,4},{4,0},{8,12},{12,8},{16,20},{20,16},{24,28},{28,24},{1,5},{5... | collective-permute-start | bytes 3981320 | tf_op jit(solution)/shard_map/ppermute | solution.py:805
  122.7 1.5 collective-permute-start.31
  125.9 2.1 collective-permute-start.28
  129.2 3.9 %collective-permute-done.30.m3 = bf16[1,192,512]{2,1,0:T(8,128)(2,1)S(1)} collective-permute-done((bf16[1,192,512]{2,1,0:T(8,128)(2,1)S(1)}, bf16[1,192,512]{2,1,0:T(8,128)(2,1)S(1)}, u32[]{:S(2)}, u32[]{:S(2)}) %collective-permute-start.30) | collective-permute-done | bytes 196640 | tf_op jit(solution)/shard_map/ppermute | solution.py:802
  133.1 4.1 %collective-permute-done.28.m1 = bf16[1,192,512]{2,1,0:T(8,128)(2,1)S(1)} collective-permute-done((bf16[1,192,512]{2,1,0:T(8,128)(2,1)S(1)}, bf16[1,192,512]{2,1,0:T(8,128)(2,1)S(1)}, u32[]{:S(2)}, u32[]{:S(2)}) %collective-permute-start.28) | collective-permute-done | bytes 196640 | tf_op jit(solution)/shard_map/ppermute | solution.py:802
  139.8 1.8 collective-permute-done.34.rest_7_
  142.6 29.9 %per_token.1 = (bf16[512,768]{1,0:T(8,128)(2,1)}, bf16[4,192,512]{2,1,0:T(8,128)(2,1)}, bf16[512,768]{1,0:T(8,128)(2,1)}, bf16[4,512,768]{2,1,0:T(8,128)(2,1)}, ...) custom-call(s32[5]{0:T(128)} %concatenate.42.pos_ref, ...), custom_call_target="tpu_custom_call" | custom-call | flops 38050725888 | bytes 16908288 | tf_op jit(solution)/shard_map/per_token/pallas_call | solution.py:426
  174.1 1.9 collective-permute-start.35
  176.0 12.8 %weight_grads.1 = (bf16[4,4,96,1728]{3,2,1,0:T(8,128)(2,1)}, bf16[4,4,96,1728]{3,2,1,0:T(8,128)(2,1)}) custom-call(s32[5]{0:T(128)} %concatenate.42.pos_ref, bf16[512,768]{1,0:T(8,128)(2,1)} %get-tuple-element.236.nb_ref, bf16[512,768]{1,0:T(8,128)(2,1)} %get-tuple-element.237.gf_ref, bf16[512,768]{1,0:T(8,128)(2,1)} %get-tuple-element.238.ga_ref, ...), custom_call_target="tpu_custom_call" | custom-call | flops 19025362944 | bytes 10616832 | tf_op jit(solution)/shard_map/weight_grads/pallas_call | solution.py:509
  189.8 17.4 %attend_back.2 = (bf16[1,2048,128]{2,1,0:T(8,128)(2,1)}, bf16[1,2048,128]{2,1,0:T(8,128)(2,1)}) custom-call(s32[5]{0:T(128)} %concatenate.42.pos_ref, bf16[3,2048,128]{2,1,0:T(8,128)(2,1)} %get-tuple-element.247.q_ref, bf16[3,2048,128]{2,1,0:T(8,128)(2,1)} %get-tuple-element.202.kc_ref, bf16[3,2048,128]{2,1,0:T(8,128)(2,1)} %get-tuple-element.203.kv_ref, ...), custom_call_target="tpu_custom_call" | custom-call | flops 18790481920 | bytes 4194304 | tf_op jit(solution)/shard_map/attend_back/pallas_call | solution.py:240
  207.3 4.8 %add_convert_fusion = (bf16[2,2,96,1728]{3,2,1,0:T(8,128)(2,1)}, bf16[2,2,96,1728]{3,2,1,0:T(8,128)(2,1)}, bf16[2,2,96,1728]{3,2,1,0:T(8,128)(2,1)}, bf16[2,2,96,1728]{3,2,1,0:T(8,128)(2,1)}) fusion(bf16[4,4,96,1728]{3,2,1,0:T(8,128)(2,1)} %collective-permute-done.38, bf16[4,4,96,1728]{3,2,1,0:T(8,128)(2,1)S(1)} %bitcast.104), kind=kLoop, calls=%fused_computation.2 | loop fusion | flops 10616832 | bytes 15925248 | tf_op jit(solution)/shard_map/convert_element_type | solution.py:932
  214.4 30.7 %attend_back.3 = (bf16[2,2048,128]{2,1,0:T(8,128)(2,1)}, bf16[2,2048,128]{2,1,0:T(8,128)(2,1)}) custom-call(s32[5]{0:T(128)} %concatenate.42.pos_ref, bf16[3,2048,128]{2,1,0:T(8,128)(2,1)} %get-tuple-element.247.q_ref, bf16[3,2048,128]{2,1,0:T(8,128)(2,1)} %get-tuple-element.202.kc_ref, bf16[3,2048,128]{2,1,0:T(8,128)(2,1)} %get-tuple-element.203.kv_ref, ...), custom_call_target="tpu_custom_call" | custom-call | flops 37580963840 | bytes 8388608 | tf_op jit(solution)/shard_map/attend_back/pallas_call | solution.py:240
  250.5 10.6 %project_grad.1 = (bf16[2,2,96,1152]{3,2,1,0:T(8,128)(2,1)}, bf16[2,96,1152]{2,1,0:T(8,128)(2,1)}, bf16[2,96,1152]{2,1,0:T(8,128)(2,1)}, f32[16,768]{1,0:T(8,128)}) custom-call(s32[5]{0:T(128)} %concatenate.42.pos_ref, bf16[512,768]{1,0:T(8,128)(2,1)} %copy-done.13, bf16[512,768]{1,0:T(8,128)(2,1)} %copy-done.14, bf16[512,768]{1,0:T(8,128)(2,1)} %copy-done.37, ...), custom_call_target="tpu_custom_call" | custom-call | flops 12683575296 | bytes 7864320 | tf_op jit(solution)/shard_map/project_grad/pallas_call | solution.py:695
  261.2 4.5 %collective-permute-done.42 = bf16[2,96,1728]{2,1,0:T(8,128)(2,1)S(1)} collective-permute-done((bf16[2,96,1728]{2,1,0:T(8,128)(2,1)}, bf16[2,96,1728]{2,1,0:T(8,128)(2,1)S(1)}, u32[]{:S(2)}, u32[]{:S(2)}) %collective-permute-start.42) | collective-permute-done | bytes 663584 | tf_op jit(solution)/shard_map/ppermute | solution.py:805
  267.4 5.9 %input_grad.2 = bf16[2,512,768]{2,1,0:T(8,128)(2,1)} custom-call(s32[5]{0:T(128)} %concatenate.42.pos_ref, bf16[1,2048,128]{2,1,0:T(8,128)(2,1)} %get-tuple-element.277.refs_0_, bf16[1,2048,128]{2,1,0:T(8,128)(2,1)} %get-tuple-element.261.refs_1_, bf16[2,2048,128]{2,1,0:T(8,128)(2,1)} %get-tuple-element.262.refs_2_, ...), custom_call_target="tpu_custom_call" | custom-call | flops 63417876 | bytes 39321 | tf_op jit(solution)/shard_map/input_grad/pallas_call | solution.py:590
  273.3 2.2 collective-permute-start.44
  275.5 1.5 collective-permute-start.46
  278.6 1.7 convert_add_fusion.1
  281.7 5.9 %input_grad.3 = bf16[2,512,768]{2,1,0:T(8,128)(2,1)} custom-call(s32[5]{0:T(128)} %concatenate.42.pos_ref, bf16[1,2048,128]{2,1,0:T(8,128)(2,1)} %get-tuple-element.277.refs_0_, bf16[1,2048,128]{2,1,0:T(8,128)(2,1)} %get-tuple-element.261.refs_1_, bf16[2,2048,128]{2,1,0:T(8,128)(2,1)} %get-tuple-element.262.refs_2_, ...), custom_call_target="tpu_custom_call" | custom-call | flops 63417876 | bytes 39321 | tf_op jit(solution)/shard_map/input_grad/pallas_call | solution.py:590
  288.3 6.9 %collective-permute-done.48 = bf16[2,96,1728]{2,1,0:T(8,128)(2,1)S(1)} collective-permute-done((bf16[2,96,1728]{2,1,0:T(8,128)(2,1)S(1)}, bf16[2,96,1728]{2,1,0:T(8,128)(2,1)S(1)}, u32[]{:S(2)}, u32[]{:S(2)}) %collective-permute-start.48) | collective-permute-done | bytes 663584 | tf_op jit(solution)/shard_map/ppermute | solution.py:808
  299.2 4.7 %collective-permute-start.52 = (bf16[96,1728]{1,0:T(8,128)(2,1)S(1)}, bf16[96,1728]{1,0:T(8,128)(2,1)S(1)}, u32[]{:S(2)}, u32[]{:S(2)}) collective-permute-start(bf16[96,1728]{1,0:T(8,128)(2,1)S(1)} %fusion.10), channel_id=1, source_target_pairs={{0,2},{1,3},{2,0},{3,1},{4,6},{5,7},{6,4},{7,5},{8,10},{9,11},{10,... | collective-permute-start | bytes 995336 | tf_op jit(solution)/shard_map/ppermute | solution.py:808
  305.3 4.7 %collective-permute-done.50 = bf16[96,1152]{1,0:T(8,128)(2,1)S(1)} collective-permute-done((bf16[96,1152]{1,0:T(8,128)(2,1)S(1)}, bf16[96,1152]{1,0:T(8,128)(2,1)S(1)}, u32[]{:S(2)}, u32[]{:S(2)}) %collective-permute-start.50) | collective-permute-done | bytes 221216 | tf_op jit(solution)/shard_map/ppermute | solution.py:805
  310.7 5.4 %collective-permute-done.52.arrived_ref = bf16[96,1728]{1,0:T(8,128)(2,1)S(1)} collective-permute-done((bf16[96,1728]{1,0:T(8,128)(2,1)S(1)}, bf16[96,1728]{1,0:T(8,128)(2,1)S(1)}, u32[]{:S(2)}, u32[]{:S(2)}) %collective-permute-start.52) | collective-permute-done | bytes 331808 | tf_op jit(solution)/shard_map/ppermute | solution.py:808
  322.3 5.0 %collective-permute-start.56 = (f32[16,768]{1,0:T(8,128)S(1)}, f32[16,768]{1,0:T(8,128)S(1)}, u32[]{:S(2)}, u32[]{:S(2)}) collective-permute-start(f32[16,768]{1,0:T(8,128)S(1)} %add.133), channel_id=1, source_target_pairs={{0,1},{1,0},{2,3},{3,2},{4,5},{5,4},{6,7},{7,6},{8,9},{9,8},{10,11... | collective-permute-start | bytes 147464 | tf_op jit(solution)/shard_map/ppermute | solution.py:808
  327.2 2.1 collective-permute-done.56
  330.0 3.5 collective-permute-done.57
  334.4 2.1 broadcast_select_fusion
  336.5 1.5 collective-permute-start.54
  338.0 4.4 %collective-permute-start.55 = (bf16[512,768]{1,0:T(8,128)(2,1)}, bf16[512,768]{1,0:T(8,128)(2,1)}, u32[]{:S(2)}, u32[]{:S(2)}) collective-permute-start(bf16[512,768]{1,0:T(8,128)(2,1)} %fusion.1), channel_id=1, source_target_pairs={{0,1},{1,0},{6,7},{7,6},{8,9},{9,8},{14,15},{15,14},{16,17},{17,16... | collective-permute-start | bytes 2359304 | tf_op jit(solution)/shard_map/ppermute | solution.py:820
  342.4 4.0 %collective-permute-start.59 = (f32[16,768]{1,0:T(8,128)S(1)}, f32[16,768]{1,0:T(8,128)S(1)}, u32[]{:S(2)}, u32[]{:S(2)}) collective-permute-start(f32[16,768]{1,0:T(8,128)S(1)} %add.143), channel_id=1, source_target_pairs={{0,4},{4,0},{8,12},{12,8},{16,20},{20,16},{24,28},{28,24},{1,5},{5... | collective-permute-start | bytes 147464 | tf_op jit(solution)/shard_map/ppermute | solution.py:805
  348.3 2.2 finish_ffn.1
  350.5 1.9 copy.40
  353.1 1.9 finish_project.1
  355.0 3.8 %collective-permute-done.55 = bf16[512,768]{1,0:T(8,128)(2,1)} collective-permute-done((bf16[512,768]{1,0:T(8,128)(2,1)}, bf16[512,768]{1,0:T(8,128)(2,1)}, u32[]{:S(2)}, u32[]{:S(2)}) %collective-permute-start.55) | collective-permute-done | bytes 786464 | tf_op jit(solution)/shard_map/ppermute | solution.py:820
  360.7 2.9 convert_select_fusion
  (252 shorter events, 76.7 us)
Async XLA Ops:
  5.2 11.3 %collective-permute-start.1 = (bf16[2,96,1152]{2,1,0:T(8,128)(2,1)}, bf16[2,96,1152]{2,1,0:T(8,128)(2,1)}, u32[]{:S(2)}, u32[]{:S(2)}) collective-permute-start(bf16[2,96,1152]{2,1,0:T(8,128)(2,1)} %maximum_select_fusion), channel_id=1, source_target_pairs={{2,4},{3,5},{4,2},{5,3},{10,12},{11,13},{12,10},{13,11},{18,20},{1... | collective-permute-start | bytes 1327112 | tf_op jit(solution)/shard_map/ppermute | solution.py:799
  6.6 35.2 %collective-permute-start.5 = (bf16[512,768]{1,0:T(8,128)(2,1)S(1)}, bf16[512,768]{1,0:T(8,128)(2,1)S(1)}, u32[]{:S(2)}, u32[]{:S(2)}) collective-permute-start(bf16[512,768]{1,0:T(8,128)(2,1)S(1)} %copy-done.11), channel_id=1, source_target_pairs={{2,4},{3,5},{4,2},{5,3},{10,12},{11,13},{12,10},{13,11},{18,20},{1... | collective-permute-start | bytes 2359304 | tf_op jit(solution)/shard_map/ppermute | solution.py:820
  7.3 34.4 %collective-permute-start.6 = (bf16[512,768]{1,0:T(8,128)(2,1)S(1)}, bf16[512,768]{1,0:T(8,128)(2,1)S(1)}, u32[]{:S(2)}, u32[]{:S(2)}) collective-permute-start(bf16[512,768]{1,0:T(8,128)(2,1)S(1)} %copy-done.11), channel_id=1, source_target_pairs={{0,1},{1,0},{6,7},{7,6},{8,9},{9,8},{14,15},{15,14},{16,17},{17,16... | collective-permute-start | bytes 2359304 | tf_op jit(solution)/shard_map/ppermute | solution.py:820
  14.7 27.0 %collective-permute-start.7 = (bf16[96,1728]{1,0:T(8,128)(2,1)S(1)}, bf16[96,1728]{1,0:T(8,128)(2,1)S(1)}, u32[]{:S(2)}, u32[]{:S(2)}) collective-permute-start(bf16[96,1728]{1,0:T(8,128)(2,1)S(1)} %pad_maximum_fusion.6), channel_id=1, source_target_pairs={{0,1},{1,0},{2,3},{3,2},{4,5},{5,4},{6,7},{7,6},{8,9},{9,8},{10,11... | collective-permute-start | bytes 995336 | tf_op jit(solution)/shard_map/ppermute | solution.py:808
  17.3 9.8 %collective-permute-start.4 = (bf16[2,96,1152]{2,1,0:T(8,128)(2,1)}, bf16[2,96,1152]{2,1,0:T(8,128)(2,1)S(1)}, u32[]{:S(2)}, u32[]{:S(2)}) collective-permute-start(bf16[2,96,1152]{2,1,0:T(8,128)(2,1)} %broadcast_select_fusion.5.rest_0_), channel_id=1, source_target_pairs={{0,16},{4,20},{8,24},{12,28},{16,0},{20,4},{24,8},{28,12},{1,17},{... | collective-permute-start | bytes 1327112 | tf_op jit(solution)/shard_map/ppermute | solution.py:805
  18.8 8.6 %collective-permute-start.3 = (bf16[2,96,1152]{2,1,0:T(8,128)(2,1)}, bf16[2,96,1152]{2,1,0:T(8,128)(2,1)}, u32[]{:S(2)}, u32[]{:S(2)}) collective-permute-start(bf16[2,96,1152]{2,1,0:T(8,128)(2,1)} %broadcast_select_fusion.5.rest_0_), channel_id=1, source_target_pairs={{0,8},{4,12},{8,0},{12,4},{16,24},{20,28},{24,16},{28,20},{1,9},{5... | collective-permute-start | bytes 1327112 | tf_op jit(solution)/shard_map/ppermute | solution.py:805
  41.8 17.6 %collective-permute-start.8 = (bf16[512,768]{1,0:T(8,128)(2,1)S(1)}, bf16[512,768]{1,0:T(8,128)(2,1)S(1)}, u32[]{:S(2)}, u32[]{:S(2)}) collective-permute-start(bf16[512,768]{1,0:T(8,128)(2,1)S(1)} %broadcast_select_fusion.3.x0.hid_ref), channel_id=1, source_target_pairs={{2,3},{3,2},{4,5},{5,4},{10,11},{11,10},{12,13},{13,12},{18,19},{1... | collective-permute-start | bytes 2359304 | tf_op jit(solution)/shard_map/ppermute | solution.py:820
  42.6 16.9 %collective-permute-start.12 = (bf16[96,1728]{1,0:T(8,128)(2,1)S(1)}, bf16[96,1728]{1,0:T(8,128)(2,1)S(1)}, u32[]{:S(2)}, u32[]{:S(2)}) collective-permute-start(bf16[96,1728]{1,0:T(8,128)(2,1)S(1)} %pad_maximum_fusion.6), channel_id=1, source_target_pairs={{0,16},{4,20},{8,24},{12,28},{16,0},{20,4},{24,8},{28,12},{1,17},{... | collective-permute-start | bytes 995336 | tf_op jit(solution)/shard_map/ppermute | solution.py:805
  44.4 15.0 %collective-permute-start.11 = (bf16[96,1728]{1,0:T(8,128)(2,1)S(1)}, bf16[96,1728]{1,0:T(8,128)(2,1)S(1)}, u32[]{:S(2)}, u32[]{:S(2)}) collective-permute-start(bf16[96,1728]{1,0:T(8,128)(2,1)S(1)} %pad_maximum_fusion.6), channel_id=1, source_target_pairs={{0,8},{4,12},{8,0},{12,4},{16,24},{20,28},{24,16},{28,20},{1,9},{5... | collective-permute-start | bytes 995336 | tf_op jit(solution)/shard_map/ppermute | solution.py:805
  45.9 11.2 %collective-permute-start.9 = (bf16[96,1152]{1,0:T(8,128)(2,1)S(1)}, bf16[96,1152]{1,0:T(8,128)(2,1)S(1)}, u32[]{:S(2)}, u32[]{:S(2)}) collective-permute-start(bf16[96,1152]{1,0:T(8,128)(2,1)S(1)} %get-tuple-element.185), channel_id=1, source_target_pairs={{0,16},{4,20},{8,24},{12,28},{16,0},{20,4},{24,8},{28,12},{1,17},{... | collective-permute-start | bytes 663560 | tf_op jit(solution)/shard_map/ppermute | solution.py:805
  46.4 13.0 %collective-permute-start.10 = (bf16[96,1152]{1,0:T(8,128)(2,1)S(1)}, bf16[96,1152]{1,0:T(8,128)(2,1)S(1)}, u32[]{:S(2)}, u32[]{:S(2)}) collective-permute-start(bf16[96,1152]{1,0:T(8,128)(2,1)S(1)} %get-tuple-element.186), channel_id=1, source_target_pairs={{0,8},{4,12},{8,0},{12,4},{16,24},{20,28},{24,16},{28,20},{1,9},{5... | collective-permute-start | bytes 663560 | tf_op jit(solution)/shard_map/ppermute | solution.py:805
  62.1 20.6 %collective-permute-start.17 = (bf16[96,1728]{1,0:T(8,128)(2,1)S(1)}, bf16[96,1728]{1,0:T(8,128)(2,1)S(1)}, u32[]{:S(2)}, u32[]{:S(2)}) collective-permute-start(bf16[96,1728]{1,0:T(8,128)(2,1)S(1)} %collective-permute-done.7), channel_id=1, source_target_pairs={{0,16},{4,20},{8,24},{12,28},{16,0},{20,4},{24,8},{28,12},{1,17},{... | collective-permute-start | bytes 995336 | tf_op jit(solution)/shard_map/ppermute | solution.py:805
  63.1 19.7 %collective-permute-start.16 = (bf16[96,1728]{1,0:T(8,128)(2,1)S(1)}, bf16[96,1728]{1,0:T(8,128)(2,1)S(1)}, u32[]{:S(2)}, u32[]{:S(2)}) collective-permute-start(bf16[96,1728]{1,0:T(8,128)(2,1)S(1)} %collective-permute-done.7), channel_id=1, source_target_pairs={{0,8},{4,12},{8,0},{12,4},{16,24},{20,28},{24,16},{28,20},{1,9},{5... | collective-permute-start | bytes 995336 | tf_op jit(solution)/shard_map/ppermute | solution.py:805
  64.7 18.0 %collective-permute-start.15 = (bf16[96,1728]{1,0:T(8,128)(2,1)S(1)}, bf16[96,1728]{1,0:T(8,128)(2,1)S(1)}, u32[]{:S(2)}, u32[]{:S(2)}) collective-permute-start(bf16[96,1728]{1,0:T(8,128)(2,1)S(1)} %pad_maximum_fusion.6), channel_id=1, source_target_pairs={{0,2},{1,3},{2,0},{3,1},{4,6},{5,7},{6,4},{7,5},{8,10},{9,11},{10,... | collective-permute-start | bytes 995336 | tf_op jit(solution)/shard_map/ppermute | solution.py:808
  66.1 16.6 %collective-permute-start.18 = (bf16[96,1728]{1,0:T(8,128)(2,1)S(1)}, bf16[96,1728]{1,0:T(8,128)(2,1)S(1)}, u32[]{:S(2)}, u32[]{:S(2)}) collective-permute-start(bf16[96,1728]{1,0:T(8,128)(2,1)S(1)} %collective-permute-done.11), channel_id=1, source_target_pairs={{0,16},{4,20},{8,24},{12,28},{16,0},{20,4},{24,8},{28,12},{1,17},{... | collective-permute-start | bytes 995336 | tf_op jit(solution)/shard_map/ppermute | solution.py:805
  83.0 13.2 %collective-permute-start.22 = (bf16[4,96,1728]{2,1,0:T(8,128)(2,1)S(1)}, bf16[4,96,1728]{2,1,0:T(8,128)(2,1)}, u32[]{:S(2)}, u32[]{:S(2)}) collective-permute-start(bf16[4,96,1728]{2,1,0:T(8,128)(2,1)S(1)} %pad_maximum_fusion.rest_0_), channel_id=1, source_target_pairs={{0,4},{4,0},{8,12},{12,8},{16,20},{20,16},{24,28},{28,24},{1,5},{5... | collective-permute-start | bytes 3981320 | tf_op jit(solution)/shard_map/ppermute | solution.py:805
  83.0 13.1 %collective-permute-start.21 = (bf16[96,1728]{1,0:T(8,128)(2,1)S(1)}, bf16[96,1728]{1,0:T(8,128)(2,1)S(1)}, u32[]{:S(2)}, u32[]{:S(2)}) collective-permute-start(bf16[96,1728]{1,0:T(8,128)(2,1)S(1)} %collective-permute-done.15), channel_id=1, source_target_pairs={{0,16},{4,20},{8,24},{12,28},{16,0},{20,4},{24,8},{28,12},{1,17},{... | collective-permute-start | bytes 995336 | tf_op jit(solution)/shard_map/ppermute | solution.py:805
  84.0 12.1 %collective-permute-start.20 = (bf16[96,1728]{1,0:T(8,128)(2,1)S(1)}, bf16[96,1728]{1,0:T(8,128)(2,1)S(1)}, u32[]{:S(2)}, u32[]{:S(2)}) collective-permute-start(bf16[96,1728]{1,0:T(8,128)(2,1)S(1)} %collective-permute-done.15), channel_id=1, source_target_pairs={{0,8},{4,12},{8,0},{12,4},{16,24},{20,28},{24,16},{28,20},{1,9},{5... | collective-permute-start | bytes 995336 | tf_op jit(solution)/shard_map/ppermute | solution.py:805
  84.6 11.6 %collective-permute-start.19 = (bf16[96,1728]{1,0:T(8,128)(2,1)S(1)}, bf16[96,1728]{1,0:T(8,128)(2,1)S(1)}, u32[]{:S(2)}, u32[]{:S(2)}) collective-permute-start(bf16[96,1728]{1,0:T(8,128)(2,1)S(1)} %collective-permute-done.15), channel_id=1, source_target_pairs={{0,1},{1,0},{2,3},{3,2},{4,5},{5,4},{6,7},{7,6},{8,9},{9,8},{10,11... | collective-permute-start | bytes 995336 | tf_op jit(solution)/shard_map/ppermute | solution.py:808
  84.6 32.6 %collective-permute-start.26 = (bf16[96,1728]{1,0:T(8,128)(2,1)S(1)}, bf16[96,1728]{1,0:T(8,128)(2,1)}, u32[]{:S(2)}, u32[]{:S(2)}) collective-permute-start(bf16[96,1728]{1,0:T(8,128)(2,1)S(1)} %collective-permute-done.17), channel_id=1, source_target_pairs={{0,8},{4,12},{8,0},{12,4},{16,24},{20,28},{24,16},{28,20},{1,9},{5... | collective-permute-start | bytes 995336 | tf_op jit(solution)/shard_map/ppermute | solution.py:805
  96.2 21.0 %collective-permute-start.24 = (bf16[96,1728]{1,0:T(8,128)(2,1)S(1)}, bf16[96,1728]{1,0:T(8,128)(2,1)S(1)}, u32[]{:S(2)}, u32[]{:S(2)}) collective-permute-start(bf16[96,1728]{1,0:T(8,128)(2,1)S(1)} %collective-permute-done.19), channel_id=1, source_target_pairs={{0,16},{4,20},{8,24},{12,28},{16,0},{20,4},{24,8},{28,12},{1,17},{... | collective-permute-start | bytes 995336 | tf_op jit(solution)/shard_map/ppermute | solution.py:805
  97.4 19.8 %collective-permute-start.23 = (bf16[96,1728]{1,0:T(8,128)(2,1)S(1)}, bf16[96,1728]{1,0:T(8,128)(2,1)S(1)}, u32[]{:S(2)}, u32[]{:S(2)}) collective-permute-start(bf16[96,1728]{1,0:T(8,128)(2,1)S(1)} %collective-permute-done.19), channel_id=1, source_target_pairs={{0,8},{4,12},{8,0},{12,4},{16,24},{20,28},{24,16},{28,20},{1,9},{5... | collective-permute-start | bytes 995336 | tf_op jit(solution)/shard_map/ppermute | solution.py:805
  97.7 19.4 %collective-permute-start.25 = (bf16[96,1728]{1,0:T(8,128)(2,1)S(1)}, bf16[96,1728]{1,0:T(8,128)(2,1)}, u32[]{:S(2)}, u32[]{:S(2)}) collective-permute-start(bf16[96,1728]{1,0:T(8,128)(2,1)S(1)} %collective-permute-done.20), channel_id=1, source_target_pairs={{0,16},{4,20},{8,24},{12,28},{16,0},{20,4},{24,8},{28,12},{1,17},{... | collective-permute-start | bytes 995336 | tf_op jit(solution)/shard_map/ppermute | solution.py:805
  98.8 18.4 %collective-permute-start.27 = (bf16[512,768]{1,0:T(8,128)(2,1)S(1)}, bf16[512,768]{1,0:T(8,128)(2,1)S(1)}, u32[]{:S(2)}, u32[]{:S(2)}) collective-permute-start(bf16[512,768]{1,0:T(8,128)(2,1)S(1)} %copy-done.12), channel_id=1, source_target_pairs={{2,4},{3,5},{4,2},{5,3},{10,12},{11,13},{12,10},{13,11},{18,20},{1... | collective-permute-start | bytes 2359304 | tf_op jit(solution)/shard_map/ppermute | solution.py:820
  118.4 18.8 %collective-permute-start.32 = (bf16[4,96,1728]{2,1,0:T(8,128)(2,1)S(1)}, bf16[4,96,1728]{2,1,0:T(8,128)(2,1)S(1)}, u32[]{:S(2)}, u32[]{:S(2)}) collective-permute-start(bf16[4,96,1728]{2,1,0:T(8,128)(2,1)S(1)} %pad_maximum_fusion.1.rest_2_), channel_id=1, source_target_pairs={{0,4},{4,0},{8,12},{12,8},{16,20},{20,16},{24,28},{28,24},{1,5},{5... | collective-permute-start | bytes 3981320 | tf_op jit(solution)/shard_map/ppermute | solution.py:805
  122.7 14.6 %collective-permute-start.31 = (bf16[96,1728]{1,0:T(8,128)(2,1)S(1)}, bf16[96,1728]{1,0:T(8,128)(2,1)S(1)}, u32[]{:S(2)}, u32[]{:S(2)}) collective-permute-start(bf16[96,1728]{1,0:T(8,128)(2,1)S(1)} %collective-permute-done.24), channel_id=1, source_target_pairs={{0,8},{4,12},{8,0},{12,4},{16,24},{20,28},{24,16},{28,20},{1,9},{5... | collective-permute-start | bytes 995336 | tf_op jit(solution)/shard_map/ppermute | solution.py:805
  125.9 11.4 %collective-permute-start.28 = (bf16[1,192,512]{2,1,0:T(8,128)(2,1)S(1)}, bf16[1,192,512]{2,1,0:T(8,128)(2,1)S(1)}, u32[]{:S(2)}, u32[]{:S(2)}) collective-permute-start(bf16[1,192,512]{2,1,0:T(8,128)(2,1)S(1)} %get-tuple-element.378), channel_id=1, source_target_pairs={{0,1},{1,0},{2,3},{3,2},{4,5},{5,4},{6,7},{7,6},{8,9},{9,8},{10,11... | collective-permute-start | bytes 589832 | tf_op jit(solution)/shard_map/ppermute | solution.py:802
  173.8 15.0 %collective-permute-start.37 = (bf16[1,192,512]{2,1,0:T(8,128)(2,1)S(1)}, bf16[1,192,512]{2,1,0:T(8,128)(2,1)S(1)}, u32[]{:S(2)}, u32[]{:S(2)}) collective-permute-start(bf16[1,192,512]{2,1,0:T(8,128)(2,1)S(1)} %get-tuple-element.373), channel_id=1, source_target_pairs={{0,5},{1,4},{2,7},{3,6},{4,1},{5,0},{6,3},{7,2},{8,13},{9,12},{10,... | collective-permute-start | bytes 589832 | tf_op jit(solution)/shard_map/ppermute | solution.py:802
  173.9 15.0 %collective-permute-start.36 = (bf16[1,192,512]{2,1,0:T(8,128)(2,1)S(1)}, bf16[1,192,512]{2,1,0:T(8,128)(2,1)S(1)}, u32[]{:S(2)}, u32[]{:S(2)}) collective-permute-start(bf16[1,192,512]{2,1,0:T(8,128)(2,1)S(1)} %get-tuple-element.374), channel_id=1, source_target_pairs={{0,4},{1,5},{2,6},{3,7},{4,0},{5,1},{6,2},{7,3},{8,12},{9,13},{10,... | collective-permute-start | bytes 589832 | tf_op jit(solution)/shard_map/ppermute | solution.py:802
  174.1 14.8 %collective-permute-start.35 = (bf16[1,192,512]{2,1,0:T(8,128)(2,1)S(1)}, bf16[1,192,512]{2,1,0:T(8,128)(2,1)S(1)}, u32[]{:S(2)}, u32[]{:S(2)}) collective-permute-start(bf16[1,192,512]{2,1,0:T(8,128)(2,1)S(1)} %get-tuple-element.375), channel_id=1, source_target_pairs={{0,1},{1,0},{2,3},{3,2},{4,5},{5,4},{6,7},{7,6},{8,9},{9,8},{10,11... | collective-permute-start | bytes 589832 | tf_op jit(solution)/shard_map/ppermute | solution.py:802
  189.8 17.5 %collective-permute-start.38 = (bf16[4,4,96,1728]{3,2,1,0:T(8,128)(2,1)}, bf16[4,4,96,1728]{3,2,1,0:T(8,128)(2,1)}, u32[]{:S(2)}, u32[]{:S(2)}) collective-permute-start(bf16[4,4,96,1728]{3,2,1,0:T(8,128)(2,1)} %get-tuple-element.244), channel_id=1, source_target_pairs={{0,4},{4,0},{8,12},{12,8},{16,20},{20,16},{24,28},{28,24},{1,5},{5... | collective-permute-start | bytes 15925256 | tf_op jit(solution)/shard_map/ppermute | solution.py:805
  212.1 33.0 %collective-permute-start.41 = (bf16[512,768]{1,0:T(8,128)(2,1)}, bf16[512,768]{1,0:T(8,128)(2,1)S(1)}, u32[]{:S(2)}, u32[]{:S(2)}) collective-permute-start(bf16[512,768]{1,0:T(8,128)(2,1)} %get-tuple-element.246), channel_id=1, source_target_pairs={{2,4},{3,5},{4,2},{5,3},{10,12},{11,13},{12,10},{13,11},{18,20},{1... | collective-permute-start | bytes 2359304 | tf_op jit(solution)/shard_map/ppermute | solution.py:820
  212.8 32.4 %collective-permute-start.39 = (bf16[2,2,96,1728]{3,2,1,0:T(8,128)(2,1)}, bf16[2,2,96,1728]{3,2,1,0:T(8,128)(2,1)S(1)}, u32[]{:S(2)}, u32[]{:S(2)}) collective-permute-start(bf16[2,2,96,1728]{3,2,1,0:T(8,128)(2,1)} %get-tuple-element.251), channel_id=1, source_target_pairs={{0,8},{4,12},{8,0},{12,4},{16,24},{20,28},{24,16},{28,20},{1,9},{5... | collective-permute-start | bytes 3981320 | tf_op jit(solution)/shard_map/ppermute | solution.py:805
  213.5 32.3 %collective-permute-start.40 = (bf16[2,2,96,1728]{3,2,1,0:T(8,128)(2,1)}, bf16[2,2,96,1728]{3,2,1,0:T(8,128)(2,1)S(1)}, u32[]{:S(2)}, u32[]{:S(2)}) collective-permute-start(bf16[2,2,96,1728]{3,2,1,0:T(8,128)(2,1)} %get-tuple-element.252), channel_id=1, source_target_pairs={{0,16},{4,20},{8,24},{12,28},{16,0},{20,4},{24,8},{28,12},{1,17},{... | collective-permute-start | bytes 3981320 | tf_op jit(solution)/shard_map/ppermute | solution.py:805
  247.9 17.7 %collective-permute-start.42 = (bf16[2,96,1728]{2,1,0:T(8,128)(2,1)}, bf16[2,96,1728]{2,1,0:T(8,128)(2,1)S(1)}, u32[]{:S(2)}, u32[]{:S(2)}) collective-permute-start(bf16[2,96,1728]{2,1,0:T(8,128)(2,1)} %get-tuple-element.270), channel_id=1, source_target_pairs={{0,16},{4,20},{8,24},{12,28},{16,0},{20,4},{24,8},{28,12},{1,17},{... | collective-permute-start | bytes 1990664 | tf_op jit(solution)/shard_map/ppermute | solution.py:805
  249.1 18.0 %collective-permute-start.43 = (bf16[2,96,1728]{2,1,0:T(8,128)(2,1)S(1)}, bf16[2,96,1728]{2,1,0:T(8,128)(2,1)S(1)}, u32[]{:S(2)}, u32[]{:S(2)}) collective-permute-start(bf16[2,96,1728]{2,1,0:T(8,128)(2,1)S(1)} %get-tuple-element.271), channel_id=1, source_target_pairs={{0,8},{4,12},{8,0},{12,4},{16,24},{20,28},{24,16},{28,20},{1,9},{5... | collective-permute-start | bytes 1990664 | tf_op jit(solution)/shard_map/ppermute | solution.py:805
  275.5 12.2 %collective-permute-start.46 = (bf16[2,96,1152]{2,1,0:T(8,128)(2,1)}, bf16[2,96,1152]{2,1,0:T(8,128)(2,1)S(1)}, u32[]{:S(2)}, u32[]{:S(2)}) collective-permute-start(bf16[2,96,1152]{2,1,0:T(8,128)(2,1)} %get-tuple-element.284), channel_id=1, source_target_pairs={{0,8},{4,12},{8,0},{12,4},{16,24},{20,28},{24,16},{28,20},{1,9},{5... | collective-permute-start | bytes 1327112 | tf_op jit(solution)/shard_map/ppermute | solution.py:805
  277.0 11.3 %collective-permute-start.47 = (bf16[2,96,1152]{2,1,0:T(8,128)(2,1)}, bf16[2,96,1152]{2,1,0:T(8,128)(2,1)S(1)}, u32[]{:S(2)}, u32[]{:S(2)}) collective-permute-start(bf16[2,96,1152]{2,1,0:T(8,128)(2,1)} %get-tuple-element.285), channel_id=1, source_target_pairs={{0,16},{4,20},{8,24},{12,28},{16,0},{20,4},{24,8},{28,12},{1,17},{... | collective-permute-start | bytes 1327112 | tf_op jit(solution)/shard_map/ppermute | solution.py:805
  278.1 17.1 %collective-permute-start.48 = (bf16[2,96,1728]{2,1,0:T(8,128)(2,1)S(1)}, bf16[2,96,1728]{2,1,0:T(8,128)(2,1)S(1)}, u32[]{:S(2)}, u32[]{:S(2)}) collective-permute-start(bf16[2,96,1728]{2,1,0:T(8,128)(2,1)S(1)} %add_convert_fusion.5), channel_id=1, source_target_pairs={{0,1},{1,0},{2,3},{3,2},{4,5},{5,4},{6,7},{7,6},{8,9},{9,8},{10,11... | collective-permute-start | bytes 1990664 | tf_op jit(solution)/shard_map/ppermute | solution.py:808
  281.2 14.0 %collective-permute-start.49 = (f32[16,768]{1,0:T(8,128)S(1)}, f32[16,768]{1,0:T(8,128)S(1)}, u32[]{:S(2)}, u32[]{:S(2)}) collective-permute-start(f32[16,768]{1,0:T(8,128)S(1)} %copy-done.28), channel_id=1, source_target_pairs={{0,2},{1,3},{2,0},{3,1},{4,6},{5,7},{6,4},{7,5},{8,10},{9,11},{10,... | collective-permute-start | bytes 147464 | tf_op jit(solution)/shard_map/ppermute | solution.py:808
  296.9 19.1 %collective-permute-start.53 = (bf16[2,512,768]{2,1,0:T(8,128)(2,1)S(1)}, bf16[2,512,768]{2,1,0:T(8,128)(2,1)S(1)}, u32[]{:S(2)}, u32[]{:S(2)}) collective-permute-start(bf16[2,512,768]{2,1,0:T(8,128)(2,1)S(1)} %copy-done.3), channel_id=1, source_target_pairs={{2,6},{3,7},{4,0},{5,1},{10,14},{11,15},{12,8},{13,9},{18,22},{19,... | collective-permute-start | bytes 4718600 | tf_op jit(solution)/shard_map/ppermute | solution.py:820
  298.2 17.8 %collective-permute-start.45 = (bf16[512,768]{1,0:T(8,128)(2,1)S(1)}, bf16[512,768]{1,0:T(8,128)(2,1)S(1)}, u32[]{:S(2)}, u32[]{:S(2)}) collective-permute-start(bf16[512,768]{1,0:T(8,128)(2,1)S(1)} %fusion), channel_id=1, source_target_pairs={{2,3},{3,2},{4,5},{5,4},{10,11},{11,10},{12,13},{13,12},{18,19},{1... | collective-permute-start | bytes 2359304 | tf_op jit(solution)/shard_map/ppermute | solution.py:820
  299.2 16.8 %collective-permute-start.52 = (bf16[96,1728]{1,0:T(8,128)(2,1)S(1)}, bf16[96,1728]{1,0:T(8,128)(2,1)S(1)}, u32[]{:S(2)}, u32[]{:S(2)}) collective-permute-start(bf16[96,1728]{1,0:T(8,128)(2,1)S(1)} %fusion.10), channel_id=1, source_target_pairs={{0,2},{1,3},{2,0},{3,1},{4,6},{5,7},{6,4},{7,5},{8,10},{9,11},{10,... | collective-permute-start | bytes 995336 | tf_op jit(solution)/shard_map/ppermute | solution.py:808
  321.6 24.9 %collective-permute-start.60 = (bf16[2,96,1152]{2,1,0:T(8,128)(2,1)S(1)}, bf16[2,96,1152]{2,1,0:T(8,128)(2,1)S(1)}, u32[]{:S(2)}, u32[]{:S(2)}) collective-permute-start(bf16[2,96,1152]{2,1,0:T(8,128)(2,1)S(1)} %pad_maximum_fusion.5), channel_id=1, source_target_pairs={{2,4},{3,5},{4,2},{5,3},{10,12},{11,13},{12,10},{13,11},{18,20},{1... | collective-permute-start | bytes 1327112 | tf_op jit(solution)/shard_map/ppermute | solution.py:820
  333.5 8.9 %collective-permute-start.58 = (f32[16,768]{1,0:T(8,128)S(1)}, f32[16,768]{1,0:T(8,128)S(1)}, u32[]{:S(2)}, u32[]{:S(2)}) collective-permute-start(f32[16,768]{1,0:T(8,128)S(1)} %add.142), channel_id=1, source_target_pairs={{0,16},{4,20},{8,24},{12,28},{16,0},{20,4},{24,8},{28,12},{1,17},{... | collective-permute-start | bytes 147464 | tf_op jit(solution)/shard_map/ppermute | solution.py:805
  336.5 18.6 %collective-permute-start.54 = (bf16[512,768]{1,0:T(8,128)(2,1)}, bf16[512,768]{1,0:T(8,128)(2,1)}, u32[]{:S(2)}, u32[]{:S(2)}) collective-permute-start(bf16[512,768]{1,0:T(8,128)(2,1)} %add_convert_fusion.4), channel_id=1, source_target_pairs={{2,4},{3,5},{4,2},{5,3},{10,12},{11,13},{12,10},{13,11},{18,20},{1... | collective-permute-start | bytes 2359304 | tf_op jit(solution)/shard_map/ppermute | solution.py:820
  338.0 20.8 %collective-permute-start.55 = (bf16[512,768]{1,0:T(8,128)(2,1)}, bf16[512,768]{1,0:T(8,128)(2,1)}, u32[]{:S(2)}, u32[]{:S(2)}) collective-permute-start(bf16[512,768]{1,0:T(8,128)(2,1)} %fusion.1), channel_id=1, source_target_pairs={{0,1},{1,0},{6,7},{7,6},{8,9},{9,8},{14,15},{15,14},{16,17},{17,16... | collective-permute-start | bytes 2359304 | tf_op jit(solution)/shard_map/ppermute | solution.py:820
  342.4 9.9 %collective-permute-start.59 = (f32[16,768]{1,0:T(8,128)S(1)}, f32[16,768]{1,0:T(8,128)S(1)}, u32[]{:S(2)}, u32[]{:S(2)}) collective-permute-start(f32[16,768]{1,0:T(8,128)S(1)} %add.143), channel_id=1, source_target_pairs={{0,4},{4,0},{8,12},{12,8},{16,20},{20,16},{24,28},{28,24},{1,5},{5... | collective-permute-start | bytes 147464 | tf_op jit(solution)/shard_map/ppermute | solution.py:805
  (59 other events, 475.0 us)
